TPU v7x, 128 devices: a whole 4x4x4 slice. The times are simulated.
128 devices in a mesh: dp: 4 (over z), latent: 32 (over x, y, core).
Axes of the slice: x: 4, y: 4, z: 4, core: 2. Of those that a mesh axis runs over, the one named last changes fastest.
Arguments:
- acts: bfloat16 [640, 8192], P(('dp', 'latent')), may hold values from -6 to 6
- chat_len: int32 [128], P(('dp', 'latent')), may hold values from 1 to 5, as said below
- group_of: int32 [640, 1], P(('dp', 'latent')), may hold values from 0 to 4; in each aligned block of 5 rows (0 to 4, 5 to 9, ...) no two rows name the same one
- w_enc: bfloat16 [2, 4096, 16384], P(None, None, 'latent'), may hold values from -0.0625 to 0.0625
- b_enc: float32 [16384], P('latent'), may hold values from -3 to 3
- w_dec: bfloat16 [16384, 8192], P('latent'), may hold values from -0.046875 to 0.046875
- b_dec: float32 [2, 4096], replicated, may hold values from -3 to 3
Outputs:
- grad_enc: bfloat16 [2, 4096, 16384], P(None, 'dp', 'latent')
- grad_dec: bfloat16 [16384, 8192], P('latent', 'dp')
- loss: float32 [], replicated
Inputs may be any that keep to these rules, and one draw needn't show every extreme that they name: `chat_len`: the last serving shard harvests all 5 rows. `group_of`: among the 5 row slots of each serving shard every value 0 to 4 appears exactly once.
All inputs are finite; a program needn't handle non-finite values.
Results may differ from a plain program's by a relative error of at most 0.02.
Values may be sent and summed in bfloat16 or wider, within the bound.
No kernel may reach another device: no remote copies, remote signals or barrier semaphores. Data moves between devices by JAX's collectives and lax.ppermute only.
A program may use at most 128 MiB of HBM per device.

v0:
```python
import jax
import jax.numpy as jnp
from jax import lax
from jax.sharding import PartitionSpec as P

sparsity_weight = 1.0
loss_scale = 8.0
norm_eps = 1e-06


def shards(acts, chat_len, group_of, w_enc, b_enc, w_dec, b_dec):
    groups = lax.axis_size("dp")
    slots = acts.shape[0]
    width = acts.shape[1]
    half = width // 2
    local_latents = w_enc.shape[2]
    capacity = slots // (groups + 1)
    slot_ids = jnp.arange(slots, dtype=jnp.int32)
    alive = (slot_ids < chat_len[0]).astype(jnp.float32)
    order = jnp.argsort(group_of[:, 0], stable=True)[: groups * capacity]
    own_count = jnp.sum(alive[order])
    outgoing = acts[order].reshape(groups, capacity, width)
    out_mask = alive[order].reshape(groups, capacity).astype(jnp.bfloat16)
    received, recv_mask = (
        lax.all_to_all(outgoing, "dp", split_axis=0, concat_axis=0, tiled=True),
        lax.all_to_all(out_mask, "dp", split_axis=0, concat_axis=0, tiled=True),
    )
    member_rows, member_mask = (
        lax.all_gather(received, "latent", axis=0, tiled=True),
        lax.all_gather(recv_mask, "latent", axis=0, tiled=True),
    )
    xg = member_rows.reshape(-1, width)
    maskg = member_mask.reshape(-1).astype(jnp.float32)
    total_rows = xg.shape[0]
    share_rows = total_rows // lax.axis_size("latent")
    first_row = lax.axis_index("latent") * share_rows
    wenc_flat = w_enc.reshape(width, local_latents)
    squares_dec = jnp.square(w_dec.astype(jnp.float32))
    norm_base = jnp.sqrt(jnp.sum(squares_dec[:, :half], axis=1) + norm_eps)
    norm_inst = jnp.sqrt(jnp.sum(squares_dec[:, half:], axis=1) + norm_eps)
    norm_sum = norm_base + norm_inst
    column_ids = jnp.arange(width, dtype=jnp.int32)
    bias_row = b_dec.reshape(width)
    pre = jnp.dot(xg, wenc_flat, preferred_element_type=jnp.float32) + b_enc[None, :]
    act = jnp.maximum(pre, 0.0)
    feats = act * act
    feats16 = feats.astype(jnp.bfloat16)
    partial_value = jnp.dot(feats16, w_dec, preferred_element_type=jnp.float32)
    recon = lax.psum(partial_value.astype(jnp.bfloat16), "latent").astype(jnp.float32)
    err = (recon + bias_row[None, :] - xg.astype(jnp.float32)) * maskg[:, None]
    err16 = err.astype(jnp.bfloat16)
    err_share = lax.dynamic_slice_in_dim(err, first_row, share_rows, 0)
    square_sum = jnp.sum(err_share * err_share)
    feat_sum = jnp.sum(feats * maskg[:, None], axis=0)
    local_loss = square_sum + sparsity_weight * jnp.sum(feat_sum * norm_sum)
    dfeat = 2.0 * lax.dot_general(
        err16, w_dec, (((1,), (1,)), ((), ())), preferred_element_type=jnp.float32
    )
    dfeat = dfeat + sparsity_weight * maskg[:, None] * norm_sum[None, :]
    dpre16 = (dfeat * 2.0 * act).astype(jnp.bfloat16)
    enc_term = lax.dot_general(
        xg, dpre16, (((0,), (0,)), ((), ())), preferred_element_type=jnp.float32
    )
    enc_term = enc_term.reshape(2, half, local_latents)
    dec_term = 2.0 * lax.dot_general(
        feats16, err16, (((0,), (0,)), ((), ())), preferred_element_type=jnp.float32
    )
    scale = jnp.where(
        column_ids[None, :] < half, (feat_sum / norm_base)[:, None], (feat_sum / norm_inst)[:, None]
    )
    dec_term = dec_term + sparsity_weight * scale * w_dec.astype(jnp.float32)
    enc_total = lax.psum_scatter(
        enc_term.astype(jnp.bfloat16), "dp", scatter_dimension=1, tiled=True
    ).astype(jnp.float32)
    dec_total = lax.psum_scatter(
        dec_term.astype(jnp.bfloat16), "dp", scatter_dimension=1, tiled=True
    ).astype(jnp.float32)
    total, count = lax.psum((local_loss, own_count), ("dp", "latent"))
    factor = loss_scale / count
    grad_enc = (enc_total * factor).astype(jnp.bfloat16)
    grad_dec = (dec_total * factor).astype(jnp.bfloat16)
    loss = total / (count * width)
    return (grad_enc, grad_dec, loss)


def solution(mesh):
    return jax.shard_map(
        shards,
        mesh=mesh,
        in_specs=(
            P(("dp", "latent"), None),
            P(("dp", "latent")),
            P(("dp", "latent"), None),
            P(None, None, "latent"),
            P("latent"),
            P("latent", None),
            P(),
        ),
        out_specs=(P(None, "dp", "latent"), P("latent", "dp"), P()),
        check_vma=False,
    )
```

profile of v0, /device:TPU:1, one launch (start us, length us, event | category | flops | bytes accessed | tf_op | source)
XLA Modules:
  0.0 414.3 jit_solution(3964806186658669848)
XLA Ops:
  7.2 1.6 sort.17
  10.0 0.7 reduce.2
  10.8 10.1 %all_to_all.14 = bf16[4,2,4096]{2,1,0:T(2,128)(2,1)S(1)} all-to-all(bf16[4,2,4096]{2,1,0:T(2,128)(2,1)S(1)} %reshape.95), channel_id=1, replica_groups=mesh['dp'=4,'latent'=32] {'dp'}, dimensions={0} | all-to-all | bytes 131072 | tf_op jit(solution)/shard_map/all_to_all | solution.py:25
  20.9 0.7 reshape.96
  22.3 0.6 gather_fusion.1
  23.6 0.7 copy.17
  24.3 3.2 all-to-all-start.1
  27.5 1.3 dynamic-slice
  29.6 1.9 all-to-all-done.1
  31.8 65.9 %all-reduce = bf16[128]{0:T(256)(128)(2,1)S(1)} all-reduce(bf16[128]{0:T(256)(128)(2,1)S(1)} %dynamic-update-slice), channel_id=2, replica_groups=mesh['dp'=4,'latent'=32] {'latent'}, use_global_device_ids=true, to_apply=%add | all-reduce | flops 128 | bytes 512
  97.8 7.3 %multiply_reduce_fusion = (f32[512]{0:T(512)S(1)}, f32[128,512]{1,0:T(8,128)S(1)}) fusion(f32[128]{0:T(128)S(1)} %mul.102, f32[512]{0:T(512)} %param.11, bf16[8192,512]{1,0:T(8,128)(2,1)} %bitcast.33, bf16[128,1,8192]{2,1,0:T(2,128)(2,1)} %all-gather.3.cloned.1.call-done), kind=kOutput, calls=%fused_computation.26 | convolution fusion | flops 1074068992 | bytes 10752512 | tf_op jit(solution)/shard_map/dot_general | solution.py:44
  105.1 6.0 %convolution_convert_fusion = bf16[128,8192]{1,0:T(8,128)(2,1)} fusion(bf16[512,8192]{1,0:T(8,128)(2,1)} %param.12, f32[128,512]{1,0:T(8,128)S(1)} %get-tuple-element.16), kind=kOutput, calls=%fused_computation.6 | convolution fusion | flops 1074921472 | bytes 10747904 | tf_op jit(solution)/shard_map/dot_general | solution.py:48
  111.3 11.3 %convert_multiply_fusion.1 = f32[512,8192]{1,0:T(8,128)} fusion(bf16[512,8192]{1,0:T(8,128)(2,1)} %param.12), kind=kLoop, calls=%fused_computation.3 | loop fusion | flops 8388608 | bytes 25165824 | tf_op jit(solution)/shard_map/square | solution.py:38
  122.6 6.5 %slice_reduce_fusion.1 = (f32[512]{0:T(512)S(1)}, f32[512]{0:T(512)S(1)}) fusion(f32[512,8192]{1,0:T(8,128)} %convert_multiply_fusion.1), kind=kLoop, calls=%fused_computation.8 | loop fusion | flops 4193280 | bytes 16781312 | tf_op jit(solution)/shard_map/reduce_sum | solution.py:39
  129.2 8.8 %copy.19 = bf16[128,1,8192]{0,2,1:T(8,128)(2,1)S(1)} copy(bf16[128,1,8192]{2,1,0:T(2,128)(2,1)} %all-gather.3.cloned.1.call-done) | data formatting | bytes 4194304 | tf_op jit(solution)/shard_map/dot_general | solution.py:61
  138.6 75.9 %all-reduce.4.cloned.1.call-done = bf16[128,8192]{1,0:T(8,128)(2,1)} async-done(((bf16[128,8192]{1,0:T(8,128)(2,1)}), bf16[128,8192]{1,0:T(8,128)(2,1)}) %all-reduce.4.cloned.1.call-update) | async-done | bytes 2097168 | tf_op jit(solution)/shard_map/psum | solution.py:49
  214.5 8.7 %subtract_multiply_fusion = f32[128,8192]{1,0:T(8,128)} fusion(bf16[128,8192]{1,0:T(8,128)(2,1)} %all-reduce.4.cloned.1.call-done, f32[128]{0:T(128)S(1)} %mul.102, f32[8192]{0:T(1024)S(1)} %bitcast.36, bf16[128,1,8192]{2,1,0:T(2,128)(2,1)} %all-gather.3.cloned.1.call-done), kind=kLoop, calls=%fused_computation.12 | loop fusion | flops 5242880 | bytes 8421888 | tf_op jit(solution)/shard_map/mul | solution.py:50
  223.2 15.0 %convolution_convert_fusion.1 = bf16[2,4096,512]{2,1,0:T(8,128)(2,1)} fusion(bf16[2,4096,128]{2,1,0:T(8,128)(2,1)S(1)} %bitcast.34, f32[128,512]{1,0:T(8,128)S(1)} %get-tuple-element.16, bf16[512,8192]{1,0:T(8,128)(2,1)} %param.12, f32[128,8192]{1,0:T(8,128)} %subtract_multiply_fusion, f32[512]{0:T(512)S(1)} %get-tuple-element.10, f32[128]{0:T(128)S(1)} %mul.102), kind=kOutput, calls=%fused_computation.9 | convolution fusion | flops 2153119744 | bytes 23333376 | tf_op jit(solution)/shard_map/dot_general | solution.py:61
  238.3 9.8 %fusion.1 = bf16[512,8192]{1,0:T(8,128)(2,1)} fusion(bf16[512,8192]{1,0:T(8,128)(2,1)} %param.12, f32[512]{0:T(512)S(1)} %get-tuple-element.12, f32[512]{0:T(512)S(1)} %get-tuple-element.11, pred[8192]{0:T(1024)(128)(4,1)S(1)} %iota_compare_fusion, f32[128,8192]{1,0:T(8,128)} %subtract_multiply_fusion, f32[128,512]{1,0:T(8,128)S(1)} %get-tuple-element.16), kind=kOutput, calls=%fused_computation.5 | convolution fusion | flops 1100087296 | bytes 21245952 | tf_op jit(solution)/shard_map/dot_general | solution.py:65
  248.1 1.6 multiply_reduce_fusion.1
  251.0 69.5 %all-reduce.1 = (f32[]{:T(128)}, f32[]{:T(128)}) all-reduce(f32[]{:T(128)} %get-tuple-element.13, f32[]{:T(128)S(6)} %add.86), channel_id=1, replica_groups=mesh['dp'=4,'latent'=32] {'dp','latent'}, use_global_device_ids=true, to_apply=%region_6.7 | all-reduce | flops 2 | bytes 16 | tf_op jit(solution)/shard_map/psum | solution.py:78
  322.5 3.3 multiply_convert_fusion.1
  325.8 77.3 %reduce-scatter.5.cloned.1.call-done = bf16[512,2048]{1,0:T(8,128)(2,1)} async-done(((bf16[512,8192]{1,0:T(8,128)(2,1)}), bf16[512,2048]{1,0:T(8,128)(2,1)}) %reduce-scatter.5.cloned.1.call-update) | async-done | bytes 2097168 | tf_op jit(solution)/shard_map/reduce_scatter | solution.py:75
  403.2 3.4 multiply_convert_fusion
  (31 shorter events, 3.3 us)
Async XLA Ops:
  7.2 1.7 copy-start
  7.2 90.6 %all-gather.3.cloned.1.call-start = ((), (), s32[]{:S(2)}) async-start(), calls=%async_computation.4 | async-start | bytes 4325376 | tf_op jit(solution)/shard_map/all_gather | solution.py:29
  24.3 7.2 %all-to-all-start.1 = ((bf16[4,1,1]{2,1,0:T(2,128)(2,1)}), bf16[4,1,1]{2,1,0:T(2,128)(2,1)S(1)}, u32[]{:S(2)}, u32[]{:S(2)}) async-start(bf16[4,1,1]{2,1,0:T(2,128)(2,1)} %copy.17), calls=%async_computation.1 | async-start | bytes 4096 | tf_op jit(solution)/shard_map/all_to_all | solution.py:26
  27.5 187.0 %all-reduce.4.cloned.1.call-start = ((), (), s32[]{:S(2)}) async-start(), calls=%async_computation.5 | async-start | bytes 4194304 | tf_op jit(solution)/shard_map/psum | solution.py:49
  111.1 11.6 %copy-start.2 = (f32[2,4096]{1,0:T(2,128)S(1)}, f32[2,4096]{1,0:T(2,128)}, u32[]{:S(2)}) copy-start(f32[2,4096]{1,0:T(2,128)} %param.13) | copy-start | bytes 98308
  111.1 211.4 %reduce-scatter.3.cloned.1.call-start = ((), (), s32[]{:S(2)}) async-start(), calls=%async_computation.6 | async-start | bytes 10485760 | tf_op jit(solution)/shard_map/reduce_scatter | solution.py:72
  238.2 165.0 %reduce-scatter.5.cloned.1.call-start = ((), (), s32[]{:S(2)}) async-start(), calls=%async_computation.7 | async-start | bytes 10485760 | tf_op jit(solution)/shard_map/reduce_scatter | solution.py:75
  321.8 84.8 %copy-start.1 = (bf16[5,8192]{1,0:T(8,128)(2,1)S(1)}, bf16[5,8192]{1,0:T(8,128)(2,1)}, u32[]{:S(2)}) copy-start(bf16[5,8192]{1,0:T(8,128)(2,1)} %param.7) | copy-start | bytes 245764
Sparse Core Ops, SparseCore 0:
  21.8 47.3 all-gather.2
  111.2 103.2 all-reduce.3
  238.3 82.5 reduce-scatter.2
  323.2 79.8 reduce-scatter.4
where the time goes:
time: 415 us; the launch traced here: 414 us
  waiting for transfers between devices  155 us (37%)
  blocking collectives  145 us (35%)
  other arithmetic  38.6 us (9%)
  matrix products  38 us (9%)
  between operations  19.7 us (5%)
  local copies, waits for them, and re-layouts  13.6 us (3%)
    reduce_scatter x1, waiting for transfers between devices, shards(): lax.psum_scatter(dec_term.astype(jnp.bfloat16), 'dp', scatter_dimension=1...  77.3 us
    psum x1, waiting for transfers between devices, shards(): lax.psum(partial_value.astype(jnp.bfloat16), 'latent').astype(jnp.float32)  75.9 us
    psum x1, blocking collectives, shards(): total, count = lax.psum((local_loss, own_count), ('dp', 'latent'))  69.5 us
    unnamed x1, blocking collectives  65.9 us
    dot_general x1, matrix products, shards(): lax.dot_general(xg, dpre16, (((0,), (0,)), ((), ())), preferred_element_t...  15 us
    square x1, other arithmetic, shards(): squares_dec = jnp.square(w_dec.astype(jnp.float32))  11.3 us
    all_to_all x1, blocking collectives, shards(): lax.all_to_all(outgoing, 'dp', split_axis=0, concat_axis=0, tiled=True)  10.1 us
    dot_general x1, matrix products, shards(): lax.dot_general(feats16, err16, (((0,), (0,)), ((), ())), preferred_eleme...  9.77 us
  transfers between devices with their start and end apart: 5, of which 3 were waited for; matrix products, arithmetic and copies ran while one was open for 11% of the time, Pallas kernels for 0%

commit v1 on v0

v1 whole, which is shorter than its diff:
```python
import jax
import jax.numpy as jnp
from jax import lax
from jax.experimental import pallas as pl
from jax.experimental.pallas import tpu as pltpu
from jax.sharding import Mesh
from jax.sharding import PartitionSpec as P

sparsity_weight = 1.0
loss_scale = 8.0
norm_eps = 1e-06

ALL = ("z", "x", "y", "c")
NZ = 4
CHIPS = 16
WIDTH = 8192
HALF = 4096
SUB = 1024
LOCAL = 512
ROWS = 128
PAD = 128
MIB = 1 << 20
f32 = jnp.float32
bf16 = jnp.bfloat16

VM = pl.BlockSpec(memory_space=pltpu.VMEM)
SM = pl.BlockSpec(memory_space=pltpu.SMEM)


def call(body, outs, args, specs=None, scratch=(), vmem=None, flops=0, nbytes=0):
    return pl.pallas_call(
        body,
        out_shape=[jax.ShapeDtypeStruct(s, d) for s, d in outs],
        in_specs=specs or [VM] * len(args),
        out_specs=[VM] * len(outs),
        scratch_shapes=list(scratch),
        compiler_params=pltpu.CompilerParams(vmem_limit_bytes=vmem or 24 * MIB),
        cost_estimate=pl.CostEstimate(flops=flops, bytes_accessed=nbytes, transcendentals=0),
    )(*args)


def lanes(start, size):
    return pl.ds(pl.multiple_of(start, 128), size)


def split3(v):
    hi = v.astype(bf16)
    rest = v - hi.astype(f32)
    mid = rest.astype(bf16)
    low = (rest - mid.astype(f32)).astype(bf16)
    return hi, mid, low


def prep_kernel(who, length, acts, group, keep, send):
    c = who[1]
    slot = lax.broadcasted_iota(jnp.int32, (5, 1), 0)
    held = jnp.sum(jnp.where(group[...] == NZ, slot, 0), axis=0, keepdims=True)
    k = lax.broadcasted_iota(jnp.int32, (4, 1), 0)
    later = k >= held
    src = k + later.astype(jnp.int32)
    live = (src < length[0]).astype(f32)
    live = jnp.broadcast_to(live, (4, PAD)).astype(bf16)

    def pick(cols):
        rows = acts[:, cols].astype(f32)
        return jnp.where(later, rows[1:5], rows[0:4]).astype(bf16)

    for out, core in ((keep, c), (send, 1 - c)):
        out[:, :HALF] = pick(lanes(core * HALF, HALF))
        for q in range(NZ):
            out[:, HALF + q * SUB : HALF + (q + 1) * SUB] = pick(lanes(q * 2 * SUB + core * SUB, SUB))
        out[:, 2 * HALF :] = live


def join_kernel(who, own, other, out, mine):
    first = who[1] == 0
    a, b = own[...].astype(f32), other[...].astype(f32)
    rows = jnp.concatenate([jnp.where(first, a, b), jnp.where(first, b, a)], axis=0)
    mine[...] = rows[:, HALF:].astype(bf16)
    for i in range(CHIPS):
        out[i, :, :HALF] = rows[:, :HALF].astype(bf16)
        out[i, :, HALF:] = rows[:, 2 * HALF :].astype(bf16)


def encode_own_kernel(who, x, w_enc, acc, *slices):
    z, c = who[0], who[1]
    for n in range(0, LOCAL, 256):
        acc[:, n : n + 256] = jnp.dot(x[:, :HALF], w_enc[c, :, n : n + 256], preferred_element_type=f32)
    for k in range(NZ):
        dest = lax.rem(z + k, NZ)
        slices[k][...] = x[:, lanes(dest * SUB, SUB)]


def encode_kernel(who, x, w_enc, acc, bias, w_dec, act_out, feats_out, send):
    c = who[1]
    for n in range(0, LOCAL, 256):
        pre = acc[:, n : n + 256] + jnp.dot(
            x[:, :HALF], w_enc[1 - c, :, n : n + 256], preferred_element_type=f32
        )
        act = jnp.maximum(pre + bias[:, n : n + 256], 0.0)
        feats = act * act
        act_out[:, n : n + 256] = act
        feats_out[:ROWS, n : n + 256] = feats.astype(bf16)
        live = x[:, HALF : HALF + 1].astype(f32)
        fsum = jnp.sum(feats * live, axis=0, keepdims=True)
        hi, mid, low = split3(fsum)
        row = lax.broadcasted_iota(jnp.int32, (16, 256), 0)
        tail = jnp.where(row == 0, hi.astype(f32), jnp.where(row == 1, mid.astype(f32), low.astype(f32)))
        feats_out[ROWS:, n : n + 256] = jnp.where(row < 3, tail, 0.0).astype(bf16)
    feats16 = feats_out[:ROWS, :]
    for q in range(NZ):
        cols = lanes(q * 2 * SUB + (1 - c) * SUB, SUB)
        send[:, q * SUB : (q + 1) * SUB] = jnp.dot(feats16, w_dec[:, cols], preferred_element_type=f32).astype(bf16)


def decode_own_kernel(who, feats, w_dec, part, norm_rows, norm_cols):
    c = who[1]
    feats16 = feats[:ROWS, :]
    for q in range(NZ):
        cols = lanes(q * 2 * SUB + c * SUB, SUB)
        part[:, q * SUB : (q + 1) * SUB] = jnp.dot(feats16, w_dec[:, cols], preferred_element_type=f32)
    for s in range(2):
        for n in range(0, LOCAL, 128):
            def add(i, total):
                v = w_dec[n : n + 128, lanes(s * HALF + i * 256, 256)].astype(f32)
                v = v * v
                return total + v[:, :128] + v[:, 128:]

            total = lax.fori_loop(0, HALF // 256, add, jnp.zeros((128, 128), f32))
            norm_rows[s : s + 1, n : n + 128] = jnp.sqrt(jnp.sum(total.T, axis=0, keepdims=True) + norm_eps)
            norm_cols[n : n + 128, s : s + 1] = jnp.sqrt(jnp.sum(total, axis=1, keepdims=True) + norm_eps)


def add_kernel(own, other, out):
    for n in range(0, HALF, SUB):
        out[:, n : n + SUB] = (own[:, n : n + SUB] + other[:, n : n + SUB].astype(f32)).astype(bf16)


def err_kernel(who, parts, mine, bias, feats, norm_rows, out):
    c = who[1]
    live = mine[:, HALF : HALF + 1].astype(f32)
    square = jnp.zeros((8, SUB), f32)
    for q in range(NZ):
        cols = slice(q * SUB, (q + 1) * SUB)
        total = parts[0, :, cols].astype(f32)
        for i in range(1, CHIPS):
            total = total + parts[i, :, cols].astype(f32)
        add = bias[q // 2 : q // 2 + 1, lanes((q % 2) * 2 * SUB + c * SUB, SUB)]
        err = (total + add - mine[:, cols].astype(f32)) * live
        square = square + err * err
        err16 = err.astype(bf16)
        for i in range(CHIPS):
            out[i, :, cols] = err16
    squares = jnp.sum(jnp.sum(square, axis=0, keepdims=True), axis=1, keepdims=True)
    fsum = jnp.sum(feats[ROWS : ROWS + 16, :].astype(f32), axis=0, keepdims=True)
    nsum = norm_rows[0:1, :] + norm_rows[1:2, :]
    sparse = sparsity_weight * jnp.sum(fsum * nsum, axis=1, keepdims=True)
    hi, mid, low = split3(squares + sparse)
    lane = lax.broadcasted_iota(jnp.int32, (8, PAD), 1)
    row = lax.broadcasted_iota(jnp.int32, (8, PAD), 0)
    tail = jnp.where(lane == 0, hi.astype(f32), jnp.where(lane == 1, mid.astype(f32), low.astype(f32)))
    tail = jnp.where((row == 0) & (lane < 3), tail, 0.0).astype(bf16)
    for i in range(CHIPS):
        out[i, :, HALF:] = tail


def dfeat_own_kernel(who, e, w_dec, acc, *slices):
    z, c = who[0], who[1]
    for n in range(0, LOCAL, 256):
        total = jnp.zeros((ROWS, 256), f32)
        for q in range(NZ):
            w = w_dec[n : n + 256, lanes(q * 2 * SUB + c * SUB, SUB)]
            total = total + lax.dot_general(
                e[:, q * SUB : (q + 1) * SUB], w, (((1,), (1,)), ((), ())), preferred_element_type=f32
            )
        acc[:, n : n + 256] = total
    for k in range(NZ):
        dest = lax.rem(z + k, NZ)
        slices[k][...] = e[:, lanes(dest * SUB, SUB)]


def dpre_kernel(who, e, own, w_dec, acc, act, x, norm_rows, out):
    c = who[1]
    live = x[:, HALF : HALF + 1].astype(f32)
    for n in range(0, LOCAL, 256):
        total = acc[:, n : n + 256]
        for q in range(NZ):
            w = w_dec[n : n + 256, lanes(q * 2 * SUB + (1 - c) * SUB, SUB)]
            total = total + lax.dot_general(
                e[:, q * SUB : (q + 1) * SUB], w, (((1,), (1,)), ((), ())), preferred_element_type=f32
            )
        nsum = norm_rows[0:1, n : n + 256] + norm_rows[1:2, n : n + 256]
        dfeat = 2.0 * total + sparsity_weight * live * nsum
        out[:ROWS, n : n + 256] = (dfeat * 2.0 * act[:, n : n + 256]).astype(bf16)
    tail = e[:, HALF:].astype(f32) + own[:, HALF:].astype(f32)
    both = jnp.sum(jnp.sum(e[:, HALF:].astype(f32), axis=0, keepdims=True), axis=1, keepdims=True)
    both = both + jnp.sum(jnp.sum(own[:, HALF:].astype(f32), axis=0, keepdims=True), axis=1, keepdims=True)
    del tail
    count = jnp.sum(live, axis=0, keepdims=True)
    hi, mid, low = split3(both)
    lane = lax.broadcasted_iota(jnp.int32, (16, LOCAL), 1)
    row = lax.broadcasted_iota(jnp.int32, (16, LOCAL), 0)
    tail = jnp.where(
        lane == 0,
        hi.astype(f32),
        jnp.where(lane == 1, mid.astype(f32), jnp.where(lane == 2, low.astype(f32), count)),
    )
    out[ROWS:, :] = jnp.where((row == 0) & (lane < 4), tail, 0.0).astype(bf16)


def totals(pres):
    total = jnp.zeros((1, 1), f32)
    count = jnp.zeros((1, 1), f32)
    for p in pres:
        row = p[ROWS : ROWS + 1, 0:PAD].astype(f32)
        lane = lax.broadcasted_iota(jnp.int32, (1, PAD), 1)
        total = total + jnp.sum(jnp.where(lane < 3, row, 0.0), axis=1, keepdims=True)
        count = count + jnp.sum(jnp.where(lane == 3, row, 0.0), axis=1, keepdims=True)
    return total, count


def grad_enc_kernel(who, *refs):
    c = who[1]
    own, other, pres = refs[0:4], refs[4:8], refs[8:12]
    out, loss, xs, ds = refs[12:]
    total, count = totals(pres)
    loss[...] = total / (count * WIDTH)
    factor = loss_scale / count
    for k in range(NZ):
        ds[k * ROWS : (k + 1) * ROWS, :] = pres[k][:ROWS, :]
    for side, group in ((c, own), (1 - c, other)):
        for k in range(NZ):
            xs[k * ROWS : (k + 1) * ROWS, :] = group[k][...]
        for n in range(0, SUB, 256):
            part = lax.dot_general(
                xs[:, n : n + 256], ds[...], (((0,), (0,)), ((), ())), preferred_element_type=f32
            )
            out[side, n : n + 256, :] = (part * factor).astype(bf16)


def grad_dec_kernel(who, *refs):
    z, c = who[0], who[1]
    own, other, feats, pres = refs[0:4], refs[4:8], refs[8:12], refs[12:16]
    norm_cols, w_dec, out, es, fs = refs[16:]
    _, count = totals(pres)
    factor = loss_scale / count
    fsum = jnp.zeros((16, LOCAL), f32)
    for k in range(NZ):
        fs[k * ROWS : (k + 1) * ROWS, :] = feats[k][:ROWS, :]
        fsum = fsum + feats[k][ROWS:, :].astype(f32)
    fsum = jnp.sum(jnp.broadcast_to(jnp.sum(fsum, axis=0, keepdims=True), (128, LOCAL)).T, axis=1, keepdims=True) * (1.0 / 128.0)
    norm = jnp.where(z < 2, norm_cols[:, 0:1], norm_cols[:, 1:2])
    scale = sparsity_weight * fsum / norm
    for side, group in ((c, own), (1 - c, other)):
        for k in range(NZ):
            es[k * ROWS : (k + 1) * ROWS, :] = group[k][...]
        for n in range(0, LOCAL, 256):
            part = 2.0 * lax.dot_general(
                fs[:, n : n + 256], es[...], (((0,), (0,)), ((), ())), preferred_element_type=f32
            )
            w = w_dec[n : n + 256, lanes(z * 2 * SUB + side * SUB, SUB)].astype(f32)
            part = part + scale[n : n + 256, :] * w
            out[n : n + 256, lanes(side * SUB, SUB)] = (part * factor).astype(bf16)


def swap(v):
    return lax.ppermute(v, "c", [(0, 1), (1, 0)])


def shift(v, k):
    return lax.ppermute(v, "z", [(i, (i + k) % NZ) for i in range(NZ)])


def shards(acts, chat_len, group_of, w_enc, b_enc, w_dec, b_dec):
    who = jnp.stack([lax.axis_index("z"), lax.axis_index("c")]).astype(jnp.int32)
    keep, send = call(
        prep_kernel,
        [((4, 2 * HALF + PAD), bf16)] * 2,
        (who, chat_len, acts, group_of),
        [SM, SM, VM, VM],
    )
    block, mine = call(
        join_kernel,
        [((CHIPS, 8, HALF + PAD), bf16), ((8, HALF + PAD), bf16)],
        (who, keep, swap(send)),
        [SM, VM, VM],
    )
    x_own = lax.all_to_all(block, ("x", "y"), split_axis=0, concat_axis=0, tiled=True).reshape(ROWS, HALF + PAD)
    x_other = swap(x_own)
    acc, *x_slices = call(
        encode_own_kernel,
        [((ROWS, LOCAL), f32)] + [((ROWS, SUB), bf16)] * NZ,
        (who, x_own, w_enc),
        [SM, VM, VM],
        flops=2 * ROWS * HALF * LOCAL,
        nbytes=6 * MIB,
    )
    act, feats, part_send = call(
        encode_kernel,
        [((ROWS, LOCAL), f32), ((ROWS + 16, LOCAL), bf16), ((ROWS, HALF), bf16)],
        (who, x_other, w_enc, acc, b_enc.reshape(1, LOCAL), w_dec),
        [SM, VM, VM, VM, VM, VM],
        flops=4 * ROWS * HALF * LOCAL,
        nbytes=12 * MIB,
    )
    part_recv = swap(part_send)
    part_own, norm_rows, norm_cols = call(
        decode_own_kernel,
        [((ROWS, HALF), f32), ((2, LOCAL), f32), ((LOCAL, 2), f32)],
        (who, feats, w_dec),
        [SM, VM, VM],
        flops=2 * ROWS * HALF * LOCAL,
        nbytes=10 * MIB,
    )
    (part,) = call(add_kernel, [((ROWS, HALF), bf16)], (part_own, part_recv))
    parts = lax.all_to_all(part.reshape(CHIPS, 8, HALF), ("x", "y"), split_axis=0, concat_axis=0, tiled=True)
    (block,) = call(
        err_kernel,
        [((CHIPS, 8, HALF + PAD), bf16)],
        (who, parts, mine, b_dec, feats, norm_rows),
        [SM] + [VM] * 5,
    )
    e_own = lax.all_to_all(block, ("x", "y"), split_axis=0, concat_axis=0, tiled=True).reshape(ROWS, HALF + PAD)
    e_other = swap(e_own)
    acc, *e_slices = call(
        dfeat_own_kernel,
        [((ROWS, LOCAL), f32)] + [((ROWS, SUB), bf16)] * NZ,
        (who, e_own, w_dec),
        [SM, VM, VM],
        flops=2 * ROWS * HALF * LOCAL,
        nbytes=6 * MIB,
    )
    (dpre,) = call(
        dpre_kernel,
        [((ROWS + 16, LOCAL), bf16)],
        (who, e_other, e_own, w_dec, acc, act, x_own, norm_rows),
        [SM] + [VM] * 7,
        flops=2 * ROWS * HALF * LOCAL,
        nbytes=6 * MIB,
    )

    def around(pieces):
        return [pieces[0]] + [shift(pieces[k], k) for k in range(1, NZ)]

    xs = around(x_slices)
    fs = around([feats] * NZ)
    es = around(e_slices)
    ds = around([dpre] * NZ)
    xs_other = [swap(v) for v in xs]
    es_other = [swap(v) for v in es]
    grad_enc, loss = call(
        grad_enc_kernel,
        [((2, SUB, LOCAL), bf16), ((1, 1), f32)],
        (who, *xs, *xs_other, *ds),
        [SM] + [VM] * 12,
        [pltpu.VMEM((NZ * ROWS, SUB), bf16), pltpu.VMEM((NZ * ROWS, LOCAL), bf16)],
        flops=2 * NZ * ROWS * 2 * SUB * LOCAL,
        nbytes=5 * MIB,
    )
    (grad_dec,) = call(
        grad_dec_kernel,
        [((LOCAL, 2 * SUB), bf16)],
        (who, *es, *es_other, *fs, *ds, norm_cols, w_dec),
        [SM] + [VM] * 18,
        [pltpu.VMEM((NZ * ROWS, SUB), bf16), pltpu.VMEM((NZ * ROWS, LOCAL), bf16)],
        flops=2 * NZ * ROWS * 2 * SUB * LOCAL,
        nbytes=7 * MIB,
    )
    return grad_enc, grad_dec, loss.reshape(())


def solution(mesh):
    fine = Mesh(mesh.devices.reshape(4, 4, 4, 2), ALL)
    lat = ("x", "y", "c")
    return jax.shard_map(
        shards,
        mesh=fine,
        in_specs=(P(ALL, None), P(ALL), P(ALL, None), P(None, None, lat), P(lat), P(lat, None), P()),
        out_specs=(P(None, "z", lat), P(lat, "z"), P()),
        check_vma=False,
    )
```

time: 415 us -> 149 us (0.36)
  waiting for transfers between devices: 155 us -> 29.2 us
  blocking collectives: 145 us -> 61.6 us
  other arithmetic: 38.6 us -> 0.08 us
  matrix products: 38 us -> 0 us
  Pallas kernels: 0 us -> 21.3 us
  starting transfers between devices: 3.57 us -> 24.2 us
  between operations: 19.7 us -> 1.41 us
    reduce_scatter x2 -> x0, waiting for transfers between devices: 77.4 us -> none  [the longest x1 77.3 us: shards(): lax.psum_scatter(dec_term.astype(jnp.bfloat16), 'dp', scatter_dimension=1...]
    psum x1 -> x0, waiting for transfers between devices: 75.9 us -> none  [shards(): lax.psum(partial_value.astype(jnp.bfloat16), 'latent').astype(jnp.float32)]
    psum x1 -> x0, blocking collectives: 69.5 us -> none  [shards(): total, count = lax.psum((local_loss, own_count), ('dp', 'latent'))]
    unnamed x1 -> x0, blocking collectives: 65.9 us -> none
    all_to_all x1 -> x3, blocking collectives: 10.1 us -> 61.6 us  [the longest x2 42.9 us: shards(): lax.all_to_all(block, ('x', 'y'), split_axis=0, concat_axis=0, tiled=True)]
    dot_general x4 -> x0, matrix products: 38 us -> none  [the longest x1 15 us: shards(): lax.dot_general(xg, dpre16, (((0,), (0,)), ((), ())), preferred_element_t...]
    ppermute x0 -> x24, waiting for transfers between devices: none -> 29.2 us  [the longest x12 28.3 us: shift(): return lax.ppermute(v, 'z', [(i, (i + k) % NZ) for i in range(NZ)])]
    ppermute x0 -> x24, starting transfers between devices: none -> 24.2 us  [the longest x12 13.3 us: shift(): return lax.ppermute(v, 'z', [(i, (i + k) % NZ) for i in range(NZ)])]
  transfers between devices with their start and end apart: 5 -> 24, of which waited for: 3 -> 9; matrix products, arithmetic and copies ran while one was open for 11% -> 0% of each run, Pallas kernels for 0% -> 9%
where the time goes in v1:
time: 149 us; the launch traced here: 148 us
  blocking collectives  61.6 us (41%)
  waiting for transfers between devices  29.2 us (20%)
  starting transfers between devices  24.2 us (16%)
  Pallas kernels  21.3 us (14%)
  local copies, waits for them, and re-layouts  10.5 us (7%)
    all_to_all x2, blocking collectives, shards(): lax.all_to_all(block, ('x', 'y'), split_axis=0, concat_axis=0, tiled=True)  42.9 us
    ppermute x12, waiting for transfers between devices, shift(): return lax.ppermute(v, 'z', [(i, (i + k) % NZ) for i in range(NZ)])  28.3 us
    pallas_call x11, Pallas kernels, call(): pl.pallas_call(body, out_shape=[jax.ShapeDtypeStruct(s, d) for s, d in ou...  21.3 us
    all_to_all x1, blocking collectives, shards(): lax.all_to_all(part.reshape(CHIPS, 8, HALF), ('x', 'y'), split_axis=0, co...  18.7 us
    ppermute x12, starting transfers between devices, shift(): return lax.ppermute(v, 'z', [(i, (i + k) % NZ) for i in range(NZ)])  13.3 us
    ppermute x12, starting transfers between devices, swap(): return lax.ppermute(v, 'c', [(0, 1), (1, 0)])  10.9 us
    unnamed x13, local copies, waits for them, and re-layouts  10.5 us
  transfers between devices with their start and end apart: 24, of which 9 were waited for; matrix products, arithmetic and copies ran while one was open for 0% of the time, Pallas kernels for 9%

profile of v1, /device:TPU:1, one launch (start us, length us, event | category | flops | bytes accessed | tf_op | source)
XLA Modules:
  0.0 148.3 jit_solution(17268201868486309365)
XLA Ops:
  6.7 23.7 %all_to_all.15 = bf16[16,8,4224]{2,1,0:T(8,128)(2,1)S(1)} all-to-all(bf16[16,8,4224]{2,1,0:T(8,128)(2,1)S(1)} %get-tuple-element.27), channel_id=1, replica_groups=mesh['z'=4,'x'=4,'y'=4,'c'=2] {'x','y'}, dimensions={0} | all-to-all | bytes 2162688 | tf_op jit(solution)/shard_map/all_to_all | solution.py:288
  32.0 3.4 %copy-done.1 = bf16[2,4096,512]{2,1,0:T(8,128)(2,1)S(1)} copy-done((bf16[2,4096,512]{2,1,0:T(8,128)(2,1)S(1)}, bf16[2,4096,512]{2,1,0:T(8,128)(2,1)}, u32[]{:S(2)}) %copy-start.1) | copy-done | bytes 8388632
  36.6 2.1 %copy-done = bf16[512,8192]{1,0:T(8,128)(2,1)S(1)} copy-done((bf16[512,8192]{1,0:T(8,128)(2,1)S(1)}, bf16[512,8192]{1,0:T(8,128)(2,1)}, u32[]{:S(2)}) %copy-start) | copy-done | bytes 8388632
  38.7 3.4 %copy-done.2 = bf16[2,4096,512]{2,1,0:T(8,128)(2,1)S(1)} copy-done((bf16[2,4096,512]{2,1,0:T(8,128)(2,1)S(1)}, bf16[2,4096,512]{2,1,0:T(8,128)(2,1)}, u32[]{:S(2)}) %copy-start.2) | copy-done | bytes 8388632
  42.1 2.0 %shard_map.97 = (f32[128,512]{1,0:T(8,128)S(1)}, bf16[144,512]{1,0:T(8,128)(2,1)S(1)}, bf16[128,4096]{1,0:T(8,128)(2,1)S(1)}) custom-call(s32[2]{0:T(128)S(1)} %pad_add_fusion.who, bf16[128,4224]{1,0:T(8,128)(2,1)S(1)} %collective-permute-done.8.x, bf16[2,4096,512]{2,1,0:T(8,128)(2,1)S(1)} %copy-done.2, f32[128,512]{1,0:T(8,128)S(1)} %get-tuple-element.32.acc, ...), custom_call_target="tpu_custom_call" | custom-call | flops 1073741824 | bytes 12582912 | tf_op jit(solution)/shard_map/pallas_call | solution.py:31
  44.2 4.6 %shard_map.98 = (f32[128,4096]{1,0:T(8,128)S(1)}, f32[2,512]{1,0:T(2,128)S(1)}, f32[512,2]{1,0:T(8,128)S(1)}) custom-call(s32[2]{0:T(128)S(1)} %pad_add_fusion.who, bf16[144,512]{1,0:T(8,128)(2,1)S(1)} %get-tuple-element.33.feats.refs_8_, bf16[512,8192]{1,0:T(8,128)(2,1)S(1)} %copy-done), custom_call_target="tpu_custom_call" | custom-call | flops 536870912 | bytes 10485760 | tf_op jit(solution)/shard_map/pallas_call | solution.py:31
  49.1 18.7 %all_to_all.16.parts = bf16[16,8,4096]{2,1,0:T(8,128)(2,1)S(1)} all-to-all(bf16[16,8,4096]{2,1,0:T(8,128)(2,1)S(1)} %bitcast.13), channel_id=1, replica_groups=mesh['z'=4,'x'=4,'y'=4,'c'=2] {'x','y'}, dimensions={0} | all-to-all | bytes 2097152 | tf_op jit(solution)/shard_map/all_to_all | solution.py:316
  68.6 19.2 %all_to_all.17 = bf16[16,8,4224]{2,1,0:T(8,128)(2,1)S(1)} all-to-all(bf16[16,8,4224]{2,1,0:T(8,128)(2,1)S(1)} %shard_map.100), channel_id=1, replica_groups=mesh['z'=4,'x'=4,'y'=4,'c'=2] {'x','y'}, dimensions={0} | all-to-all | bytes 2162688 | tf_op jit(solution)/shard_map/all_to_all | solution.py:323
  87.8 3.0 %collective-permute-start.10 = (bf16[128,4224]{1,0:T(8,128)(2,1)S(1)}, bf16[128,4224]{1,0:T(8,128)(2,1)S(1)}, u32[]{:S(2)}, u32[]{:S(2)}) collective-permute-start(bf16[128,4224]{1,0:T(8,128)(2,1)S(1)} %bitcast.10), channel_id=1, source_target_pairs={{0,1},{1,0},{2,3},{3,2},{4,5},{5,4},{6,7},{7,6},{8,9},{9,8},{10,11... | collective-permute-start | bytes 3244040 | tf_op jit(solution)/shard_map/ppermute | solution.py:267
  92.4 3.3 %collective-permute-start.2 = (bf16[128,1024]{1,0:T(8,128)(2,1)S(1)}, bf16[128,1024]{1,0:T(8,128)(2,1)S(1)}, u32[]{:S(2)}, u32[]{:S(2)}) collective-permute-start(bf16[128,1024]{1,0:T(8,128)(2,1)S(1)} %get-tuple-element.30), channel_id=1, source_target_pairs={{0,64},{32,96},{64,0},{96,32},{1,65},{33,97},{65,1},{97,33},{2,66}... | collective-permute-start | bytes 786440 | tf_op jit(solution)/shard_map/ppermute | solution.py:271
  97.3 3.9 %collective-permute-done.1.refs_1_ = bf16[128,1024]{1,0:T(8,128)(2,1)S(1)} collective-permute-done((bf16[128,1024]{1,0:T(8,128)(2,1)S(1)}, bf16[128,1024]{1,0:T(8,128)(2,1)S(1)}, u32[]{:S(2)}, u32[]{:S(2)}) %collective-permute-start.1) | collective-permute-done | bytes 262176 | tf_op jit(solution)/shard_map/ppermute | solution.py:271
  101.8 6.0 %collective-permute-done.2.refs_2_ = bf16[128,1024]{1,0:T(8,128)(2,1)S(1)} collective-permute-done((bf16[128,1024]{1,0:T(8,128)(2,1)S(1)}, bf16[128,1024]{1,0:T(8,128)(2,1)S(1)}, u32[]{:S(2)}, u32[]{:S(2)}) %collective-permute-start.2) | collective-permute-done | bytes 262176 | tf_op jit(solution)/shard_map/ppermute | solution.py:271
  108.6 2.0 %shard_map.101 = (f32[128,512]{1,0:T(8,128)S(1)}, bf16[128,1024]{1,0:T(8,128)(2,1)S(1)}, bf16[128,1024]{1,0:T(8,128)(2,1)S(1)}, bf16[128,1024]{1,0:T(8,128)(2,1)S(1)}, bf16[128,1024]{1,0:T(8,128)(2,1)S(1)}) custom-call(s32[2]{0:T(128)S(1)} %pad_add_fusion.who, bf16[128,4224]{1,0:T(8,128)(2,1)S(1)} %bitcast.11, bf16[512,8192]{1,0:T(8,128)(2,1)S(1)} %copy-done), custom_call_target="tpu_custom_call" | custom-call | flops 536870912 | bytes 6291456 | tf_op jit(solution)/shard_map/pallas_call | solution.py:31
  112.4 2.2 %collective-permute-start.22 = (bf16[144,512]{1,0:T(8,128)(2,1)S(1)}, bf16[144,512]{1,0:T(8,128)(2,1)S(1)}, u32[]{:S(2)}, u32[]{:S(2)}) collective-permute-start(bf16[144,512]{1,0:T(8,128)(2,1)S(1)} %get-tuple-element.33.feats.refs_8_), channel_id=1, source_target_pairs={{0,64},{32,96},{64,0},{96,32},{1,65},{33,97},{65,1},{97,33},{2,66}... | collective-permute-start | bytes 442376 | tf_op jit(solution)/shard_map/ppermute | solution.py:271
  115.3 1.9 %collective-permute-start.16 = (bf16[128,1024]{1,0:T(8,128)(2,1)S(1)}, bf16[128,1024]{1,0:T(8,128)(2,1)S(1)}, u32[]{:S(2)}, u32[]{:S(2)}) collective-permute-start(bf16[128,1024]{1,0:T(8,128)(2,1)S(1)} %get-tuple-element.44), channel_id=1, source_target_pairs={{0,96},{32,0},{64,32},{96,64},{1,97},{33,1},{65,33},{97,65},{2,98}... | collective-permute-start | bytes 786440 | tf_op jit(solution)/shard_map/ppermute | solution.py:271
  117.2 2.1 %shard_map.102.refs_8_.refs_12_ = bf16[144,512]{1,0:T(8,128)(2,1)S(1)} custom-call(s32[2]{0:T(128)S(1)} %pad_add_fusion.who, bf16[128,4224]{1,0:T(8,128)(2,1)S(1)} %collective-permute-done.10.e, bf16[128,4224]{1,0:T(8,128)(2,1)S(1)} %bitcast.12, bf16[512,8192]{1,0:T(8,128)(2,1)S(1)} %copy-done, f32[128,512]{1,0:T(8,128)S(1)} %get-tuple-element.38.acc, ...), custom_call_target="tpu_custom_call" | custom-call | flops 536870912 | bytes 6291456 | tf_op jit(solution)/shard_map/pallas_call | solution.py:31
  119.3 3.2 %collective-permute-done.21.refs_9_ = bf16[144,512]{1,0:T(8,128)(2,1)S(1)} collective-permute-done((bf16[144,512]{1,0:T(8,128)(2,1)S(1)}, bf16[144,512]{1,0:T(8,128)(2,1)S(1)}, u32[]{:S(2)}, u32[]{:S(2)}) %collective-permute-start.21) | collective-permute-done | bytes 147488 | tf_op jit(solution)/shard_map/ppermute | solution.py:271
  122.7 3.8 %collective-permute-done.22.refs_10_ = bf16[144,512]{1,0:T(8,128)(2,1)S(1)} collective-permute-done((bf16[144,512]{1,0:T(8,128)(2,1)S(1)}, bf16[144,512]{1,0:T(8,128)(2,1)S(1)}, u32[]{:S(2)}, u32[]{:S(2)}) %collective-permute-start.22) | collective-permute-done | bytes 147488 | tf_op jit(solution)/shard_map/ppermute | solution.py:271
  127.3 4.8 %collective-permute-done.15.refs_2_ = bf16[128,1024]{1,0:T(8,128)(2,1)S(1)} collective-permute-done((bf16[128,1024]{1,0:T(8,128)(2,1)S(1)}, bf16[128,1024]{1,0:T(8,128)(2,1)S(1)}, u32[]{:S(2)}, u32[]{:S(2)}) %collective-permute-start.15) | collective-permute-done | bytes 262176 | tf_op jit(solution)/shard_map/ppermute | solution.py:271
  133.3 2.5 %collective-permute-done.11.refs_9_.refs_13_ = bf16[144,512]{1,0:T(8,128)(2,1)S(1)} collective-permute-done((bf16[144,512]{1,0:T(8,128)(2,1)S(1)}, bf16[144,512]{1,0:T(8,128)(2,1)S(1)}, u32[]{:S(2)}, u32[]{:S(2)}) %collective-permute-start.11) | collective-permute-done | bytes 147488 | tf_op jit(solution)/shard_map/ppermute | solution.py:271
  136.4 2.0 %collective-permute-done.12.refs_10_.refs_14_ = bf16[144,512]{1,0:T(8,128)(2,1)S(1)} collective-permute-done((bf16[144,512]{1,0:T(8,128)(2,1)S(1)}, bf16[144,512]{1,0:T(8,128)(2,1)S(1)}, u32[]{:S(2)}, u32[]{:S(2)}) %collective-permute-start.12) | collective-permute-done | bytes 147488 | tf_op jit(solution)/shard_map/ppermute | solution.py:271
  139.3 3.4 %shard_map.103 = (bf16[2,1024,512]{2,1,0:T(8,128)(2,1)}, f32[1,1]{1,0:T(1,128)}) custom-call(s32[2]{0:T(128)S(1)} %pad_add_fusion.who, bf16[128,1024]{1,0:T(8,128)(2,1)S(1)} %get-tuple-element.28.refs_0_, bf16[128,1024]{1,0:T(8,128)(2,1)S(1)} %collective-permute-done.1.refs_1_, bf16[128,1024]{1,0:T(8,128)(2,1)S(1)} %collective-permute-done.2.refs_2_, ...), custom_call_target="tpu_custom_call" | custom-call | flops 1073741824 | bytes 5242880 | tf_op jit(solution)/shard_map/pallas_call | solution.py:31
  142.6 2.1 %collective-permute-done.23.refs_11_ = bf16[144,512]{1,0:T(8,128)(2,1)S(1)} collective-permute-done((bf16[144,512]{1,0:T(8,128)(2,1)S(1)}, bf16[144,512]{1,0:T(8,128)(2,1)S(1)}, u32[]{:S(2)}, u32[]{:S(2)}) %collective-permute-start.23) | collective-permute-done | bytes 147488 | tf_op jit(solution)/shard_map/ppermute | solution.py:271
  144.8 3.6 %shard_map.104 = bf16[512,2048]{1,0:T(8,128)(2,1)} custom-call(s32[2]{0:T(128)S(1)} %pad_add_fusion.who, bf16[128,1024]{1,0:T(8,128)(2,1)S(1)} %get-tuple-element.41.refs_0_, bf16[128,1024]{1,0:T(8,128)(2,1)S(1)} %collective-permute-done.14.refs_1_, bf16[128,1024]{1,0:T(8,128)(2,1)S(1)} %collective-permute-done.15.refs_2_, ...), custom_call_target="tpu_custom_call" | custom-call | flops 1073741824 | bytes 7340032 | tf_op jit(solution)/shard_map/pallas_call | solution.py:31
  (52 shorter events, 20.1 us)
Async XLA Ops:
  3.7 2.4 %collective-permute-start = (bf16[4,8320]{1,0:T(4,128)(2,1)S(1)}, bf16[4,8320]{1,0:T(4,128)(2,1)S(1)}, u32[]{:S(2)}, u32[]{:S(2)}) collective-permute-start(bf16[4,8320]{1,0:T(4,128)(2,1)S(1)} %get-tuple-element.26), channel_id=1, source_target_pairs={{0,1},{1,0},{2,3},{3,2},{4,5},{5,4},{6,7},{7,6},{8,9},{9,8},{10,11... | collective-permute-start | bytes 199688 | tf_op jit(solution)/shard_map/ppermute | solution.py:267
  30.5 6.1 %collective-permute-start.8 = (bf16[128,4224]{1,0:T(8,128)(2,1)S(1)}, bf16[128,4224]{1,0:T(8,128)(2,1)S(1)}, u32[]{:S(2)}, u32[]{:S(2)}) collective-permute-start(bf16[128,4224]{1,0:T(8,128)(2,1)S(1)} %bitcast.7), channel_id=1, source_target_pairs={{0,1},{1,0},{2,3},{3,2},{4,5},{5,4},{6,7},{7,6},{8,9},{9,8},{10,11... | collective-permute-start | bytes 3244040 | tf_op jit(solution)/shard_map/ppermute | solution.py:267
  44.1 4.7 %collective-permute-start.9 = (bf16[128,4096]{1,0:T(8,128)(2,1)S(1)}, bf16[128,4096]{1,0:T(8,128)(2,1)S(1)}, u32[]{:S(2)}, u32[]{:S(2)}) collective-permute-start(bf16[128,4096]{1,0:T(8,128)(2,1)S(1)} %get-tuple-element.35), channel_id=1, source_target_pairs={{0,1},{1,0},{2,3},{3,2},{4,5},{5,4},{6,7},{7,6},{8,9},{9,8},{10,11... | collective-permute-start | bytes 3145736 | tf_op jit(solution)/shard_map/ppermute | solution.py:267
  87.8 27.5 %collective-permute-start.10 = (bf16[128,4224]{1,0:T(8,128)(2,1)S(1)}, bf16[128,4224]{1,0:T(8,128)(2,1)S(1)}, u32[]{:S(2)}, u32[]{:S(2)}) collective-permute-start(bf16[128,4224]{1,0:T(8,128)(2,1)S(1)} %bitcast.10), channel_id=1, source_target_pairs={{0,1},{1,0},{2,3},{3,2},{4,5},{5,4},{6,7},{7,6},{8,9},{9,8},{10,11... | collective-permute-start | bytes 3244040 | tf_op jit(solution)/shard_map/ppermute | solution.py:267
  90.8 10.4 %collective-permute-start.1 = (bf16[128,1024]{1,0:T(8,128)(2,1)S(1)}, bf16[128,1024]{1,0:T(8,128)(2,1)S(1)}, u32[]{:S(2)}, u32[]{:S(2)}) collective-permute-start(bf16[128,1024]{1,0:T(8,128)(2,1)S(1)} %get-tuple-element.29), channel_id=1, source_target_pairs={{0,32},{32,64},{64,96},{96,0},{1,33},{33,65},{65,97},{97,1},{2,34}... | collective-permute-start | bytes 786440 | tf_op jit(solution)/shard_map/ppermute | solution.py:271
  92.4 15.4 %collective-permute-start.2 = (bf16[128,1024]{1,0:T(8,128)(2,1)S(1)}, bf16[128,1024]{1,0:T(8,128)(2,1)S(1)}, u32[]{:S(2)}, u32[]{:S(2)}) collective-permute-start(bf16[128,1024]{1,0:T(8,128)(2,1)S(1)} %get-tuple-element.30), channel_id=1, source_target_pairs={{0,64},{32,96},{64,0},{96,32},{1,65},{33,97},{65,1},{97,33},{2,66}... | collective-permute-start | bytes 786440 | tf_op jit(solution)/shard_map/ppermute | solution.py:271
  95.7 12.9 %collective-permute-start.3 = (bf16[128,1024]{1,0:T(8,128)(2,1)S(1)}, bf16[128,1024]{1,0:T(8,128)(2,1)S(1)}, u32[]{:S(2)}, u32[]{:S(2)}) collective-permute-start(bf16[128,1024]{1,0:T(8,128)(2,1)S(1)} %get-tuple-element.31), channel_id=1, source_target_pairs={{0,96},{32,0},{64,32},{96,64},{1,97},{33,1},{65,33},{97,65},{2,98}... | collective-permute-start | bytes 786440 | tf_op jit(solution)/shard_map/ppermute | solution.py:271
  96.4 14.2 %collective-permute-start.4 = (bf16[128,1024]{1,0:T(8,128)(2,1)S(1)}, bf16[128,1024]{1,0:T(8,128)(2,1)S(1)}, u32[]{:S(2)}, u32[]{:S(2)}) collective-permute-start(bf16[128,1024]{1,0:T(8,128)(2,1)S(1)} %get-tuple-element.28.refs_0_), channel_id=1, source_target_pairs={{0,1},{1,0},{2,3},{3,2},{4,5},{5,4},{6,7},{7,6},{8,9},{9,8},{10,11... | collective-permute-start | bytes 786440 | tf_op jit(solution)/shard_map/ppermute | solution.py:267
  101.2 10.4 %collective-permute-start.5 = (bf16[128,1024]{1,0:T(8,128)(2,1)S(1)}, bf16[128,1024]{1,0:T(8,128)(2,1)S(1)}, u32[]{:S(2)}, u32[]{:S(2)}) collective-permute-start(bf16[128,1024]{1,0:T(8,128)(2,1)S(1)} %collective-permute-done.1.refs_1_), channel_id=1, source_target_pairs={{0,1},{1,0},{2,3},{3,2},{4,5},{5,4},{6,7},{7,6},{8,9},{9,8},{10,11... | collective-permute-start | bytes 786440 | tf_op jit(solution)/shard_map/ppermute | solution.py:267
  107.8 4.5 %collective-permute-start.6 = (bf16[128,1024]{1,0:T(8,128)(2,1)S(1)}, bf16[128,1024]{1,0:T(8,128)(2,1)S(1)}, u32[]{:S(2)}, u32[]{:S(2)}) collective-permute-start(bf16[128,1024]{1,0:T(8,128)(2,1)S(1)} %collective-permute-done.2.refs_2_), channel_id=1, source_target_pairs={{0,1},{1,0},{2,3},{3,2},{4,5},{5,4},{6,7},{7,6},{8,9},{9,8},{10,11... | collective-permute-start | bytes 786440 | tf_op jit(solution)/shard_map/ppermute | solution.py:267
  108.6 6.0 %collective-permute-start.7 = (bf16[128,1024]{1,0:T(8,128)(2,1)S(1)}, bf16[128,1024]{1,0:T(8,128)(2,1)S(1)}, u32[]{:S(2)}, u32[]{:S(2)}) collective-permute-start(bf16[128,1024]{1,0:T(8,128)(2,1)S(1)} %collective-permute-done.3.refs_3_), channel_id=1, source_target_pairs={{0,1},{1,0},{2,3},{3,2},{4,5},{5,4},{6,7},{7,6},{8,9},{9,8},{10,11... | collective-permute-start | bytes 786440 | tf_op jit(solution)/shard_map/ppermute | solution.py:267
  110.7 16.7 %collective-permute-start.14 = (bf16[128,1024]{1,0:T(8,128)(2,1)S(1)}, bf16[128,1024]{1,0:T(8,128)(2,1)S(1)}, u32[]{:S(2)}, u32[]{:S(2)}) collective-permute-start(bf16[128,1024]{1,0:T(8,128)(2,1)S(1)} %get-tuple-element.42), channel_id=1, source_target_pairs={{0,32},{32,64},{64,96},{96,0},{1,33},{33,65},{65,97},{97,1},{2,34}... | collective-permute-start | bytes 786440 | tf_op jit(solution)/shard_map/ppermute | solution.py:271
  111.6 10.9 %collective-permute-start.21 = (bf16[144,512]{1,0:T(8,128)(2,1)S(1)}, bf16[144,512]{1,0:T(8,128)(2,1)S(1)}, u32[]{:S(2)}, u32[]{:S(2)}) collective-permute-start(bf16[144,512]{1,0:T(8,128)(2,1)S(1)} %get-tuple-element.33.feats.refs_8_), channel_id=1, source_target_pairs={{0,32},{32,64},{64,96},{96,0},{1,33},{33,65},{65,97},{97,1},{2,34}... | collective-permute-start | bytes 442376 | tf_op jit(solution)/shard_map/ppermute | solution.py:271
  112.4 14.1 %collective-permute-start.22 = (bf16[144,512]{1,0:T(8,128)(2,1)S(1)}, bf16[144,512]{1,0:T(8,128)(2,1)S(1)}, u32[]{:S(2)}, u32[]{:S(2)}) collective-permute-start(bf16[144,512]{1,0:T(8,128)(2,1)S(1)} %get-tuple-element.33.feats.refs_8_), channel_id=1, source_target_pairs={{0,64},{32,96},{64,0},{96,32},{1,65},{33,97},{65,1},{97,33},{2,66}... | collective-permute-start | bytes 442376 | tf_op jit(solution)/shard_map/ppermute | solution.py:271
  114.6 17.5 %collective-permute-start.15 = (bf16[128,1024]{1,0:T(8,128)(2,1)S(1)}, bf16[128,1024]{1,0:T(8,128)(2,1)S(1)}, u32[]{:S(2)}, u32[]{:S(2)}) collective-permute-start(bf16[128,1024]{1,0:T(8,128)(2,1)S(1)} %get-tuple-element.43), channel_id=1, source_target_pairs={{0,64},{32,96},{64,0},{96,32},{1,65},{33,97},{65,1},{97,33},{2,66}... | collective-permute-start | bytes 786440 | tf_op jit(solution)/shard_map/ppermute | solution.py:271
  115.3 18.0 %collective-permute-start.16 = (bf16[128,1024]{1,0:T(8,128)(2,1)S(1)}, bf16[128,1024]{1,0:T(8,128)(2,1)S(1)}, u32[]{:S(2)}, u32[]{:S(2)}) collective-permute-start(bf16[128,1024]{1,0:T(8,128)(2,1)S(1)} %get-tuple-element.44), channel_id=1, source_target_pairs={{0,96},{32,0},{64,32},{96,64},{1,97},{33,1},{65,33},{97,65},{2,98}... | collective-permute-start | bytes 786440 | tf_op jit(solution)/shard_map/ppermute | solution.py:271
  122.5 13.3 %collective-permute-start.11 = (bf16[144,512]{1,0:T(8,128)(2,1)S(1)}, bf16[144,512]{1,0:T(8,128)(2,1)S(1)}, u32[]{:S(2)}, u32[]{:S(2)}) collective-permute-start(bf16[144,512]{1,0:T(8,128)(2,1)S(1)} %shard_map.102.refs_8_.refs_12_), channel_id=1, source_target_pairs={{0,32},{32,64},{64,96},{96,0},{1,33},{33,65},{65,97},{97,1},{2,34}... | collective-permute-start | bytes 442376 | tf_op jit(solution)/shard_map/ppermute | solution.py:271
  126.5 12.0 %collective-permute-start.12 = (bf16[144,512]{1,0:T(8,128)(2,1)S(1)}, bf16[144,512]{1,0:T(8,128)(2,1)S(1)}, u32[]{:S(2)}, u32[]{:S(2)}) collective-permute-start(bf16[144,512]{1,0:T(8,128)(2,1)S(1)} %shard_map.102.refs_8_.refs_12_), channel_id=1, source_target_pairs={{0,64},{32,96},{64,0},{96,32},{1,65},{33,97},{65,1},{97,33},{2,66}... | collective-permute-start | bytes 442376 | tf_op jit(solution)/shard_map/ppermute | solution.py:271
  127.3 11.9 %collective-permute-start.13 = (bf16[144,512]{1,0:T(8,128)(2,1)S(1)}, bf16[144,512]{1,0:T(8,128)(2,1)S(1)}, u32[]{:S(2)}, u32[]{:S(2)}) collective-permute-start(bf16[144,512]{1,0:T(8,128)(2,1)S(1)} %shard_map.102.refs_8_.refs_12_), channel_id=1, source_target_pairs={{0,96},{32,0},{64,32},{96,64},{1,97},{33,1},{65,33},{97,65},{2,98}... | collective-permute-start | bytes 442376 | tf_op jit(solution)/shard_map/ppermute | solution.py:271
  132.1 12.6 %collective-permute-start.17 = (bf16[128,1024]{1,0:T(8,128)(2,1)S(1)}, bf16[128,1024]{1,0:T(8,128)(2,1)S(1)}, u32[]{:S(2)}, u32[]{:S(2)}) collective-permute-start(bf16[128,1024]{1,0:T(8,128)(2,1)S(1)} %get-tuple-element.41.refs_0_), channel_id=1, source_target_pairs={{0,1},{1,0},{2,3},{3,2},{4,5},{5,4},{6,7},{7,6},{8,9},{9,8},{10,11... | collective-permute-start | bytes 786440 | tf_op jit(solution)/shard_map/ppermute | solution.py:267
  133.3 11.4 %collective-permute-start.18 = (bf16[128,1024]{1,0:T(8,128)(2,1)S(1)}, bf16[128,1024]{1,0:T(8,128)(2,1)S(1)}, u32[]{:S(2)}, u32[]{:S(2)}) collective-permute-start(bf16[128,1024]{1,0:T(8,128)(2,1)S(1)} %collective-permute-done.14.refs_1_), channel_id=1, source_target_pairs={{0,1},{1,0},{2,3},{3,2},{4,5},{5,4},{6,7},{7,6},{8,9},{9,8},{10,11... | collective-permute-start | bytes 786440 | tf_op jit(solution)/shard_map/ppermute | solution.py:267
  135.8 8.9 %collective-permute-start.19 = (bf16[128,1024]{1,0:T(8,128)(2,1)S(1)}, bf16[128,1024]{1,0:T(8,128)(2,1)S(1)}, u32[]{:S(2)}, u32[]{:S(2)}) collective-permute-start(bf16[128,1024]{1,0:T(8,128)(2,1)S(1)} %collective-permute-done.15.refs_2_), channel_id=1, source_target_pairs={{0,1},{1,0},{2,3},{3,2},{4,5},{5,4},{6,7},{7,6},{8,9},{9,8},{10,11... | collective-permute-start | bytes 786440 | tf_op jit(solution)/shard_map/ppermute | solution.py:267
  138.4 6.3 %collective-permute-start.20 = (bf16[128,1024]{1,0:T(8,128)(2,1)S(1)}, bf16[128,1024]{1,0:T(8,128)(2,1)S(1)}, u32[]{:S(2)}, u32[]{:S(2)}) collective-permute-start(bf16[128,1024]{1,0:T(8,128)(2,1)S(1)} %collective-permute-done.16.refs_3_), channel_id=1, source_target_pairs={{0,1},{1,0},{2,3},{3,2},{4,5},{5,4},{6,7},{7,6},{8,9},{9,8},{10,11... | collective-permute-start | bytes 786440 | tf_op jit(solution)/shard_map/ppermute | solution.py:267
  139.3 5.5 %collective-permute-start.23 = (bf16[144,512]{1,0:T(8,128)(2,1)S(1)}, bf16[144,512]{1,0:T(8,128)(2,1)S(1)}, u32[]{:S(2)}, u32[]{:S(2)}) collective-permute-start(bf16[144,512]{1,0:T(8,128)(2,1)S(1)} %get-tuple-element.33.feats.refs_8_), channel_id=1, source_target_pairs={{0,96},{32,0},{64,32},{96,64},{1,97},{33,1},{65,33},{97,65},{2,98}... | collective-permute-start | bytes 442376 | tf_op jit(solution)/shard_map/ppermute | solution.py:271
  (6 other events, 33.2 us)

commit v2 on v1

v2 whole, which is shorter than its diff:
```python
import jax
import jax.numpy as jnp
from jax import lax
from jax.experimental import pallas as pl
from jax.experimental.pallas import tpu as pltpu
from jax.sharding import Mesh
from jax.sharding import PartitionSpec as P

sparsity_weight = 1.0
loss_scale = 8.0
norm_eps = 1e-06

ALL = ("z", "x", "y", "c")
NZ = 4
CHIPS = 16
WIDTH = 8192
HALF = 4096
SUB = 1024
LOCAL = 512
ROWS = 128
PAD = 128
MIB = 1 << 20
f32 = jnp.float32
bf16 = jnp.bfloat16

VM = pl.BlockSpec(memory_space=pltpu.VMEM)


def at_hbm(v):
    return pltpu.with_memory_space_constraint(v, pltpu.HBM)


def call(body, outs, args, specs=None, scratch=(), vmem=None, flops=0, nbytes=0, out_specs=None):
    return pl.pallas_call(
        body,
        out_shape=[pltpu.VMEM(o[0], o[1]) if len(o) == 3 else jax.ShapeDtypeStruct(*o) for o in outs],
        in_specs=specs or [VM] * len(args),
        out_specs=out_specs or [VM] * len(outs),
        scratch_shapes=list(scratch),
        compiler_params=pltpu.CompilerParams(vmem_limit_bytes=vmem or 16 * MIB),
        cost_estimate=pl.CostEstimate(flops=flops, bytes_accessed=nbytes, transcendentals=0),
    )(*args)


def lanes(start, size):
    return pl.ds(pl.multiple_of(start, 128), size)


def split3(v):
    hi = v.astype(bf16)
    rest = v - hi.astype(f32)
    mid = rest.astype(bf16)
    low = (rest - mid.astype(f32)).astype(bf16)
    return hi, mid, low


def prep_kernel(length, acts_hbm, group_hbm, keep, send, acts, group, sems):
    copies = [
        pltpu.make_async_copy(src, dst, sems.at[i])
        for i, (src, dst) in enumerate(((acts_hbm, acts), (group_hbm, group)))
    ]
    for copy in copies:
        copy.start()
    for copy in copies:
        copy.wait()
    c = lax.axis_index("c")
    slot = lax.broadcasted_iota(jnp.int32, (1, 5), 1)
    held = jnp.sum(jnp.where(group[...] == NZ, slot, 0), axis=1, keepdims=True)
    k = lax.broadcasted_iota(jnp.int32, (4, 1), 0)
    later = k >= held
    src = k + later.astype(jnp.int32)
    live = (src < length[0]).astype(f32)
    live = jnp.broadcast_to(live, (4, PAD)).astype(bf16)

    def pick(cols):
        rows = acts[:, cols].astype(f32)
        return jnp.where(later, rows[1:5], rows[0:4]).astype(bf16)

    for out, core in ((keep, c), (send, 1 - c)):
        out[:, :HALF] = pick(lanes(core * HALF, HALF))
        for q in range(NZ):
            out[:, HALF + q * SUB : HALF + (q + 1) * SUB] = pick(lanes(q * 2 * SUB + core * SUB, SUB))
        out[:, 2 * HALF :] = live


def join_kernel(own, other, out, mine):
    first = lax.axis_index("c") == 0
    a, b = own[...].astype(f32), other[...].astype(f32)
    rows = jnp.concatenate([jnp.where(first, a, b), jnp.where(first, b, a)], axis=0)
    mine[...] = rows[:, HALF:].astype(bf16)
    for i in range(CHIPS):
        out[i, :, :HALF] = rows[:, :HALF].astype(bf16)
        out[i, :, HALF:] = rows[:, 2 * HALF :].astype(bf16)


def norm_kernel(w_dec_hbm, norm_row, norm_col, w_dec, sems):
    rows = LOCAL // 4
    copies = [
        pltpu.make_async_copy(w_dec_hbm.at[pl.ds(i * rows, rows)], w_dec.at[pl.ds(i * rows, rows)], sems.at[i])
        for i in range(4)
    ]
    for copy in copies:
        copy.start()
    for i in range(4):
        copies[i].wait()
        n = i * rows
        for s in range(2):

            def add(j, total):
                for m in range(4):
                    v = w_dec[n : n + rows, lanes(s * HALF + j * 512 + m * 128, 128)].astype(f32)
                    total = total + v * v
                return total

            total = lax.fori_loop(0, HALF // 512, add, jnp.zeros((rows, 128), f32))
            norm_row[s : s + 1, n : n + rows] = jnp.sqrt(jnp.sum(total.T, axis=0, keepdims=True) + norm_eps)
            norm_col[n : n + rows, s : s + 1] = jnp.sqrt(jnp.sum(total, axis=1, keepdims=True) + norm_eps)


def fetch_enc(w_hbm, core, buf, sems, at=0):
    copies = [
        pltpu.make_async_copy(w_hbm.at[core, pl.ds(i * SUB, SUB)], buf.at[i], sems.at[at + i]) for i in range(4)
    ]
    for copy in copies:
        copy.start()
    return copies


def fetch_dec(w_hbm, core, buf, sems, at=0):
    copies = [
        pltpu.make_async_copy(w_hbm.at[:, lanes(q * 2 * SUB + core * SUB, SUB)], buf.at[q], sems.at[at + q])
        for q in range(NZ)
    ]
    for copy in copies:
        copy.start()
    return copies


def project(x, copies, buf, acc):
    for i in range(4):
        if copies:
            copies[i].wait()
        for n in range(0, LOCAL, 256):
            acc[:, n : n + 256] += jnp.dot(
                x[:, i * SUB : (i + 1) * SUB], buf[i, :, n : n + 256], preferred_element_type=f32
            )


def encode_own_kernel(x, w_enc, acc, rest, mask, buf, sems):
    c = lax.axis_index("c")
    copies = fetch_enc(w_enc, c, buf, sems)
    later = fetch_enc(w_enc, 1 - c, rest, sems, 4)
    acc[...] = jnp.zeros_like(acc)
    mask[...] = x[:, HALF:]
    project(x, copies, buf, acc)
    for copy in later:
        copy.wait()


def encode_kernel(x, mask, part, bias, w_enc, w_dec, act_out, feats_out, send, acc, dec, dec_sems):
    c = lax.axis_index("c")
    dec_copies = fetch_dec(w_dec, 1 - c, dec, dec_sems)
    live = mask[:, 0:1].astype(f32)
    count = jnp.sum(live, axis=0, keepdims=True)
    acc[...] = part[...]
    project(x, None, w_enc, acc)
    for n in range(0, LOCAL, 256):
        act = jnp.maximum(acc[:, n : n + 256] + bias[:, n : n + 256], 0.0)
        feats = act * act
        act_out[:, n : n + 256] = act
        feats_out[:ROWS, n : n + 256] = feats.astype(bf16)
        fsum = jnp.sum(feats * live, axis=0, keepdims=True)
        tail = jnp.zeros((16, 256), f32)
        row = lax.broadcasted_iota(jnp.int32, (16, 256), 0)
        for i, piece in enumerate((*split3(fsum), jnp.broadcast_to(count, (1, 256)))):
            tail = jnp.where(row == i, piece.astype(f32), tail)
        feats_out[ROWS:, n : n + 256] = tail.astype(bf16)
    feats16 = feats_out[:ROWS, :]
    for q in range(NZ):
        dec_copies[q].wait()
        send[:, q * SUB : (q + 1) * SUB] = jnp.dot(feats16, dec[q], preferred_element_type=f32).astype(bf16)


def decode_own_kernel(feats, w_dec, part, buf, sems):
    copies = fetch_dec(w_dec, lax.axis_index("c"), buf, sems)
    feats16 = feats[:ROWS, :]
    for q in range(NZ):
        copies[q].wait()
        part[:, q * SUB : (q + 1) * SUB] = jnp.dot(feats16, buf[q], preferred_element_type=f32)


def pack_kernel(x, *pieces):
    z = lax.axis_index("z")
    for k in range(1, NZ):
        pieces[k - 1][...] = x[:, lanes(lax.rem(z + k, NZ) * SUB, SUB)]


def add_kernel(own, other, out):
    for n in range(0, HALF, SUB):
        out[:, n : n + SUB] = (own[:, n : n + SUB] + other[:, n : n + SUB].astype(f32)).astype(bf16)


def err_kernel(parts, mine, bias, feats, norm_row, out):
    c = lax.axis_index("c")
    live = mine[:, HALF : HALF + 1].astype(f32)
    square = jnp.zeros((8, SUB), f32)
    for q in range(NZ):
        cols = slice(q * SUB, (q + 1) * SUB)
        total = parts[0, :, cols].astype(f32)
        for i in range(1, CHIPS):
            total = total + parts[i, :, cols].astype(f32)
        add = bias[q // 2 : q // 2 + 1, lanes((q % 2) * 2 * SUB + c * SUB, SUB)]
        err = (total + add - mine[:, cols].astype(f32)) * live
        square = square + err * err
        err16 = err.astype(bf16)
        for i in range(CHIPS):
            out[i, :, cols] = err16
    squares = jnp.sum(jnp.sum(square, axis=0, keepdims=True), axis=1, keepdims=True)
    fsum = jnp.sum(feats[ROWS : ROWS + 3, :].astype(f32), axis=0, keepdims=True)
    nsum = norm_row[0:1, :] + norm_row[1:2, :]
    sparse = sparsity_weight * jnp.sum(fsum * nsum, axis=1, keepdims=True)
    lane = lax.broadcasted_iota(jnp.int32, (8, PAD), 1)
    row = lax.broadcasted_iota(jnp.int32, (8, PAD), 0)
    tail = jnp.zeros((8, PAD), f32)
    for i, piece in enumerate(split3(squares + sparse)):
        tail = jnp.where((lane == i) & (row == 0), piece.astype(f32), tail)
    for i in range(CHIPS):
        out[i, :, HALF:] = tail.astype(bf16)


def dfeat(e, copies, buf, acc):
    for q in range(NZ):
        if copies:
            copies[q].wait()
        for n in range(0, LOCAL, 256):
            acc[:, n : n + 256] += lax.dot_general(
                e[:, q * SUB : (q + 1) * SUB],
                buf[q, n : n + 256, :],
                (((1,), (1,)), ((), ())),
                preferred_element_type=f32,
            )


def dfeat_own_kernel(e, w_dec, acc, rest, s1, s2, s3, buf, sems):
    z, c = lax.axis_index("z"), lax.axis_index("c")
    copies = fetch_dec(w_dec, c, buf, sems)
    later = fetch_dec(w_dec, 1 - c, rest, sems, 4)
    for k, out in enumerate((s1, s2, s3)):
        out[...] = e[:, lanes(lax.rem(z + k + 1, NZ) * SUB, SUB)]
    acc[...] = jnp.zeros_like(acc)
    dfeat(e, copies, buf, acc)
    for copy in later:
        copy.wait()


def dpre_kernel(e, own, part, act, mask, norm_row, w_dec, out, acc):
    acc[...] = part[...]
    both = e[:, HALF:].astype(f32) + own[:, HALF:].astype(f32)
    both = jnp.sum(jnp.sum(both, axis=0, keepdims=True), axis=1, keepdims=True)
    lane = lax.broadcasted_iota(jnp.int32, (16, LOCAL), 1)
    tail = jnp.zeros((16, LOCAL), f32)
    for i, piece in enumerate(split3(both)):
        tail = jnp.where(lane == i, piece.astype(f32), tail)
    out[ROWS:, :] = tail.astype(bf16)
    live = mask[:, 0:1].astype(f32)
    dfeat(e, None, w_dec, acc)
    for n in range(0, LOCAL, 256):
        nsum = norm_row[0:1, n : n + 256] + norm_row[1:2, n : n + 256]
        grad = 2.0 * acc[:, n : n + 256] + sparsity_weight * live * nsum
        out[:ROWS, n : n + 256] = (grad * 2.0 * act[:, n : n + 256]).astype(bf16)


def merge_kernel(a, b, d, *refs):
    out = refs[-1]
    for k, v in enumerate((a, b, d)):
        out[k * ROWS : (k + 1) * ROWS, :] = v[...]


def count_of(feats):
    count = jnp.zeros((1, 1), f32)
    for p in feats:
        count = count + p[ROWS + 3 : ROWS + 4, 0:1].astype(f32)
    return count


def grad_enc_kernel(*refs):
    z, c = lax.axis_index("z"), lax.axis_index("c")
    x_own, x_other, own, other, feats, pres = *refs[0:4], refs[4:8], refs[8:12]
    out, loss, xs, ds, done, sems = refs[12:]
    count = count_of(feats)
    total = jnp.zeros((1, 1), f32)
    for k in range(NZ):
        total = total + jnp.sum(pres[k][ROWS : ROWS + 1, 0:3].astype(f32), axis=1, keepdims=True)
        ds[k * ROWS : (k + 1) * ROWS, :] = pres[k][:ROWS, :]
    loss[...] = total / (count * WIDTH)
    factor = loss_scale / count
    copies = []
    for side, plane, rest in ((c, x_own, own), (1 - c, x_other, other)):
        xs[:ROWS, :] = plane[:, lanes(z * SUB, SUB)]
        xs[ROWS:, :] = rest[...]
        for n in range(0, SUB, 256):
            part = lax.dot_general(
                xs[:, n : n + 256], ds[...], (((0,), (0,)), ((), ())), preferred_element_type=f32
            )
            done[side, n : n + 256, :] = (part * factor).astype(bf16)
            piece = pl.ds(n, 256)
            copies.append(pltpu.make_async_copy(done.at[side, piece], out.at[side, piece], sems.at[len(copies)]))
            copies[-1].start()
    for copy in copies:
        copy.wait()


def grad_dec_kernel(*refs):
    z, c = lax.axis_index("z"), lax.axis_index("c")
    e_own, e_other, own, other, feats, norm_col, w_dec = *refs[0:4], refs[4:8], refs[8], refs[9]
    out, es, fs, done, w, w_sem, sems = refs[10:]
    fetch = pltpu.make_async_copy(w_dec.at[:, lanes(z * 2 * SUB, 2 * SUB)], w, w_sem)
    fetch.start()
    factor = loss_scale / count_of(feats)
    fsum = jnp.zeros((1, LOCAL), f32)
    for k in range(NZ):
        fs[k * ROWS : (k + 1) * ROWS, :] = feats[k][:ROWS, :]
        fsum = fsum + jnp.sum(feats[k][ROWS : ROWS + 3, :].astype(f32), axis=0, keepdims=True)
    fsum = jnp.broadcast_to(fsum, (128, LOCAL)).T[:, 0:1]
    norm = jnp.where(z < 2, norm_col[:, 0:1], norm_col[:, 1:2])
    scale = sparsity_weight * fsum / norm
    for side, plane, rest in ((c, e_own, own), (1 - c, e_other, other)):
        es[:ROWS, lanes(side * SUB, SUB)] = plane[:, lanes(z * SUB, SUB)]
        es[ROWS:, lanes(side * SUB, SUB)] = rest[...]
    copies = []
    for n in range(0, LOCAL, 256):
        piece = pl.ds(n, 256)
        for m in range(0, 2 * SUB, 512):
            part = 2.0 * lax.dot_general(
                fs[:, n : n + 256], es[:, m : m + 512], (((0,), (0,)), ((), ())), preferred_element_type=f32
            )
            if n == m == 0:
                fetch.wait()
            part = part + scale[n : n + 256, :] * w[n : n + 256, m : m + 512].astype(f32)
            done[n : n + 256, m : m + 512] = (part * factor).astype(bf16)
        copies.append(pltpu.make_async_copy(done.at[piece], out.at[piece], sems.at[len(copies)]))
        copies[-1].start()
    for copy in copies:
        copy.wait()


def swap(v):
    return lax.ppermute(v, "c", [(0, 1), (1, 0)])


def chips(v):
    return lax.all_to_all(v, ("x", "y"), split_axis=0, concat_axis=0, tiled=True)


def planes(v):
    return lax.all_to_all(v, "z", split_axis=0, concat_axis=0, tiled=True)


def shift(v, k):
    return lax.ppermute(v, "z", [(i, (i + k) % NZ) for i in range(NZ)])


def shards(acts, chat_len, group_of, w_enc, b_enc, w_dec, b_dec):
    half_flops = 2 * ROWS * HALF * LOCAL
    w_enc, w_dec = at_hbm(w_enc), at_hbm(w_dec)
    hbm = pl.BlockSpec(memory_space=pltpu.HBM)
    enc_scratch = [pltpu.VMEM((4, SUB, LOCAL), bf16), pltpu.SemaphoreType.DMA((4,))]
    dec_scratch = [pltpu.VMEM((4, LOCAL, SUB), bf16), pltpu.SemaphoreType.DMA((4,))]
    acc_scratch = pltpu.VMEM((ROWS, LOCAL), f32)
    keep, send = call(
        prep_kernel,
        [((4, 2 * HALF + PAD), bf16)] * 2,
        (chat_len, at_hbm(acts), at_hbm(group_of.reshape(1, 5))),
        [pl.BlockSpec(memory_space=pltpu.SMEM), hbm, hbm],
        [
            pltpu.VMEM((5, WIDTH), bf16),
            pltpu.VMEM((1, 5), jnp.int32),
            pltpu.SemaphoreType.DMA((2,)),
        ],
    )
    block, mine = call(
        join_kernel,
        [((CHIPS, 8, HALF + PAD), bf16), ((8, HALF + PAD), bf16)],
        (keep, swap(send)),
    )
    norm_row, norm_col = call(
        norm_kernel,
        [((2, LOCAL), f32), ((LOCAL, 2), f32)],
        (w_dec,),
        [hbm],
        [pltpu.VMEM((LOCAL, WIDTH), bf16), pltpu.SemaphoreType.DMA((4,))],
        flops=4 * LOCAL * WIDTH,
        nbytes=8 * MIB,
    )
    x_own, norm_row, norm_col = lax.optimization_barrier((chips(block), norm_row, norm_col))
    x_own = x_own.reshape(ROWS, HALF + PAD)
    x_other = swap(x_own)
    acc, w_rest, mask = call(
        encode_own_kernel,
        [((ROWS, LOCAL), f32), ((4, SUB, LOCAL), bf16, 1), ((ROWS, PAD), bf16)],
        (x_own, w_enc),
        [VM, hbm],
        [enc_scratch[0], pltpu.SemaphoreType.DMA((8,))],
        flops=half_flops,
        nbytes=10 * MIB,
    )
    act, feats, part_send = call(
        encode_kernel,
        [((ROWS, LOCAL), f32), ((ROWS + 16, LOCAL), bf16), ((ROWS, HALF), bf16)],
        (x_other, mask, acc, b_enc.reshape(1, LOCAL), w_rest, w_dec),
        [VM] * 5 + [hbm],
        [acc_scratch, *dec_scratch],
        flops=2 * half_flops,
        nbytes=8 * MIB,
    )
    part_recv = swap(part_send)
    (part_own,) = call(
        decode_own_kernel,
        [((ROWS, HALF), f32)],
        (feats, w_dec),
        [VM, hbm],
        dec_scratch,
        flops=half_flops,
        nbytes=6 * MIB,
    )
    (part,) = call(add_kernel, [((ROWS, HALF), bf16)], (part_own, part_recv))
    parts = chips(part.reshape(CHIPS, 8, HALF))
    xs = call(pack_kernel, [((ROWS, SUB), bf16)] * 3, (x_own,), nbytes=2 * MIB)
    xs = [shift(xs[k - 1], k) for k in range(1, NZ)]
    parts, *xs = lax.optimization_barrier((parts, *xs))
    (block,) = call(
        err_kernel,
        [((CHIPS, 8, HALF + PAD), bf16)],
        (parts, mine, b_dec, feats, norm_row),
    )
    fs = [feats] + [shift(feats, k) for k in range(1, NZ)]
    e_own, *fs = lax.optimization_barrier((chips(block), *fs))
    e_own = e_own.reshape(ROWS, HALF + PAD)
    e_other = swap(e_own)
    acc, w_rest, *slices = call(
        dfeat_own_kernel,
        [((ROWS, LOCAL), f32), ((4, LOCAL, SUB), bf16, 1)] + [((ROWS, SUB), bf16)] * 3,
        (e_own, w_dec),
        [VM, hbm],
        [dec_scratch[0], pltpu.SemaphoreType.DMA((8,))],
        flops=half_flops,
        nbytes=10 * MIB,
    )
    es = [shift(slices[k - 1], k) for k in range(1, NZ)]
    (dpre,) = call(
        dpre_kernel,
        [((ROWS + 16, LOCAL), bf16)],
        (e_other, e_own, acc, act, mask, norm_row, w_rest),
        scratch=[acc_scratch],
        flops=half_flops,
        nbytes=2 * MIB,
    )
    ds = [dpre] + [shift(dpre, k) for k in range(1, NZ)]
    anywhere = pl.BlockSpec(memory_space=pl.ANY)
    (xs,) = call(merge_kernel, [((3 * ROWS, SUB), bf16)], (*xs, dpre), [VM] * 3 + [anywhere], nbytes=2 * MIB)
    (es,) = call(merge_kernel, [((3 * ROWS, SUB), bf16)], (*es, *ds[1:]), [VM] * 3 + [anywhere] * 3, nbytes=2 * MIB)
    grad_enc, loss = call(
        grad_enc_kernel,
        [((2, SUB, LOCAL), bf16), ((1, 1), f32)],
        (x_own, x_other, xs, swap(xs), *fs, *ds),
        scratch=[
            pltpu.VMEM((NZ * ROWS, SUB), bf16),
            pltpu.VMEM((NZ * ROWS, LOCAL), bf16),
            pltpu.VMEM((2, SUB, LOCAL), bf16),
            pltpu.SemaphoreType.DMA((8,)),
        ],
        out_specs=[hbm, VM],
        flops=4 * half_flops,
        nbytes=5 * MIB,
    )
    (grad_dec,) = call(
        grad_dec_kernel,
        [((LOCAL, 2 * SUB), bf16)],
        (e_own, e_other, es, swap(es), *fs, norm_col, w_dec),
        [VM] * 9 + [hbm],
        [
            pltpu.VMEM((NZ * ROWS, 2 * SUB), bf16),
            pltpu.VMEM((NZ * ROWS, LOCAL), bf16),
            pltpu.VMEM((LOCAL, 2 * SUB), bf16),
            pltpu.VMEM((LOCAL, 2 * SUB), bf16),
            pltpu.SemaphoreType.DMA,
            pltpu.SemaphoreType.DMA((2,)),
        ],
        out_specs=[hbm],
        flops=4 * half_flops,
        nbytes=7 * MIB,
    )
    return grad_enc, grad_dec, loss.reshape(())


def solution(mesh):
    fine = Mesh(mesh.devices.reshape(4, 4, 4, 2), ALL)
    lat = ("x", "y", "c")
    return jax.shard_map(
        shards,
        mesh=fine,
        in_specs=(P(ALL, None), P(ALL), P(ALL, None), P(None, None, lat), P(lat), P(lat, None), P()),
        out_specs=(P(None, "z", lat), P(lat, "z"), P()),
        check_vma=False,
    )
```

time: 149 us -> 126 us (0.85)
  blocking collectives: 61.6 us -> 0 us
  starting transfers between devices: 24.2 us -> 41.9 us
  waiting for transfers between devices: 29.2 us -> 46.2 us
  Pallas kernels: 21.3 us -> 31.2 us
  local copies, waits for them, and re-layouts: 10.5 us -> 4.89 us
    all_to_all x3 -> x0, blocking collectives: 61.6 us -> none  [the longest x2 42.9 us: shards(): lax.all_to_all(block, ('x', 'y'), split_axis=0, concat_axis=0, tiled=True)]
    all_to_all x0 -> x3, starting transfers between devices: none -> 16.9 us  [chips(): lax.all_to_all(v, ('x', 'y'), split_axis=0, concat_axis=0, tiled=True)]
    all_to_all x0 -> x3, waiting for transfers between devices: none -> 12.6 us  [chips(): lax.all_to_all(v, ('x', 'y'), split_axis=0, concat_axis=0, tiled=True)]
    pallas_call x11 -> x15, Pallas kernels: 21.3 us -> 31.2 us  [call(): pl.pallas_call(body, out_shape=[pltpu.VMEM(o[0], o[1]) if len(o) == 3 els...]
    unnamed x13 -> x36, local copies, waits for them, and re-layouts: 10.5 us -> 4.89 us
    ppermute x12, waiting for transfers between devices: 28.3 us -> 32.6 us  [shift(): return lax.ppermute(v, 'z', [(i, (i + k) % NZ) for i in range(NZ)])]
    ppermute x12 -> x6, starting transfers between devices: 10.9 us -> 10.9 us  [swap(): return lax.ppermute(v, 'c', [(0, 1), (1, 0)])]
  transfers between devices with their start and end apart: 24 -> 21, of which waited for: 9 -> 14; matrix products, arithmetic and copies ran while one was open for 0% -> 0% of each run, Pallas kernels for 9% -> 15%
where the time goes in v2:
time: 126 us
  waiting for transfers between devices  46.2 us (37%)
  starting transfers between devices  41.9 us (33%)
  Pallas kernels  31.2 us (25%)
  local copies, waits for them, and re-layouts  4.89 us (4%)
  between operations  1.72 us (1%)
    ppermute x12, waiting for transfers between devices, shift(): return lax.ppermute(v, 'z', [(i, (i + k) % NZ) for i in range(NZ)])  32.6 us
    pallas_call x15, Pallas kernels, call(): pl.pallas_call(body, out_shape=[pltpu.VMEM(o[0], o[1]) if len(o) == 3 els...  31.2 us
    all_to_all x3, starting transfers between devices, chips(): lax.all_to_all(v, ('x', 'y'), split_axis=0, concat_axis=0, tiled=True)  16.9 us
    ppermute x12, starting transfers between devices, shift(): return lax.ppermute(v, 'z', [(i, (i + k) % NZ) for i in range(NZ)])  14.1 us
    all_to_all x3, waiting for transfers between devices, chips(): lax.all_to_all(v, ('x', 'y'), split_axis=0, concat_axis=0, tiled=True)  12.6 us
    ppermute x6, starting transfers between devices, swap(): return lax.ppermute(v, 'c', [(0, 1), (1, 0)])  10.9 us
    unnamed x36, local copies, waits for them, and re-layouts  4.89 us
  transfers between devices with their start and end apart: 21, of which 14 were waited for; matrix products, arithmetic and copies ran while one was open for 0% of the time, Pallas kernels for 15%

profile of v2, /device:TPU:1, one launch (start us, length us, event | category | flops | bytes accessed | tf_op | source)
XLA Modules:
  0.0 125.9 jit_solution(3929614521642075978)
XLA Ops:
  5.8 6.8 %all-to-all-start = ((bf16[16,8,4224]{2,1,0:T(8,128)(2,1)}), bf16[16,8,4224]{2,1,0:T(8,128)(2,1)S(1)}, u32[]{:S(2)}, u32[]{:S(2)}) async-start(bf16[16,8,4224]{2,1,0:T(8,128)(2,1)} %get-tuple-element.39), calls=%async_computation | async-start | bytes 2162688 | tf_op jit(solution)/shard_map/all_to_all | solution.py:352
  12.7 5.0 %shard_map.96 = (f32[2,512]{1,0:T(2,128)S(1)}, f32[512,2]{1,0:T(8,128)S(1)}) custom-call(bf16[512,8192]{1,0:T(8,128)(2,1)} %refs_9_.1), custom_call_target="tpu_custom_call" | custom-call | flops 16777216 | bytes 8388608 | tf_op jit(solution)/shard_map/pallas_call | solution.py:34
  18.4 10.3 %all-to-all-done = bf16[16,8,4224]{2,1,0:T(8,128)(2,1)S(1)} async-done(((bf16[16,8,4224]{2,1,0:T(8,128)(2,1)}), bf16[16,8,4224]{2,1,0:T(8,128)(2,1)S(1)}, u32[]{:S(2)}, u32[]{:S(2)}) %all-to-all-start) | async-done | bytes 1081376 | tf_op jit(solution)/shard_map/all_to_all | solution.py:352
  28.7 3.1 %collective-permute-start.1 = (bf16[128,4224]{1,0:T(8,128)(2,1)S(1)}, bf16[128,4224]{1,0:T(8,128)(2,1)S(1)}, u32[]{:S(2)}, u32[]{:S(2)}) collective-permute-start(bf16[128,4224]{1,0:T(8,128)(2,1)S(1)} %bitcast.10), channel_id=1, source_target_pairs={{0,1},{1,0},{2,3},{3,2},{4,5},{5,4},{6,7},{7,6},{8,9},{9,8},{10,11... | collective-permute-start | bytes 3244040 | tf_op jit(solution)/shard_map/ppermute | solution.py:348
  31.8 3.5 %shard_map.97 = (f32[128,512]{1,0:T(8,128)S(1)}, bf16[4,1024,512]{2,1,0:T(8,128)(2,1)S(1)}, bf16[128,128]{1,0:T(8,128)(2,1)S(1)}) custom-call(bf16[128,4224]{1,0:T(8,128)(2,1)S(1)} %bitcast.11, bf16[2,4096,512]{2,1,0:T(8,128)(2,1)} %w_enc.1), custom_call_target="tpu_custom_call" | custom-call | flops 536870912 | bytes 10485760 | tf_op jit(solution)/shard_map/pallas_call | solution.py:34
  35.3 3.1 %shard_map.98 = (f32[128,512]{1,0:T(8,128)S(1)}, bf16[144,512]{1,0:T(8,128)(2,1)S(1)}, bf16[128,4096]{1,0:T(8,128)(2,1)S(1)}) custom-call(bf16[128,4224]{1,0:T(8,128)(2,1)S(1)} %collective-permute-done.1.x.refs_1_, bf16[128,128]{1,0:T(8,128)(2,1)S(1)} %get-tuple-element.43.mask, f32[128,512]{1,0:T(8,128)S(1)} %get-tuple-element.44.part, ...), custom_call_target="tpu_custom_call" | custom-call | flops 1073741824 | bytes 8388608 | tf_op jit(solution)/shard_map/pallas_call | solution.py:34
  39.1 2.5 %shard_map.99.own = f32[128,4096]{1,0:T(8,128)S(1)} custom-call(bf16[144,512]{1,0:T(8,128)(2,1)S(1)} %get-tuple-element.61.feats.refs_4_, bf16[512,8192]{1,0:T(8,128)(2,1)} %refs_9_.1), custom_call_target="tpu_custom_call" | custom-call | flops 536870912 | bytes 6291456 | tf_op jit(solution)/shard_map/pallas_call | solution.py:34
  42.9 3.8 %all-to-all-start.1 = ((bf16[16,8,4096]{2,1,0:T(8,128)(2,1)}), bf16[16,8,4096]{2,1,0:T(8,128)(2,1)S(1)}, u32[]{:S(2)}, u32[]{:S(2)}) async-start(bf16[16,8,4096]{2,1,0:T(8,128)(2,1)} %bitcast.3), calls=%async_computation.1 | async-start | bytes 2097152 | tf_op jit(solution)/shard_map/all_to_all | solution.py:352
  48.5 3.3 %collective-permute-start.4 = (bf16[128,1024]{1,0:T(8,128)(2,1)S(1)}, bf16[128,1024]{1,0:T(8,128)(2,1)S(1)}, u32[]{:S(2)}, u32[]{:S(2)}) collective-permute-start(bf16[128,1024]{1,0:T(8,128)(2,1)S(1)} %get-tuple-element.49), channel_id=1, source_target_pairs={{0,64},{32,96},{64,0},{96,32},{1,65},{33,97},{65,1},{97,33},{2,66}... | collective-permute-start | bytes 786440 | tf_op jit(solution)/shard_map/ppermute | solution.py:360
  52.6 4.4 %collective-permute-done.3.a = bf16[128,1024]{1,0:T(8,128)(2,1)S(1)} collective-permute-done((bf16[128,1024]{1,0:T(8,128)(2,1)S(1)}, bf16[128,1024]{1,0:T(8,128)(2,1)S(1)}, u32[]{:S(2)}, u32[]{:S(2)}) %collective-permute-start.3) | collective-permute-done | bytes 262176 | tf_op jit(solution)/shard_map/ppermute | solution.py:360
  57.7 5.8 %collective-permute-done.4.b = bf16[128,1024]{1,0:T(8,128)(2,1)S(1)} collective-permute-done((bf16[128,1024]{1,0:T(8,128)(2,1)S(1)}, bf16[128,1024]{1,0:T(8,128)(2,1)S(1)}, u32[]{:S(2)}, u32[]{:S(2)}) %collective-permute-start.4) | collective-permute-done | bytes 262176 | tf_op jit(solution)/shard_map/ppermute | solution.py:360
  66.2 6.3 %all-to-all-start.2 = ((bf16[16,8,4224]{2,1,0:T(8,128)(2,1)}), bf16[16,8,4224]{2,1,0:T(8,128)(2,1)S(1)}, u32[]{:S(2)}, u32[]{:S(2)}) async-start(bf16[16,8,4224]{2,1,0:T(8,128)(2,1)} %shard_map.102), calls=%async_computation.2 | async-start | bytes 2162688 | tf_op jit(solution)/shard_map/all_to_all | solution.py:352
  72.4 2.3 %collective-permute-start.8 = (bf16[144,512]{1,0:T(8,128)(2,1)S(1)}, bf16[144,512]{1,0:T(8,128)(2,1)S(1)}, u32[]{:S(2)}, u32[]{:S(2)}) collective-permute-start(bf16[144,512]{1,0:T(8,128)(2,1)S(1)} %get-tuple-element.61.feats.refs_4_), channel_id=1, source_target_pairs={{0,96},{32,0},{64,32},{96,64},{1,97},{33,1},{65,33},{97,65},{2,98}... | collective-permute-start | bytes 442376 | tf_op jit(solution)/shard_map/ppermute | solution.py:360
  75.4 3.8 %collective-permute-done.8.refs_7_ = bf16[144,512]{1,0:T(8,128)(2,1)S(1)} collective-permute-done((bf16[144,512]{1,0:T(8,128)(2,1)S(1)}, bf16[144,512]{1,0:T(8,128)(2,1)S(1)}, u32[]{:S(2)}, u32[]{:S(2)}) %collective-permute-start.8) | collective-permute-done | bytes 147488 | tf_op jit(solution)/shard_map/ppermute | solution.py:360
  81.2 3.6 %collective-permute-done.6.refs_5_ = bf16[144,512]{1,0:T(8,128)(2,1)S(1)} collective-permute-done((bf16[144,512]{1,0:T(8,128)(2,1)S(1)}, bf16[144,512]{1,0:T(8,128)(2,1)S(1)}, u32[]{:S(2)}, u32[]{:S(2)}) %collective-permute-start.6) | collective-permute-done | bytes 147488 | tf_op jit(solution)/shard_map/ppermute | solution.py:360
  85.5 2.3 %all-to-all-done.2 = bf16[16,8,4224]{2,1,0:T(8,128)(2,1)S(1)} async-done(((bf16[16,8,4224]{2,1,0:T(8,128)(2,1)}), bf16[16,8,4224]{2,1,0:T(8,128)(2,1)S(1)}, u32[]{:S(2)}, u32[]{:S(2)}) %all-to-all-start.2) | async-done | bytes 1081376 | tf_op jit(solution)/shard_map/all_to_all | solution.py:352
  87.8 3.2 %collective-permute-start.9 = (bf16[128,4224]{1,0:T(8,128)(2,1)S(1)}, bf16[128,4224]{1,0:T(8,128)(2,1)S(1)}, u32[]{:S(2)}, u32[]{:S(2)}) collective-permute-start(bf16[128,4224]{1,0:T(8,128)(2,1)S(1)} %bitcast.6), channel_id=1, source_target_pairs={{0,1},{1,0},{2,3},{3,2},{4,5},{5,4},{6,7},{7,6},{8,9},{9,8},{10,11... | collective-permute-start | bytes 3244040 | tf_op jit(solution)/shard_map/ppermute | solution.py:348
  91.0 3.5 %shard_map.103 = (f32[128,512]{1,0:T(8,128)S(1)}, bf16[4,512,1024]{2,1,0:T(8,128)(2,1)S(1)}, bf16[128,1024]{1,0:T(8,128)(2,1)S(1)}, bf16[128,1024]{1,0:T(8,128)(2,1)S(1)}, bf16[128,1024]{1,0:T(8,128)(2,1)S(1)}) custom-call(bf16[128,4224]{1,0:T(8,128)(2,1)S(1)} %bitcast.7, bf16[512,8192]{1,0:T(8,128)(2,1)} %refs_9_.1), custom_call_target="tpu_custom_call" | custom-call | flops 536870912 | bytes 10485760 | tf_op jit(solution)/shard_map/pallas_call | solution.py:34
  95.9 2.7 %collective-permute-start.15 = (bf16[128,1024]{1,0:T(8,128)(2,1)S(1)}, bf16[128,1024]{1,0:T(8,128)(2,1)S(1)}, u32[]{:S(2)}, u32[]{:S(2)}) collective-permute-start(bf16[128,1024]{1,0:T(8,128)(2,1)S(1)} %get-tuple-element.67), channel_id=1, source_target_pairs={{0,64},{32,96},{64,0},{96,32},{1,65},{33,97},{65,1},{97,33},{2,66}... | collective-permute-start | bytes 786440 | tf_op jit(solution)/shard_map/ppermute | solution.py:360
  104.5 6.2 %collective-permute-done.15.b = bf16[128,1024]{1,0:T(8,128)(2,1)S(1)} collective-permute-done((bf16[128,1024]{1,0:T(8,128)(2,1)S(1)}, bf16[128,1024]{1,0:T(8,128)(2,1)S(1)}, u32[]{:S(2)}, u32[]{:S(2)}) %collective-permute-start.15) | collective-permute-done | bytes 262176 | tf_op jit(solution)/shard_map/ppermute | solution.py:360
  110.6 2.6 %collective-permute-done.13.refs_11_.refs_2_ = bf16[144,512]{1,0:T(8,128)(2,1)S(1)} collective-permute-done((bf16[144,512]{1,0:T(8,128)(2,1)S(1)}, bf16[144,512]{1,0:T(8,128)(2,1)S(1)}, u32[]{:S(2)}, u32[]{:S(2)}) %collective-permute-start.13) | collective-permute-done | bytes 147488 | tf_op jit(solution)/shard_map/ppermute | solution.py:360
  115.9 2.4 %collective-permute-start.17 = (bf16[384,1024]{1,0:T(8,128)(2,1)S(1)}, bf16[384,1024]{1,0:T(8,128)(2,1)S(1)}, u32[]{:S(2)}, u32[]{:S(2)}) collective-permute-start(bf16[384,1024]{1,0:T(8,128)(2,1)S(1)} %shard_map.107.refs_2_), channel_id=1, source_target_pairs={{0,1},{1,0},{2,3},{3,2},{4,5},{5,4},{6,7},{7,6},{8,9},{9,8},{10,11... | collective-permute-start | bytes 2359304 | tf_op jit(solution)/shard_map/ppermute | solution.py:348
  118.4 2.6 %shard_map.106 = (bf16[2,1024,512]{2,1,0:T(8,128)(2,1)}, f32[1,1]{1,0:T(1,128)}) custom-call(bf16[128,4224]{1,0:T(8,128)(2,1)S(1)} %bitcast.13, bf16[128,4224]{1,0:T(8,128)(2,1)S(1)} %collective-permute-done.1.x.refs_1_, bf16[384,1024]{1,0:T(8,128)(2,1)S(1)} %shard_map.105.refs_2_, bf16[384,1024]{1,0:T(8,128)(2,1)S(1)} %collective-permute-done.10.refs_3_, ...), custom_call_target="tpu_custom_call" | custom-call | flops 2147483648 | bytes 5242880 | tf_op jit(solution)/shard_map/pallas_call | solution.py:34
  121.0 4.7 %shard_map.108 = bf16[512,2048]{1,0:T(8,128)(2,1)} custom-call(bf16[128,4224]{1,0:T(8,128)(2,1)S(1)} %bitcast.9, bf16[128,4224]{1,0:T(8,128)(2,1)S(1)} %collective-permute-done.9.e.refs_1_, bf16[384,1024]{1,0:T(8,128)(2,1)S(1)} %shard_map.107.refs_2_, bf16[384,1024]{1,0:T(8,128)(2,1)S(1)} %collective-permute-done.17.refs_3_, ...), custom_call_target="tpu_custom_call" | custom-call | flops 2147483648 | bytes 7340032 | tf_op jit(solution)/shard_map/pallas_call | solution.py:34
  (69 shorter events, 26.3 us)
Async XLA Ops:
  2.4 2.4 %collective-permute-start = (bf16[4,8320]{1,0:T(4,128)(2,1)S(1)}, bf16[4,8320]{1,0:T(4,128)(2,1)S(1)}, u32[]{:S(2)}, u32[]{:S(2)}) collective-permute-start(bf16[4,8320]{1,0:T(4,128)(2,1)S(1)} %get-tuple-element.38), channel_id=1, source_target_pairs={{0,1},{1,0},{2,3},{3,2},{4,5},{5,4},{6,7},{7,6},{8,9},{9,8},{10,11... | collective-permute-start | bytes 199688 | tf_op jit(solution)/shard_map/ppermute | solution.py:348
  5.8 22.9 %all-to-all-start = ((bf16[16,8,4224]{2,1,0:T(8,128)(2,1)}), bf16[16,8,4224]{2,1,0:T(8,128)(2,1)S(1)}, u32[]{:S(2)}, u32[]{:S(2)}) async-start(bf16[16,8,4224]{2,1,0:T(8,128)(2,1)} %get-tuple-element.39), calls=%async_computation | async-start | bytes 2162688 | tf_op jit(solution)/shard_map/all_to_all | solution.py:352
  28.7 6.6 %collective-permute-start.1 = (bf16[128,4224]{1,0:T(8,128)(2,1)S(1)}, bf16[128,4224]{1,0:T(8,128)(2,1)S(1)}, u32[]{:S(2)}, u32[]{:S(2)}) collective-permute-start(bf16[128,4224]{1,0:T(8,128)(2,1)S(1)} %bitcast.10), channel_id=1, source_target_pairs={{0,1},{1,0},{2,3},{3,2},{4,5},{5,4},{6,7},{7,6},{8,9},{9,8},{10,11... | collective-permute-start | bytes 3244040 | tf_op jit(solution)/shard_map/ppermute | solution.py:348
  39.1 2.7 %collective-permute-start.2 = (bf16[128,4096]{1,0:T(8,128)(2,1)S(1)}, bf16[128,4096]{1,0:T(8,128)(2,1)S(1)}, u32[]{:S(2)}, u32[]{:S(2)}) collective-permute-start(bf16[128,4096]{1,0:T(8,128)(2,1)S(1)} %get-tuple-element.47), channel_id=1, source_target_pairs={{0,1},{1,0},{2,3},{3,2},{4,5},{5,4},{6,7},{7,6},{8,9},{9,8},{10,11... | collective-permute-start | bytes 3145736 | tf_op jit(solution)/shard_map/ppermute | solution.py:348
  42.9 22.0 %copy-start.16 = (f32[2,4096]{1,0:T(2,128)S(1)}, f32[2,4096]{1,0:T(2,128)}, u32[]{:S(2)}) copy-start(f32[2,4096]{1,0:T(2,128)} %bias.1) | copy-start | bytes 98308
  42.9 22.0 %all-to-all-start.1 = ((bf16[16,8,4096]{2,1,0:T(8,128)(2,1)}), bf16[16,8,4096]{2,1,0:T(8,128)(2,1)S(1)}, u32[]{:S(2)}, u32[]{:S(2)}) async-start(bf16[16,8,4096]{2,1,0:T(8,128)(2,1)} %bitcast.3), calls=%async_computation.1 | async-start | bytes 2097152 | tf_op jit(solution)/shard_map/all_to_all | solution.py:352
  46.8 10.2 %collective-permute-start.3 = (bf16[128,1024]{1,0:T(8,128)(2,1)S(1)}, bf16[128,1024]{1,0:T(8,128)(2,1)S(1)}, u32[]{:S(2)}, u32[]{:S(2)}) collective-permute-start(bf16[128,1024]{1,0:T(8,128)(2,1)S(1)} %get-tuple-element.48), channel_id=1, source_target_pairs={{0,32},{32,64},{64,96},{96,0},{1,33},{33,65},{65,97},{97,1},{2,34}... | collective-permute-start | bytes 786440 | tf_op jit(solution)/shard_map/ppermute | solution.py:360
  48.5 15.0 %collective-permute-start.4 = (bf16[128,1024]{1,0:T(8,128)(2,1)S(1)}, bf16[128,1024]{1,0:T(8,128)(2,1)S(1)}, u32[]{:S(2)}, u32[]{:S(2)}) collective-permute-start(bf16[128,1024]{1,0:T(8,128)(2,1)S(1)} %get-tuple-element.49), channel_id=1, source_target_pairs={{0,64},{32,96},{64,0},{96,32},{1,65},{33,97},{65,1},{97,33},{2,66}... | collective-permute-start | bytes 786440 | tf_op jit(solution)/shard_map/ppermute | solution.py:360
  51.8 12.4 %collective-permute-start.5 = (bf16[128,1024]{1,0:T(8,128)(2,1)S(1)}, bf16[128,1024]{1,0:T(8,128)(2,1)S(1)}, u32[]{:S(2)}, u32[]{:S(2)}) collective-permute-start(bf16[128,1024]{1,0:T(8,128)(2,1)S(1)} %get-tuple-element.50), channel_id=1, source_target_pairs={{0,96},{32,0},{64,32},{96,64},{1,97},{33,1},{65,33},{97,65},{2,98}... | collective-permute-start | bytes 786440 | tf_op jit(solution)/shard_map/ppermute | solution.py:360
  66.2 21.6 %all-to-all-start.2 = ((bf16[16,8,4224]{2,1,0:T(8,128)(2,1)}), bf16[16,8,4224]{2,1,0:T(8,128)(2,1)S(1)}, u32[]{:S(2)}, u32[]{:S(2)}) async-start(bf16[16,8,4224]{2,1,0:T(8,128)(2,1)} %shard_map.102), calls=%async_computation.2 | async-start | bytes 2162688 | tf_op jit(solution)/shard_map/all_to_all | solution.py:352
  72.4 6.7 %collective-permute-start.8 = (bf16[144,512]{1,0:T(8,128)(2,1)S(1)}, bf16[144,512]{1,0:T(8,128)(2,1)S(1)}, u32[]{:S(2)}, u32[]{:S(2)}) collective-permute-start(bf16[144,512]{1,0:T(8,128)(2,1)S(1)} %get-tuple-element.61.feats.refs_4_), channel_id=1, source_target_pairs={{0,96},{32,0},{64,32},{96,64},{1,97},{33,1},{65,33},{97,65},{2,98}... | collective-permute-start | bytes 442376 | tf_op jit(solution)/shard_map/ppermute | solution.py:360
  74.7 5.8 %collective-permute-start.7 = (bf16[144,512]{1,0:T(8,128)(2,1)S(1)}, bf16[144,512]{1,0:T(8,128)(2,1)S(1)}, u32[]{:S(2)}, u32[]{:S(2)}) collective-permute-start(bf16[144,512]{1,0:T(8,128)(2,1)S(1)} %get-tuple-element.61.feats.refs_4_), channel_id=1, source_target_pairs={{0,64},{32,96},{64,0},{96,32},{1,65},{33,97},{65,1},{97,33},{2,66}... | collective-permute-start | bytes 442376 | tf_op jit(solution)/shard_map/ppermute | solution.py:360
  75.2 9.6 %collective-permute-start.6 = (bf16[144,512]{1,0:T(8,128)(2,1)S(1)}, bf16[144,512]{1,0:T(8,128)(2,1)S(1)}, u32[]{:S(2)}, u32[]{:S(2)}) collective-permute-start(bf16[144,512]{1,0:T(8,128)(2,1)S(1)} %get-tuple-element.61.feats.refs_4_), channel_id=1, source_target_pairs={{0,32},{32,64},{64,96},{96,0},{1,33},{33,65},{65,97},{97,1},{2,34}... | collective-permute-start | bytes 442376 | tf_op jit(solution)/shard_map/ppermute | solution.py:360
  87.8 10.8 %collective-permute-start.9 = (bf16[128,4224]{1,0:T(8,128)(2,1)S(1)}, bf16[128,4224]{1,0:T(8,128)(2,1)S(1)}, u32[]{:S(2)}, u32[]{:S(2)}) collective-permute-start(bf16[128,4224]{1,0:T(8,128)(2,1)S(1)} %bitcast.6), channel_id=1, source_target_pairs={{0,1},{1,0},{2,3},{3,2},{4,5},{5,4},{6,7},{7,6},{8,9},{9,8},{10,11... | collective-permute-start | bytes 3244040 | tf_op jit(solution)/shard_map/ppermute | solution.py:348
  94.5 9.5 %collective-permute-start.14 = (bf16[128,1024]{1,0:T(8,128)(2,1)S(1)}, bf16[128,1024]{1,0:T(8,128)(2,1)S(1)}, u32[]{:S(2)}, u32[]{:S(2)}) collective-permute-start(bf16[128,1024]{1,0:T(8,128)(2,1)S(1)} %get-tuple-element.66), channel_id=1, source_target_pairs={{0,32},{32,64},{64,96},{96,0},{1,33},{33,65},{65,97},{97,1},{2,34}... | collective-permute-start | bytes 786440 | tf_op jit(solution)/shard_map/ppermute | solution.py:360
  95.9 14.8 %collective-permute-start.15 = (bf16[128,1024]{1,0:T(8,128)(2,1)S(1)}, bf16[128,1024]{1,0:T(8,128)(2,1)S(1)}, u32[]{:S(2)}, u32[]{:S(2)}) collective-permute-start(bf16[128,1024]{1,0:T(8,128)(2,1)S(1)} %get-tuple-element.67), channel_id=1, source_target_pairs={{0,64},{32,96},{64,0},{96,32},{1,65},{33,97},{65,1},{97,33},{2,66}... | collective-permute-start | bytes 786440 | tf_op jit(solution)/shard_map/ppermute | solution.py:360
  98.6 12.1 %collective-permute-start.16 = (bf16[128,1024]{1,0:T(8,128)(2,1)S(1)}, bf16[128,1024]{1,0:T(8,128)(2,1)S(1)}, u32[]{:S(2)}, u32[]{:S(2)}) collective-permute-start(bf16[128,1024]{1,0:T(8,128)(2,1)S(1)} %get-tuple-element.68), channel_id=1, source_target_pairs={{0,96},{32,0},{64,32},{96,64},{1,97},{33,1},{65,33},{97,65},{2,98}... | collective-permute-start | bytes 786440 | tf_op jit(solution)/shard_map/ppermute | solution.py:360
  100.2 18.2 %copy-start.11 = (bf16[144,512]{1,0:T(8,128)(2,1)S(1)}, bf16[144,512]{1,0:T(8,128)(2,1)}, u32[]{:S(2)}) copy-start(bf16[144,512]{1,0:T(8,128)(2,1)} %copy-done.10) | copy-start | bytes 442372
  100.2 18.2 %copy-start.13 = (bf16[144,512]{1,0:T(8,128)(2,1)S(1)}, bf16[144,512]{1,0:T(8,128)(2,1)}, u32[]{:S(2)}) copy-start(bf16[144,512]{1,0:T(8,128)(2,1)} %copy-done.12) | copy-start | bytes 442372
  100.3 18.1 %collective-permute-start.10 = (bf16[384,1024]{1,0:T(8,128)(2,1)S(1)}, bf16[384,1024]{1,0:T(8,128)(2,1)S(1)}, u32[]{:S(2)}, u32[]{:S(2)}) collective-permute-start(bf16[384,1024]{1,0:T(8,128)(2,1)S(1)} %shard_map.105.refs_2_), channel_id=1, source_target_pairs={{0,1},{1,0},{2,3},{3,2},{4,5},{5,4},{6,7},{7,6},{8,9},{9,8},{10,11... | collective-permute-start | bytes 2359304 | tf_op jit(solution)/shard_map/ppermute | solution.py:348
  100.9 12.3 %collective-permute-start.13 = (bf16[144,512]{1,0:T(8,128)(2,1)S(1)}, bf16[144,512]{1,0:T(8,128)(2,1)S(1)}, u32[]{:S(2)}, u32[]{:S(2)}) collective-permute-start(bf16[144,512]{1,0:T(8,128)(2,1)S(1)} %shard_map.104.refs_0_.refs_8_), channel_id=1, source_target_pairs={{0,96},{32,0},{64,32},{96,64},{1,97},{33,1},{65,33},{97,65},{2,98}... | collective-permute-start | bytes 442376 | tf_op jit(solution)/shard_map/ppermute | solution.py:360
  104.0 9.8 %collective-permute-start.12 = (bf16[144,512]{1,0:T(8,128)(2,1)S(1)}, bf16[144,512]{1,0:T(8,128)(2,1)S(1)}, u32[]{:S(2)}, u32[]{:S(2)}) collective-permute-start(bf16[144,512]{1,0:T(8,128)(2,1)S(1)} %shard_map.104.refs_0_.refs_8_), channel_id=1, source_target_pairs={{0,64},{32,96},{64,0},{96,32},{1,65},{33,97},{65,1},{97,33},{2,66}... | collective-permute-start | bytes 442376 | tf_op jit(solution)/shard_map/ppermute | solution.py:360
  110.6 5.2 %collective-permute-start.11 = (bf16[144,512]{1,0:T(8,128)(2,1)S(1)}, bf16[144,512]{1,0:T(8,128)(2,1)S(1)}, u32[]{:S(2)}, u32[]{:S(2)}) collective-permute-start(bf16[144,512]{1,0:T(8,128)(2,1)S(1)} %shard_map.104.refs_0_.refs_8_), channel_id=1, source_target_pairs={{0,32},{32,64},{64,96},{96,0},{1,33},{33,65},{65,97},{97,1},{2,34}... | collective-permute-start | bytes 442376 | tf_op jit(solution)/shard_map/ppermute | solution.py:360
  115.9 5.0 %collective-permute-start.17 = (bf16[384,1024]{1,0:T(8,128)(2,1)S(1)}, bf16[384,1024]{1,0:T(8,128)(2,1)S(1)}, u32[]{:S(2)}, u32[]{:S(2)}) collective-permute-start(bf16[384,1024]{1,0:T(8,128)(2,1)S(1)} %shard_map.107.refs_2_), channel_id=1, source_target_pairs={{0,1},{1,0},{2,3},{3,2},{4,5},{5,4},{6,7},{7,6},{8,9},{9,8},{10,11... | collective-permute-start | bytes 2359304 | tf_op jit(solution)/shard_map/ppermute | solution.py:348
  (15 other events, 45.9 us)

commit v3 on v2

v3 whole, which is shorter than its diff:
```python
import jax
import jax.numpy as jnp
from jax import lax
from jax.experimental import pallas as pl
from jax.experimental.pallas import tpu as pltpu
from jax.sharding import Mesh
from jax.sharding import PartitionSpec as P

sparsity_weight = 1.0
loss_scale = 8.0
norm_eps = 1e-06

ALL = ("z", "x", "y", "c")
NZ = 4
CHIPS = 16
WIDTH = 8192
HALF = 4096
SUB = 1024
LOCAL = 512
ROWS = 128
PAD = 128
MIB = 1 << 20
f32 = jnp.float32
bf16 = jnp.bfloat16

VM = pl.BlockSpec(memory_space=pltpu.VMEM)


def at_hbm(v):
    return pltpu.with_memory_space_constraint(v, pltpu.HBM)


def call(body, outs, args, specs=None, scratch=(), vmem=None, flops=0, nbytes=0, out_specs=None):
    return pl.pallas_call(
        body,
        out_shape=[o[2](o[0], o[1]) if len(o) == 3 else jax.ShapeDtypeStruct(*o) for o in outs],
        in_specs=specs or [VM] * len(args),
        out_specs=out_specs or [VM] * len(outs),
        scratch_shapes=list(scratch),
        compiler_params=pltpu.CompilerParams(vmem_limit_bytes=vmem or 16 * MIB),
        cost_estimate=pl.CostEstimate(flops=flops, bytes_accessed=nbytes, transcendentals=0),
    )(*args)


def lanes(start, size):
    return pl.ds(pl.multiple_of(start, 128), size)


def split3(v):
    hi = v.astype(bf16)
    rest = v - hi.astype(f32)
    mid = rest.astype(bf16)
    low = (rest - mid.astype(f32)).astype(bf16)
    return hi, mid, low


def prep_kernel(length, acts_hbm, group_hbm, keep, send, acts, group, sems):
    copies = [
        pltpu.make_async_copy(src, dst, sems.at[i])
        for i, (src, dst) in enumerate(((acts_hbm, acts), (group_hbm, group)))
    ]
    for copy in copies:
        copy.start()
    for copy in copies:
        copy.wait()
    c = lax.axis_index("c")
    slot = lax.broadcasted_iota(jnp.int32, (1, 5), 1)
    held = jnp.sum(jnp.where(group[...] == NZ, slot, 0), axis=1, keepdims=True)
    k = lax.broadcasted_iota(jnp.int32, (4, 1), 0)
    later = k >= held
    src = k + later.astype(jnp.int32)
    live = (src < length[0]).astype(f32)
    live = jnp.broadcast_to(live, (4, PAD)).astype(bf16)

    def pick(cols):
        rows = acts[:, cols].astype(f32)
        return jnp.where(later, rows[1:5], rows[0:4]).astype(bf16)

    for out, core in ((keep, c), (send, 1 - c)):
        out[:, :HALF] = pick(lanes(core * HALF, HALF))
        for q in range(NZ):
            out[:, HALF + q * SUB : HALF + (q + 1) * SUB] = pick(lanes(q * 2 * SUB + core * SUB, SUB))
        out[:, 2 * HALF :] = live


def join_kernel(own, other, out, mine):
    first = lax.axis_index("c") == 0
    a, b = own[...].astype(f32), other[...].astype(f32)
    rows = jnp.concatenate([jnp.where(first, a, b), jnp.where(first, b, a)], axis=0)
    mine[...] = rows[:, HALF:].astype(bf16)
    for i in range(CHIPS):
        out[i, :, :HALF] = rows[:, :HALF].astype(bf16)
        out[i, :, HALF:] = rows[:, 2 * HALF :].astype(bf16)


def norm_kernel(w_dec_hbm, norm_row, norm_col, w_dec, sems):
    rows = LOCAL // 4
    copies = [
        pltpu.make_async_copy(w_dec_hbm.at[pl.ds(i * rows, rows)], w_dec.at[pl.ds(i * rows, rows)], sems.at[i])
        for i in range(4)
    ]
    for copy in copies:
        copy.start()
    for i in range(4):
        copies[i].wait()
        n = i * rows
        for s in range(2):

            def add(j, total):
                for m in range(4):
                    v = w_dec[n : n + rows, lanes(s * HALF + j * 512 + m * 128, 128)].astype(f32)
                    total = total + v * v
                return total

            total = lax.fori_loop(0, HALF // 512, add, jnp.zeros((rows, 128), f32))
            norm_row[s : s + 1, n : n + rows] = jnp.sqrt(jnp.sum(total.T, axis=0, keepdims=True) + norm_eps)
            norm_col[n : n + rows, s : s + 1] = jnp.sqrt(jnp.sum(total, axis=1, keepdims=True) + norm_eps)


def fetch_enc(w_hbm, core, buf, sems, at=0):
    copies = [
        pltpu.make_async_copy(w_hbm.at[core, pl.ds(i * SUB, SUB)], buf.at[pl.ds(i * SUB, SUB)], sems.at[at + i])
        for i in range(4)
    ]
    for copy in copies:
        copy.start()
    return copies


def fetch_dec(w_hbm, core, buf, sems, at=0):
    copies = [
        pltpu.make_async_copy(w_hbm.at[:, lanes(q * 2 * SUB + core * SUB, SUB)], buf.at[q], sems.at[at + q])
        for q in range(NZ)
    ]
    for copy in copies:
        copy.start()
    return copies


def encode_own_kernel(x, w_enc, acc, rest, mask, home, p1, p2, p3, buf, sems):
    z, c = lax.axis_index("z"), lax.axis_index("c")
    copies = fetch_enc(w_enc, c, buf, sems)
    later = fetch_enc(w_enc, 1 - c, rest, sems, 4)
    mask[...] = x[:, HALF:]
    home[...] = x[:, lanes(z * SUB, SUB)]
    for k, out in enumerate((p1, p2, p3)):
        out[...] = x[:, lanes(lax.rem(z + k + 1, NZ) * SUB, SUB)]
    for i in range(0, 4, 2):
        copies[i].wait()
        copies[i + 1].wait()
        rows = slice(i * SUB, (i + 2) * SUB)
        for n in range(0, LOCAL, 256):
            part = jnp.dot(x[:, rows], buf[rows, n : n + 256], preferred_element_type=f32)
            acc[:, n : n + 256] = part if i == 0 else acc[:, n : n + 256] + part
    for copy in later:
        copy.wait()


def encode_kernel(x, mask, part, bias, w_enc, w_dec, act_out, feats_out, send, home, dec, dec_sems):
    z, c = lax.axis_index("z"), lax.axis_index("c")
    dec_copies = fetch_dec(w_dec, 1 - c, dec, dec_sems)
    home[...] = x[:, lanes(z * SUB, SUB)]
    live = mask[:, 0:1].astype(f32)
    count = jnp.sum(live, axis=0, keepdims=True)
    for n in range(0, LOCAL, 256):
        pre = part[:, n : n + 256] + jnp.dot(x[:, :HALF], w_enc[:, n : n + 256], preferred_element_type=f32)
        act = jnp.maximum(pre + bias[:, n : n + 256], 0.0)
        feats = act * act
        act_out[:, n : n + 256] = act
        feats_out[:ROWS, n : n + 256] = feats.astype(bf16)
        fsum = jnp.sum(feats * live, axis=0, keepdims=True)
        tail = jnp.zeros((16, 256), f32)
        row = lax.broadcasted_iota(jnp.int32, (16, 256), 0)
        for i, piece in enumerate((*split3(fsum), jnp.broadcast_to(count, (1, 256)))):
            tail = jnp.where(row == i, piece.astype(f32), tail)
        feats_out[ROWS:, n : n + 256] = tail.astype(bf16)
    feats16 = feats_out[:ROWS, :]
    for q in range(NZ):
        dec_copies[q].wait()
        send[:, q * SUB : (q + 1) * SUB] = jnp.dot(feats16, dec[q], preferred_element_type=f32).astype(bf16)


def decode_own_kernel(feats, w_dec, part, buf, sems):
    copies = fetch_dec(w_dec, lax.axis_index("c"), buf, sems)
    feats16 = feats[:ROWS, :]
    for q in range(NZ):
        copies[q].wait()
        part[:, q * SUB : (q + 1) * SUB] = jnp.dot(feats16, buf[q], preferred_element_type=f32)


def turn_kernel(home_own, home_other, own, other, *refs):
    z, c = lax.axis_index("z"), lax.axis_index("c")
    feats, norm_col, w_dec = refs[0:4], refs[4], refs[5]
    xt, ft, scale, count, w, sem = refs[7:]
    fetch = pltpu.make_async_copy(w_dec.at[:, lanes(z * 2 * SUB, 2 * SUB)], w, sem)
    fetch.start()
    fsum = jnp.zeros((1, LOCAL), f32)
    total = jnp.zeros((1, 1), f32)
    for side, mine, rest in ((c, home_own, own), (1 - c, home_other, other)):
        xt[side, :, :ROWS] = mine[...].T
        for k in range(1, NZ):
            xt[side, :, k * ROWS : (k + 1) * ROWS] = rest[(k - 1) * ROWS : k * ROWS, :].T
    for k in range(NZ):
        ft[:, k * ROWS : (k + 1) * ROWS] = feats[k][:ROWS, :].T
        fsum = fsum + jnp.sum(feats[k][ROWS : ROWS + 3, :].astype(f32), axis=0, keepdims=True)
        total = total + feats[k][ROWS + 3 : ROWS + 4, 0:1].astype(f32)
    count[...] = total
    fsum = jnp.broadcast_to(fsum, (128, LOCAL)).T[:, 0:1]
    norm = jnp.where(z < 2, norm_col[:, 0:1], norm_col[:, 1:2])
    scale[...] = sparsity_weight * fsum / norm
    fetch.wait()


def add_kernel(own, other, out):
    for n in range(0, HALF, SUB):
        out[:, n : n + SUB] = (own[:, n : n + SUB] + other[:, n : n + SUB].astype(f32)).astype(bf16)


def err_kernel(parts, mine, bias, feats, norm_row, out):
    c = lax.axis_index("c")
    live = mine[:, HALF : HALF + 1].astype(f32)
    square = jnp.zeros((8, SUB), f32)
    for q in range(NZ):
        cols = slice(q * SUB, (q + 1) * SUB)
        total = parts[0, :, cols].astype(f32)
        for i in range(1, CHIPS):
            total = total + parts[i, :, cols].astype(f32)
        add = bias[q // 2 : q // 2 + 1, lanes((q % 2) * 2 * SUB + c * SUB, SUB)]
        err = (total + add - mine[:, cols].astype(f32)) * live
        square = square + err * err
        err16 = err.astype(bf16)
        for i in range(CHIPS):
            out[i, :, cols] = err16
    squares = jnp.sum(jnp.sum(square, axis=0, keepdims=True), axis=1, keepdims=True)
    fsum = jnp.sum(feats[ROWS : ROWS + 3, :].astype(f32), axis=0, keepdims=True)
    nsum = norm_row[0:1, :] + norm_row[1:2, :]
    sparse = sparsity_weight * jnp.sum(fsum * nsum, axis=1, keepdims=True)
    lane = lax.broadcasted_iota(jnp.int32, (8, PAD), 1)
    row = lax.broadcasted_iota(jnp.int32, (8, PAD), 0)
    tail = jnp.zeros((8, PAD), f32)
    for i, piece in enumerate(split3(squares + sparse)):
        tail = jnp.where((lane == i) & (row == 0), piece.astype(f32), tail)
    for i in range(CHIPS):
        out[i, :, HALF:] = tail.astype(bf16)


def slice_kernel(e, s1, s2, s3):
    z = lax.axis_index("z")
    for k, out in enumerate((s1, s2, s3)):
        out[...] = e[:, lanes(lax.rem(z + k + 1, NZ) * SUB, SUB)]


def dpre_kernel(own, e, mask, norm_row, act_hbm, w_dec, out, act, buf, act_sem, sems):
    c = lax.axis_index("c")
    copies = fetch_dec(w_dec, c, buf.at[0], sems) + fetch_dec(w_dec, 1 - c, buf.at[1], sems, 4)
    fetch = pltpu.make_async_copy(act_hbm, act, act_sem)
    fetch.start()
    both = e[:, HALF:].astype(f32) + own[:, HALF:].astype(f32)
    both = jnp.sum(jnp.sum(both, axis=0, keepdims=True), axis=1, keepdims=True)
    lane = lax.broadcasted_iota(jnp.int32, (16, LOCAL), 1)
    tail = jnp.zeros((16, LOCAL), f32)
    for i, piece in enumerate(split3(both)):
        tail = jnp.where(lane == i, piece.astype(f32), tail)
    out[ROWS:, :] = tail.astype(bf16)
    live = mask[:, 0:1].astype(f32)
    totals = [jnp.zeros((ROWS, 256), f32), jnp.zeros((ROWS, 256), f32)]
    for q in range(2 * NZ):
        copies[q].wait()
        rows = (own, e)[q // NZ]
        for i in range(2):
            totals[i] = totals[i] + lax.dot_general(
                rows[:, (q % NZ) * SUB : (q % NZ + 1) * SUB],
                buf[q // NZ, q % NZ, i * 256 : (i + 1) * 256, :],
                (((1,), (1,)), ((), ())),
                preferred_element_type=f32,
            )
    fetch.wait()
    for i in range(2):
        n = slice(i * 256, (i + 1) * 256)
        nsum = norm_row[0:1, n] + norm_row[1:2, n]
        grad = 2.0 * totals[i] + sparsity_weight * live * nsum
        out[:ROWS, n] = (grad * 2.0 * act[:, n]).astype(bf16)


def merge_kernel(a, b, d, out):
    for k, v in enumerate((a, b, d)):
        out[k * ROWS : (k + 1) * ROWS, :] = v[...]


def part_kernel(*refs):
    pres, slices, count = refs[0:4], refs[4:7], refs[7]
    es, ds, loss = refs[8:]
    total = jnp.zeros((1, 1), f32)
    for k, p in enumerate(pres):
        total = total + jnp.sum(p[ROWS : ROWS + 1, 0:3].astype(f32), axis=1, keepdims=True)
        ds[k * ROWS : (k + 1) * ROWS, :] = p[:ROWS, :]
    for k, p in enumerate(slices):
        es[k * ROWS : (k + 1) * ROWS, :] = p[...]
    loss[...] = total / (count[...] * WIDTH)


def grad_enc_kernel(xt, count, ds, out, done, sems):
    factor = loss_scale / count[...]
    copies = []
    for i in range(4):
        rows = pl.ds(i % 2 * 512, 512)
        for n in range(0, 512, 256):
            at = i % 2 * 512 + n
            part = jnp.dot(xt[i // 2, at : at + 256, :], ds[...], preferred_element_type=f32)
            done[i // 2, at : at + 256, :] = (part * factor).astype(bf16)
        copies.append(pltpu.make_async_copy(done.at[i // 2, rows], out.at[i // 2, rows], sems.at[i]))
        copies[-1].start()
    for copy in copies:
        copy.wait()


def grad_dec_kernel(e_own, e_other, own, other, ft, scale, count, w, out, es, done, sems):
    z, c = lax.axis_index("z"), lax.axis_index("c")
    factor = loss_scale / count[...]
    for side, plane, rest in ((c, e_own, own), (1 - c, e_other, other)):
        es[:ROWS, lanes(side * SUB, SUB)] = plane[:, lanes(z * SUB, SUB)]
        es[ROWS:, lanes(side * SUB, SUB)] = rest[...]
    copies = []
    for i, n in enumerate(range(0, LOCAL, 128)):
        for m in range(0, 2 * SUB, 512):
            part = 2.0 * jnp.dot(ft[n : n + 128, :], es[:, m : m + 512], preferred_element_type=f32)
            part = part + scale[n : n + 128, :] * w[n : n + 128, m : m + 512].astype(f32)
            done[n : n + 128, m : m + 512] = (part * factor).astype(bf16)
        piece = pl.ds(n, 128)
        copies.append(pltpu.make_async_copy(done.at[piece], out.at[piece], sems.at[i]))
        copies[-1].start()
    for copy in copies:
        copy.wait()


def swap(v):
    return lax.ppermute(v, "c", [(0, 1), (1, 0)])


def chips(v):
    return lax.all_to_all(v, ("x", "y"), split_axis=0, concat_axis=0, tiled=True)


def planes(v):
    return lax.all_to_all(v, "z", split_axis=0, concat_axis=0, tiled=True)


def shift(v, k):
    return lax.ppermute(v, "z", [(i, (i + k) % NZ) for i in range(NZ)])


def shards(acts, chat_len, group_of, w_enc, b_enc, w_dec, b_dec):
    half_flops = 2 * ROWS * HALF * LOCAL
    w_enc, w_dec = at_hbm(w_enc), at_hbm(w_dec)
    dec_scratch = [pltpu.VMEM((4, LOCAL, SUB), bf16), pltpu.SemaphoreType.DMA((4,))]
    hbm = pl.BlockSpec(memory_space=pltpu.HBM)
    anywhere = pl.BlockSpec(memory_space=pl.ANY)
    keep, send = call(
        prep_kernel,
        [((4, 2 * HALF + PAD), bf16)] * 2,
        (chat_len, at_hbm(acts), at_hbm(group_of.reshape(1, 5))),
        [pl.BlockSpec(memory_space=pltpu.SMEM), hbm, hbm],
        [
            pltpu.VMEM((5, WIDTH), bf16),
            pltpu.VMEM((1, 5), jnp.int32),
            pltpu.SemaphoreType.DMA((2,)),
        ],
        vmem=4 * MIB,
    )
    block, mine = call(
        join_kernel,
        [((CHIPS, 8, HALF + PAD), bf16), ((8, HALF + PAD), bf16)],
        (keep, swap(send)),
        vmem=4 * MIB,
    )
    norm_row, norm_col = call(
        norm_kernel,
        [((2, LOCAL), f32), ((LOCAL, 2), f32)],
        (w_dec,),
        [hbm],
        [pltpu.VMEM((LOCAL, WIDTH), bf16), pltpu.SemaphoreType.DMA((4,))],
        flops=4 * LOCAL * WIDTH,
        nbytes=8 * MIB,
    )
    x_own, norm_row, norm_col = lax.optimization_barrier((chips(block), norm_row, norm_col))
    x_own = x_own.reshape(ROWS, HALF + PAD)
    x_other = swap(x_own)
    acc, w_rest, mask, home_own, *xs = call(
        encode_own_kernel,
        [((ROWS, LOCAL), f32), ((HALF, LOCAL), bf16, pltpu.VMEM), ((ROWS, PAD), bf16)] + [((ROWS, SUB), bf16)] * 4,
        (x_own, w_enc),
        [VM, hbm],
        [pltpu.VMEM((HALF, LOCAL), bf16), pltpu.SemaphoreType.DMA((8,))],
        flops=half_flops,
        nbytes=10 * MIB,
    )
    act, feats, part_send, home_other = call(
        encode_kernel,
        [((ROWS, LOCAL), f32), ((ROWS + 16, LOCAL), bf16), ((ROWS, HALF), bf16), ((ROWS, SUB), bf16)],
        (x_other, mask, acc, b_enc.reshape(1, LOCAL), w_rest, w_dec),
        [VM] * 5 + [hbm],
        dec_scratch,
        flops=2 * half_flops,
        nbytes=8 * MIB,
    )
    part_recv = swap(part_send)
    (part_own,) = call(
        decode_own_kernel,
        [((ROWS, HALF), f32)],
        (feats, w_dec),
        [VM, hbm],
        dec_scratch,
        flops=half_flops,
        nbytes=6 * MIB,
    )
    (part,) = call(add_kernel, [((ROWS, HALF), bf16)], (part_own, part_recv), vmem=8 * MIB)
    parts = chips(part.reshape(CHIPS, 8, HALF))
    xs = [shift(xs[k - 1], k) for k in range(1, NZ)]
    (block,) = call(
        err_kernel,
        [((CHIPS, 8, HALF + PAD), bf16)],
        (parts, mine, b_dec, feats, norm_row),
    )
    block, *xs = lax.optimization_barrier((block, *xs))
    (xs,) = call(merge_kernel, [((3 * ROWS, SUB), bf16)], xs, nbytes=2 * MIB)
    fs = [feats] + [shift(feats, k) for k in range(1, NZ)]
    e_own, xs, xs_other, *fs = lax.optimization_barrier((chips(block), xs, swap(xs), *fs))
    e_own = e_own.reshape(ROWS, HALF + PAD)
    e_other = swap(e_own)
    slices = call(slice_kernel, [((ROWS, SUB), bf16)] * 3, (e_own,), nbytes=MIB)
    es = [shift(slices[k - 1], k) for k in range(1, NZ)]
    (dpre,) = call(
        dpre_kernel,
        [((ROWS + 16, LOCAL), bf16)],
        (e_own, e_other, mask, norm_row, at_hbm(act), w_dec),
        [VM] * 4 + [hbm] * 2,
        [
            pltpu.VMEM((ROWS, LOCAL), f32),
            pltpu.VMEM((2, NZ, LOCAL, SUB), bf16),
            pltpu.SemaphoreType.DMA,
            pltpu.SemaphoreType.DMA((8,)),
        ],
        flops=2 * half_flops,
        nbytes=10 * MIB,
    )
    ds = [dpre] + [shift(dpre, k) for k in range(1, NZ)]
    xt, ft, scale, count, w_slice = call(
        turn_kernel,
        [
            ((2, SUB, NZ * ROWS), bf16),
            ((LOCAL, NZ * ROWS), bf16),
            ((LOCAL, 1), f32),
            ((1, 1), f32),
            ((LOCAL, 2 * SUB), bf16),
        ],
        (home_own, home_other, xs, xs_other, *fs, norm_col, w_dec, dpre),
        [VM] * 9 + [hbm, anywhere],
        [pltpu.SemaphoreType.DMA],
        nbytes=6 * MIB,
    )
    es, ds, loss = call(
        part_kernel,
        [((3 * ROWS, SUB), bf16), ((NZ * ROWS, LOCAL), bf16), ((1, 1), f32)],
        (*ds, *es, count),
        nbytes=3 * MIB,
    )
    (grad_enc,) = call(
        grad_enc_kernel,
        [((2, SUB, LOCAL), bf16)],
        (xt, count, ds),
        scratch=[pltpu.VMEM((2, SUB, LOCAL), bf16), pltpu.SemaphoreType.DMA((4,))],
        out_specs=[hbm],
        flops=4 * half_flops,
        nbytes=5 * MIB,
    )
    (grad_dec,) = call(
        grad_dec_kernel,
        [((LOCAL, 2 * SUB), bf16)],
        (e_own, e_other, es, swap(es), ft, scale, count, w_slice),
        scratch=[
            pltpu.VMEM((NZ * ROWS, 2 * SUB), bf16),
            pltpu.VMEM((LOCAL, 2 * SUB), bf16),
            pltpu.SemaphoreType.DMA((4,)),
        ],
        out_specs=[hbm],
        flops=4 * half_flops,
        nbytes=7 * MIB,
    )
    return grad_enc, grad_dec, loss.reshape(())


def solution(mesh):
    fine = Mesh(mesh.devices.reshape(4, 4, 4, 2), ALL)
    lat = ("x", "y", "c")
    return jax.shard_map(
        shards,
        mesh=fine,
        in_specs=(P(ALL, None), P(ALL), P(ALL, None), P(None, None, lat), P(lat), P(lat, None), P()),
        out_specs=(P(None, "z", lat), P(lat, "z"), P()),
        check_vma=False,
    )
```

time: 126 us -> 120 us (0.952)
  waiting for transfers between devices: 46.2 us -> 36.3 us
  starting transfers between devices: 41.9 us -> 45.5 us
  local copies, waits for them, and re-layouts: 4.89 us -> 1.35 us
  Pallas kernels: 31.2 us -> 34.7 us
    ppermute x12, waiting for transfers between devices: 32.6 us -> 12.7 us  [shift(): return lax.ppermute(v, 'z', [(i, (i + k) % NZ) for i in range(NZ)])]
    all_to_all x3, waiting for transfers between devices: 12.6 us -> 22.6 us  [chips(): lax.all_to_all(v, ('x', 'y'), split_axis=0, concat_axis=0, tiled=True)]
    ppermute x12, starting transfers between devices: 14.1 us -> 18.7 us  [shift(): return lax.ppermute(v, 'z', [(i, (i + k) % NZ) for i in range(NZ)])]
    unnamed x36 -> x18, local copies, waits for them, and re-layouts: 4.89 us -> 1.35 us
    pallas_call x15, Pallas kernels: 31.2 us -> 34.7 us  [call(): pl.pallas_call(body, out_shape=[o[2](o[0], o[1]) if len(o) == 3 else jax....]
  transfers between devices with their start and end apart: 21 -> 21, of which waited for: 14 -> 8; matrix products, arithmetic and copies ran while one was open for 0% -> 0% of each run, Pallas kernels for 15% -> 20%
where the time goes in v3:
time: 120 us; the launch traced here: 119 us
  starting transfers between devices  45.5 us (38%)
  waiting for transfers between devices  36.3 us (30%)
  Pallas kernels  34.7 us (29%)
  between operations  1.63 us (1%)
  local copies, waits for them, and re-layouts  1.35 us (1%)
    pallas_call x15, Pallas kernels, call(): pl.pallas_call(body, out_shape=[o[2](o[0], o[1]) if len(o) == 3 else jax....  34.7 us
    all_to_all x3, waiting for transfers between devices, chips(): lax.all_to_all(v, ('x', 'y'), split_axis=0, concat_axis=0, tiled=True)  22.6 us
    ppermute x12, starting transfers between devices, shift(): return lax.ppermute(v, 'z', [(i, (i + k) % NZ) for i in range(NZ)])  18.7 us
    all_to_all x3, starting transfers between devices, chips(): lax.all_to_all(v, ('x', 'y'), split_axis=0, concat_axis=0, tiled=True)  16.2 us
    ppermute x12, waiting for transfers between devices, shift(): return lax.ppermute(v, 'z', [(i, (i + k) % NZ) for i in range(NZ)])  12.7 us
    ppermute x6, starting transfers between devices, swap(): return lax.ppermute(v, 'c', [(0, 1), (1, 0)])  10.6 us
  transfers between devices with their start and end apart: 21, of which 8 were waited for; matrix products, arithmetic and copies ran while one was open for 0% of the time, Pallas kernels for 20%

profile of v3, /device:TPU:1, one launch (start us, length us, event | category | flops | bytes accessed | tf_op | source)
XLA Modules:
  0.0 119.4 jit_solution(8902430079679284126)
XLA Ops:
  5.8 6.8 %all-to-all-start = ((bf16[16,8,4224]{2,1,0:T(8,128)(2,1)}), bf16[16,8,4224]{2,1,0:T(8,128)(2,1)S(1)}, u32[]{:S(2)}, u32[]{:S(2)}) async-start(bf16[16,8,4224]{2,1,0:T(8,128)(2,1)} %get-tuple-element.47), calls=%async_computation | async-start | bytes 2162688 | tf_op jit(solution)/shard_map/all_to_all | solution.py:341
  12.7 5.0 %shard_map.96 = (f32[2,512]{1,0:T(2,128)S(1)}, f32[512,2]{1,0:T(8,128)S(1)}) custom-call(bf16[512,8192]{1,0:T(8,128)(2,1)} %refs_5_.1), custom_call_target="tpu_custom_call" | custom-call | flops 16777216 | bytes 8388608 | tf_op jit(solution)/shard_map/pallas_call | solution.py:34
  17.7 11.0 %all-to-all-done = bf16[16,8,4224]{2,1,0:T(8,128)(2,1)S(1)} async-done(((bf16[16,8,4224]{2,1,0:T(8,128)(2,1)}), bf16[16,8,4224]{2,1,0:T(8,128)(2,1)S(1)}, u32[]{:S(2)}, u32[]{:S(2)}) %all-to-all-start) | async-done | bytes 1081376 | tf_op jit(solution)/shard_map/all_to_all | solution.py:341
  28.7 3.1 %collective-permute-start.1 = (bf16[128,4224]{1,0:T(8,128)(2,1)S(1)}, bf16[128,4224]{1,0:T(8,128)(2,1)S(1)}, u32[]{:S(2)}, u32[]{:S(2)}) collective-permute-start(bf16[128,4224]{1,0:T(8,128)(2,1)S(1)} %bitcast.10), channel_id=1, source_target_pairs={{0,1},{1,0},{2,3},{3,2},{4,5},{5,4},{6,7},{7,6},{8,9},{9,8},{10,11... | collective-permute-start | bytes 3244040 | tf_op jit(solution)/shard_map/ppermute | solution.py:337
  31.8 4.2 %shard_map.97 = (f32[128,512]{1,0:T(8,128)S(1)}, bf16[4096,512]{1,0:T(8,128)(2,1)S(1)}, bf16[128,128]{1,0:T(8,128)(2,1)S(1)}, bf16[128,1024]{1,0:T(8,128)(2,1)S(...) custom-call(bf16[128,4224]{1,0:T(8,128)(2,1)S(1)} %bitcast.11, ...), custom_call_target="tpu_custom_call" | custom-call | flops 536870912 | bytes 10485760 | tf_op jit(solution)/shard_map/pallas_call | solution.py:34
  36.0 3.1 %shard_map.98 = (f32[128,512]{1,0:T(8,128)S(1)}, bf16[144,512]{1,0:T(8,128)(2,1)S(1)}, bf16[128,4096]{1,0:T(8,128)(2,1)S(1)}, bf16[128,1024]{1,0:T(8,128)(2,1)S(1)}) custom-call(bf16[128,4224]{1,0:T(8,128)(2,1)S(1)} %collective-permute-done.1.x, bf16[128,128]{1,0:T(8,128)(2,1)S(1)} %get-tuple-element.52.mask, f32[128,512]{1,0:T(8,128)S(1)} %get-tuple-element.53.part, ...), custom_call_target="tpu_custom_call" | custom-call | flops 1073741824 | bytes 8388608 | tf_op jit(solution)/shard_map/pallas_call | solution.py:34
  39.2 2.6 %shard_map.99.own = f32[128,4096]{1,0:T(8,128)S(1)} custom-call(bf16[144,512]{1,0:T(8,128)(2,1)S(1)} %get-tuple-element.69.feats.refs_0_, bf16[512,8192]{1,0:T(8,128)(2,1)} %refs_5_.1), custom_call_target="tpu_custom_call" | custom-call | flops 536870912 | bytes 6291456 | tf_op jit(solution)/shard_map/pallas_call | solution.py:34
  43.0 3.8 %all-to-all-start.1 = ((bf16[16,8,4096]{2,1,0:T(8,128)(2,1)}), bf16[16,8,4096]{2,1,0:T(8,128)(2,1)S(1)}, u32[]{:S(2)}, u32[]{:S(2)}) async-start(bf16[16,8,4096]{2,1,0:T(8,128)(2,1)} %bitcast.3), calls=%async_computation.1 | async-start | bytes 2097152 | tf_op jit(solution)/shard_map/all_to_all | solution.py:341
  48.5 3.3 %collective-permute-start.4 = (bf16[128,1024]{1,0:T(8,128)(2,1)S(1)}, bf16[128,1024]{1,0:T(8,128)(2,1)S(1)}, u32[]{:S(2)}, u32[]{:S(2)}) collective-permute-start(bf16[128,1024]{1,0:T(8,128)(2,1)S(1)} %get-tuple-element.61), channel_id=1, source_target_pairs={{0,64},{32,96},{64,0},{96,32},{1,65},{33,97},{65,1},{97,33},{2,66}... | collective-permute-start | bytes 786440 | tf_op jit(solution)/shard_map/ppermute | solution.py:349
  52.6 10.5 %all-to-all-done.1.parts = bf16[16,8,4096]{2,1,0:T(8,128)(2,1)S(1)} async-done(((bf16[16,8,4096]{2,1,0:T(8,128)(2,1)}), bf16[16,8,4096]{2,1,0:T(8,128)(2,1)S(1)}, u32[]{:S(2)}, u32[]{:S(2)}) %all-to-all-start.1) | async-done | bytes 1048608 | tf_op jit(solution)/shard_map/all_to_all | solution.py:341
  64.3 5.5 %all-to-all-start.2 = ((bf16[16,8,4224]{2,1,0:T(8,128)(2,1)}), bf16[16,8,4224]{2,1,0:T(8,128)(2,1)S(1)}, u32[]{:S(2)}, u32[]{:S(2)}) async-start(bf16[16,8,4224]{2,1,0:T(8,128)(2,1)} %shard_map.101), calls=%async_computation.2 | async-start | bytes 2162688 | tf_op jit(solution)/shard_map/all_to_all | solution.py:341
  69.9 1.9 %collective-permute-start.6 = (bf16[384,1024]{1,0:T(8,128)(2,1)S(1)}, bf16[384,1024]{1,0:T(8,128)(2,1)S(1)}, u32[]{:S(2)}, u32[]{:S(2)}) collective-permute-start(bf16[384,1024]{1,0:T(8,128)(2,1)S(1)} %shard_map.102.own), channel_id=1, source_target_pairs={{0,1},{1,0},{2,3},{3,2},{4,5},{5,4},{6,7},{7,6},{8,9},{9,8},{10,11... | collective-permute-start | bytes 2359304 | tf_op jit(solution)/shard_map/ppermute | solution.py:337
  72.6 3.0 %collective-permute-start.8 = (bf16[144,512]{1,0:T(8,128)(2,1)S(1)}, bf16[144,512]{1,0:T(8,128)(2,1)S(1)}, u32[]{:S(2)}, u32[]{:S(2)}) collective-permute-start(bf16[144,512]{1,0:T(8,128)(2,1)S(1)} %get-tuple-element.69.feats.refs_0_), channel_id=1, source_target_pairs={{0,64},{32,96},{64,0},{96,32},{1,65},{33,97},{65,1},{97,33},{2,66}... | collective-permute-start | bytes 442376 | tf_op jit(solution)/shard_map/ppermute | solution.py:349
  76.4 2.1 %collective-permute-done.7.refs_1_ = bf16[144,512]{1,0:T(8,128)(2,1)S(1)} collective-permute-done((bf16[144,512]{1,0:T(8,128)(2,1)S(1)}, bf16[144,512]{1,0:T(8,128)(2,1)S(1)}, u32[]{:S(2)}, u32[]{:S(2)}) %collective-permute-start.7) | collective-permute-done | bytes 147488 | tf_op jit(solution)/shard_map/ppermute | solution.py:349
  78.5 4.2 %collective-permute-done.8.refs_2_ = bf16[144,512]{1,0:T(8,128)(2,1)S(1)} collective-permute-done((bf16[144,512]{1,0:T(8,128)(2,1)S(1)}, bf16[144,512]{1,0:T(8,128)(2,1)S(1)}, u32[]{:S(2)}, u32[]{:S(2)}) %collective-permute-start.8) | collective-permute-done | bytes 147488 | tf_op jit(solution)/shard_map/ppermute | solution.py:349
  85.2 3.2 %collective-permute-start.10 = (bf16[128,4224]{1,0:T(8,128)(2,1)S(1)}, bf16[128,4224]{1,0:T(8,128)(2,1)S(1)}, u32[]{:S(2)}, u32[]{:S(2)}) collective-permute-start(bf16[128,4224]{1,0:T(8,128)(2,1)S(1)} %bitcast.6), channel_id=1, source_target_pairs={{0,1},{1,0},{2,3},{3,2},{4,5},{5,4},{6,7},{7,6},{8,9},{9,8},{10,11... | collective-permute-start | bytes 3244040 | tf_op jit(solution)/shard_map/ppermute | solution.py:337
  90.3 2.4 %collective-permute-start.15 = (bf16[128,1024]{1,0:T(8,128)(2,1)S(1)}, bf16[128,1024]{1,0:T(8,128)(2,1)S(1)}, u32[]{:S(2)}, u32[]{:S(2)}) collective-permute-start(bf16[128,1024]{1,0:T(8,128)(2,1)S(1)} %get-tuple-element.79), channel_id=1, source_target_pairs={{0,64},{32,96},{64,0},{96,32},{1,65},{33,97},{65,1},{97,33},{2,66}... | collective-permute-start | bytes 786440 | tf_op jit(solution)/shard_map/ppermute | solution.py:349
  92.9 4.9 %shard_map.103.refs_6_.refs_0_ = bf16[144,512]{1,0:T(8,128)(2,1)S(1)} custom-call(bf16[128,4224]{1,0:T(8,128)(2,1)S(1)} %bitcast.8, bf16[128,4224]{1,0:T(8,128)(2,1)S(1)} %collective-permute-done.10.e.e_other, bf16[128,128]{1,0:T(8,128)(2,1)S(1)} %get-tuple-element.52.mask, f32[2,512]{1,0:T(2,128)S(1)} %get-tuple-element.59.norm_row, f32[128,512]{1,0:T(8,128)} %copy-done.2, ...), custom_call_target="tpu_custom_call" | custom-call | flops 1073741824 | bytes 10485760 | tf_op jit(solution)/shard_map/pallas_call | solution.py:34
  99.8 1.9 %collective-permute-start.13 = (bf16[144,512]{1,0:T(8,128)(2,1)S(1)}, bf16[144,512]{1,0:T(8,128)(2,1)S(1)}, u32[]{:S(2)}, u32[]{:S(2)}) collective-permute-start(bf16[144,512]{1,0:T(8,128)(2,1)S(1)} %shard_map.103.refs_6_.refs_0_), channel_id=1, source_target_pairs={{0,96},{32,0},{64,32},{96,64},{1,97},{33,1},{65,33},{97,65},{2,98}... | collective-permute-start | bytes 442376 | tf_op jit(solution)/shard_map/ppermute | solution.py:349
  101.8 3.0 %shard_map.104 = (bf16[2,1024,512]{2,1,0:T(8,128)(2,1)S(1)}, bf16[512,512]{1,0:T(8,128)(2,1)S(1)}, f32[512,1]{1,0:T(8,128)S(1)}, f32[1,1]{1,0:T(1,128)}, bf16[512,2048]{1,0:T(8,128)(2,1)S(1)}) custom-call(bf16[128,1024]{1,0:T(8,128)(2,1)S(1)} %get-tuple-element.51.home_own, bf16[128,1024]{1,0:T(8,128)(2,1)S(1)} %copy-done.1, ...), custom_call_target="tpu_custom_call" | custom-call | bytes 6291456 | tf_op jit(solution)/shard_map/pallas_call | solution.py:34
  104.8 3.6 %collective-permute-done.11.refs_1_ = bf16[144,512]{1,0:T(8,128)(2,1)S(1)} collective-permute-done((bf16[144,512]{1,0:T(8,128)(2,1)S(1)}, bf16[144,512]{1,0:T(8,128)(2,1)S(1)}, u32[]{:S(2)}, u32[]{:S(2)}) %collective-permute-start.11) | collective-permute-done | bytes 147488 | tf_op jit(solution)/shard_map/ppermute | solution.py:349
  108.5 2.7 %collective-permute-done.12.refs_2_ = bf16[144,512]{1,0:T(8,128)(2,1)S(1)} collective-permute-done((bf16[144,512]{1,0:T(8,128)(2,1)S(1)}, bf16[144,512]{1,0:T(8,128)(2,1)S(1)}, u32[]{:S(2)}, u32[]{:S(2)}) %collective-permute-start.12) | collective-permute-done | bytes 147488 | tf_op jit(solution)/shard_map/ppermute | solution.py:349
  113.2 2.7 %shard_map.107 = bf16[2,1024,512]{2,1,0:T(8,128)(2,1)} custom-call(bf16[2,1024,512]{2,1,0:T(8,128)(2,1)S(1)} %get-tuple-element.76.xt, f32[1,1]{1,0:T(1,128)} %get-tuple-element.77.refs_7_.count, bf16[512,512]{1,0:T(8,128)(2,1)S(1)} %get-tuple-element.81.ds), custom_call_target="tpu_custom_call" | custom-call | flops 2147483648 | bytes 5242880 | tf_op jit(solution)/shard_map/pallas_call | solution.py:34
  115.9 3.4 %shard_map.108 = bf16[512,2048]{1,0:T(8,128)(2,1)} custom-call(bf16[128,4224]{1,0:T(8,128)(2,1)S(1)} %bitcast.9, bf16[128,4224]{1,0:T(8,128)(2,1)S(1)} %collective-permute-done.10.e.e_other, bf16[384,1024]{1,0:T(8,128)(2,1)S(1)} %get-tuple-element.82.own, bf16[384,1024]{1,0:T(8,128)(2,1)S(1)} %collective-permute-done.17.other, ...), custom_call_target="tpu_custom_call" | custom-call | flops 2147483648 | bytes 7340032 | tf_op jit(solution)/shard_map/pallas_call | solution.py:34
  (51 shorter events, 19.8 us)
Async XLA Ops:
  2.4 2.4 %collective-permute-start = (bf16[4,8320]{1,0:T(4,128)(2,1)S(1)}, bf16[4,8320]{1,0:T(4,128)(2,1)S(1)}, u32[]{:S(2)}, u32[]{:S(2)}) collective-permute-start(bf16[4,8320]{1,0:T(4,128)(2,1)S(1)} %get-tuple-element.46), channel_id=1, source_target_pairs={{0,1},{1,0},{2,3},{3,2},{4,5},{5,4},{6,7},{7,6},{8,9},{9,8},{10,11... | collective-permute-start | bytes 199688 | tf_op jit(solution)/shard_map/ppermute | solution.py:337
  5.8 22.9 %all-to-all-start = ((bf16[16,8,4224]{2,1,0:T(8,128)(2,1)}), bf16[16,8,4224]{2,1,0:T(8,128)(2,1)S(1)}, u32[]{:S(2)}, u32[]{:S(2)}) async-start(bf16[16,8,4224]{2,1,0:T(8,128)(2,1)} %get-tuple-element.47), calls=%async_computation | async-start | bytes 2162688 | tf_op jit(solution)/shard_map/all_to_all | solution.py:341
  28.7 7.3 %collective-permute-start.1 = (bf16[128,4224]{1,0:T(8,128)(2,1)S(1)}, bf16[128,4224]{1,0:T(8,128)(2,1)S(1)}, u32[]{:S(2)}, u32[]{:S(2)}) collective-permute-start(bf16[128,4224]{1,0:T(8,128)(2,1)S(1)} %bitcast.10), channel_id=1, source_target_pairs={{0,1},{1,0},{2,3},{3,2},{4,5},{5,4},{6,7},{7,6},{8,9},{9,8},{10,11... | collective-permute-start | bytes 3244040 | tf_op jit(solution)/shard_map/ppermute | solution.py:337
  39.1 2.7 %collective-permute-start.2 = (bf16[128,4096]{1,0:T(8,128)(2,1)S(1)}, bf16[128,4096]{1,0:T(8,128)(2,1)S(1)}, u32[]{:S(2)}, u32[]{:S(2)}) collective-permute-start(bf16[128,4096]{1,0:T(8,128)(2,1)S(1)} %get-tuple-element.57), channel_id=1, source_target_pairs={{0,1},{1,0},{2,3},{3,2},{4,5},{5,4},{6,7},{7,6},{8,9},{9,8},{10,11... | collective-permute-start | bytes 3145736 | tf_op jit(solution)/shard_map/ppermute | solution.py:337
  43.0 20.0 %copy-start.7 = (f32[2,4096]{1,0:T(2,128)S(1)}, f32[2,4096]{1,0:T(2,128)}, u32[]{:S(2)}) copy-start(f32[2,4096]{1,0:T(2,128)} %bias.1) | copy-start | bytes 98308
  43.0 20.0 %all-to-all-start.1 = ((bf16[16,8,4096]{2,1,0:T(8,128)(2,1)}), bf16[16,8,4096]{2,1,0:T(8,128)(2,1)S(1)}, u32[]{:S(2)}, u32[]{:S(2)}) async-start(bf16[16,8,4096]{2,1,0:T(8,128)(2,1)} %bitcast.3), calls=%async_computation.1 | async-start | bytes 2097152 | tf_op jit(solution)/shard_map/all_to_all | solution.py:341
  46.8 17.5 %collective-permute-start.3 = (bf16[128,1024]{1,0:T(8,128)(2,1)}, bf16[128,1024]{1,0:T(8,128)(2,1)S(1)}, u32[]{:S(2)}, u32[]{:S(2)}) collective-permute-start(bf16[128,1024]{1,0:T(8,128)(2,1)} %get-tuple-element.60), channel_id=1, source_target_pairs={{0,32},{32,64},{64,96},{96,0},{1,33},{33,65},{65,97},{97,1},{2,34}... | collective-permute-start | bytes 786440 | tf_op jit(solution)/shard_map/ppermute | solution.py:349
  48.5 15.8 %collective-permute-start.4 = (bf16[128,1024]{1,0:T(8,128)(2,1)S(1)}, bf16[128,1024]{1,0:T(8,128)(2,1)S(1)}, u32[]{:S(2)}, u32[]{:S(2)}) collective-permute-start(bf16[128,1024]{1,0:T(8,128)(2,1)S(1)} %get-tuple-element.61), channel_id=1, source_target_pairs={{0,64},{32,96},{64,0},{96,32},{1,65},{33,97},{65,1},{97,33},{2,66}... | collective-permute-start | bytes 786440 | tf_op jit(solution)/shard_map/ppermute | solution.py:349
  51.8 12.5 %collective-permute-start.5 = (bf16[128,1024]{1,0:T(8,128)(2,1)S(1)}, bf16[128,1024]{1,0:T(8,128)(2,1)S(1)}, u32[]{:S(2)}, u32[]{:S(2)}) collective-permute-start(bf16[128,1024]{1,0:T(8,128)(2,1)S(1)} %get-tuple-element.62), channel_id=1, source_target_pairs={{0,96},{32,0},{64,32},{96,64},{1,97},{33,1},{65,33},{97,65},{2,98}... | collective-permute-start | bytes 786440 | tf_op jit(solution)/shard_map/ppermute | solution.py:349
  64.3 20.9 %all-to-all-start.2 = ((bf16[16,8,4224]{2,1,0:T(8,128)(2,1)}), bf16[16,8,4224]{2,1,0:T(8,128)(2,1)S(1)}, u32[]{:S(2)}, u32[]{:S(2)}) async-start(bf16[16,8,4224]{2,1,0:T(8,128)(2,1)} %shard_map.101), calls=%async_computation.2 | async-start | bytes 2162688 | tf_op jit(solution)/shard_map/all_to_all | solution.py:341
  69.9 14.1 %collective-permute-start.6 = (bf16[384,1024]{1,0:T(8,128)(2,1)S(1)}, bf16[384,1024]{1,0:T(8,128)(2,1)S(1)}, u32[]{:S(2)}, u32[]{:S(2)}) collective-permute-start(bf16[384,1024]{1,0:T(8,128)(2,1)S(1)} %shard_map.102.own), channel_id=1, source_target_pairs={{0,1},{1,0},{2,3},{3,2},{4,5},{5,4},{6,7},{7,6},{8,9},{9,8},{10,11... | collective-permute-start | bytes 2359304 | tf_op jit(solution)/shard_map/ppermute | solution.py:337
  71.9 6.6 %collective-permute-start.7 = (bf16[144,512]{1,0:T(8,128)(2,1)S(1)}, bf16[144,512]{1,0:T(8,128)(2,1)S(1)}, u32[]{:S(2)}, u32[]{:S(2)}) collective-permute-start(bf16[144,512]{1,0:T(8,128)(2,1)S(1)} %get-tuple-element.69.feats.refs_0_), channel_id=1, source_target_pairs={{0,32},{32,64},{64,96},{96,0},{1,33},{33,65},{65,97},{97,1},{2,34}... | collective-permute-start | bytes 442376 | tf_op jit(solution)/shard_map/ppermute | solution.py:349
  72.6 10.1 %collective-permute-start.8 = (bf16[144,512]{1,0:T(8,128)(2,1)S(1)}, bf16[144,512]{1,0:T(8,128)(2,1)S(1)}, u32[]{:S(2)}, u32[]{:S(2)}) collective-permute-start(bf16[144,512]{1,0:T(8,128)(2,1)S(1)} %get-tuple-element.69.feats.refs_0_), channel_id=1, source_target_pairs={{0,64},{32,96},{64,0},{96,32},{1,65},{33,97},{65,1},{97,33},{2,66}... | collective-permute-start | bytes 442376 | tf_op jit(solution)/shard_map/ppermute | solution.py:349
  75.6 7.8 %collective-permute-start.9 = (bf16[144,512]{1,0:T(8,128)(2,1)S(1)}, bf16[144,512]{1,0:T(8,128)(2,1)S(1)}, u32[]{:S(2)}, u32[]{:S(2)}) collective-permute-start(bf16[144,512]{1,0:T(8,128)(2,1)S(1)} %get-tuple-element.69.feats.refs_0_), channel_id=1, source_target_pairs={{0,96},{32,0},{64,32},{96,64},{1,97},{33,1},{65,33},{97,65},{2,98}... | collective-permute-start | bytes 442376 | tf_op jit(solution)/shard_map/ppermute | solution.py:349
  85.2 7.7 %collective-permute-start.10 = (bf16[128,4224]{1,0:T(8,128)(2,1)S(1)}, bf16[128,4224]{1,0:T(8,128)(2,1)S(1)}, u32[]{:S(2)}, u32[]{:S(2)}) collective-permute-start(bf16[128,4224]{1,0:T(8,128)(2,1)S(1)} %bitcast.6), channel_id=1, source_target_pairs={{0,1},{1,0},{2,3},{3,2},{4,5},{5,4},{6,7},{7,6},{8,9},{9,8},{10,11... | collective-permute-start | bytes 3244040 | tf_op jit(solution)/shard_map/ppermute | solution.py:337
  88.5 11.4 %collective-permute-start.14 = (bf16[128,1024]{1,0:T(8,128)(2,1)S(1)}, bf16[128,1024]{1,0:T(8,128)(2,1)S(1)}, u32[]{:S(2)}, u32[]{:S(2)}) collective-permute-start(bf16[128,1024]{1,0:T(8,128)(2,1)S(1)} %get-tuple-element.78), channel_id=1, source_target_pairs={{0,32},{32,64},{64,96},{96,0},{1,33},{33,65},{65,97},{97,1},{2,34}... | collective-permute-start | bytes 786440 | tf_op jit(solution)/shard_map/ppermute | solution.py:349
  90.3 14.5 %collective-permute-start.15 = (bf16[128,1024]{1,0:T(8,128)(2,1)S(1)}, bf16[128,1024]{1,0:T(8,128)(2,1)S(1)}, u32[]{:S(2)}, u32[]{:S(2)}) collective-permute-start(bf16[128,1024]{1,0:T(8,128)(2,1)S(1)} %get-tuple-element.79), channel_id=1, source_target_pairs={{0,64},{32,96},{64,0},{96,32},{1,65},{33,97},{65,1},{97,33},{2,66}... | collective-permute-start | bytes 786440 | tf_op jit(solution)/shard_map/ppermute | solution.py:349
  92.7 12.1 %collective-permute-start.16 = (bf16[128,1024]{1,0:T(8,128)(2,1)S(1)}, bf16[128,1024]{1,0:T(8,128)(2,1)S(1)}, u32[]{:S(2)}, u32[]{:S(2)}) collective-permute-start(bf16[128,1024]{1,0:T(8,128)(2,1)S(1)} %get-tuple-element.80), channel_id=1, source_target_pairs={{0,96},{32,0},{64,32},{96,64},{1,97},{33,1},{65,33},{97,65},{2,98}... | collective-permute-start | bytes 786440 | tf_op jit(solution)/shard_map/ppermute | solution.py:349
  92.9 8.9 %copy-start.4 = (bf16[144,512]{1,0:T(8,128)(2,1)S(1)}, bf16[144,512]{1,0:T(8,128)(2,1)}, u32[]{:S(2)}) copy-start(bf16[144,512]{1,0:T(8,128)(2,1)} %copy-done.3) | copy-start | bytes 442372
  92.9 8.9 %copy-start.6 = (bf16[144,512]{1,0:T(8,128)(2,1)S(1)}, bf16[144,512]{1,0:T(8,128)(2,1)}, u32[]{:S(2)}) copy-start(bf16[144,512]{1,0:T(8,128)(2,1)} %copy-done.5) | copy-start | bytes 442372
  97.8 10.7 %collective-permute-start.11 = (bf16[144,512]{1,0:T(8,128)(2,1)S(1)}, bf16[144,512]{1,0:T(8,128)(2,1)S(1)}, u32[]{:S(2)}, u32[]{:S(2)}) collective-permute-start(bf16[144,512]{1,0:T(8,128)(2,1)S(1)} %shard_map.103.refs_6_.refs_0_), channel_id=1, source_target_pairs={{0,32},{32,64},{64,96},{96,0},{1,33},{33,65},{65,97},{97,1},{2,34}... | collective-permute-start | bytes 442376 | tf_op jit(solution)/shard_map/ppermute | solution.py:349
  99.1 12.0 %collective-permute-start.12 = (bf16[144,512]{1,0:T(8,128)(2,1)S(1)}, bf16[144,512]{1,0:T(8,128)(2,1)S(1)}, u32[]{:S(2)}, u32[]{:S(2)}) collective-permute-start(bf16[144,512]{1,0:T(8,128)(2,1)S(1)} %shard_map.103.refs_6_.refs_0_), channel_id=1, source_target_pairs={{0,64},{32,96},{64,0},{96,32},{1,65},{33,97},{65,1},{97,33},{2,66}... | collective-permute-start | bytes 442376 | tf_op jit(solution)/shard_map/ppermute | solution.py:349
  99.8 11.3 %collective-permute-start.13 = (bf16[144,512]{1,0:T(8,128)(2,1)S(1)}, bf16[144,512]{1,0:T(8,128)(2,1)S(1)}, u32[]{:S(2)}, u32[]{:S(2)}) collective-permute-start(bf16[144,512]{1,0:T(8,128)(2,1)S(1)} %shard_map.103.refs_6_.refs_0_), channel_id=1, source_target_pairs={{0,96},{32,0},{64,32},{96,64},{1,97},{33,1},{65,33},{97,65},{2,98}... | collective-permute-start | bytes 442376 | tf_op jit(solution)/shard_map/ppermute | solution.py:349
  112.4 3.5 %collective-permute-start.17 = (bf16[384,1024]{1,0:T(8,128)(2,1)S(1)}, bf16[384,1024]{1,0:T(8,128)(2,1)S(1)}, u32[]{:S(2)}, u32[]{:S(2)}) collective-permute-start(bf16[384,1024]{1,0:T(8,128)(2,1)S(1)} %get-tuple-element.82.own), channel_id=1, source_target_pairs={{0,1},{1,0},{2,3},{3,2},{4,5},{5,4},{6,7},{7,6},{8,9},{9,8},{10,11... | collective-permute-start | bytes 2359304 | tf_op jit(solution)/shard_map/ppermute | solution.py:337
  (6 other events, 23.0 us)

commit v4 on v3

--- a/solution.py
+++ b/solution.py
@@ -30,13 +30,14 @@
     return pltpu.with_memory_space_constraint(v, pltpu.HBM)
 
 
-def call(body, outs, args, specs=None, scratch=(), vmem=None, flops=0, nbytes=0, out_specs=None):
+def call(body, outs, args, specs=None, scratch=(), vmem=None, flops=0, nbytes=0, out_specs=None, aliases=None):
     return pl.pallas_call(
         body,
         out_shape=[o[2](o[0], o[1]) if len(o) == 3 else jax.ShapeDtypeStruct(*o) for o in outs],
         in_specs=specs or [VM] * len(args),
         out_specs=out_specs or [VM] * len(outs),
         scratch_shapes=list(scratch),
+        input_output_aliases=aliases or {},
         compiler_params=pltpu.CompilerParams(vmem_limit_bytes=vmem or 16 * MIB),
         cost_estimate=pl.CostEstimate(flops=flops, bytes_accessed=nbytes, transcendentals=0),
     )(*args)
@@ -137,14 +138,15 @@
     return copies
 
 
-def encode_own_kernel(x, w_enc, acc, rest, mask, home, p1, p2, p3, buf, sems):
+def encode_own_kernel(x, w_enc, acc, rest, mask, home, p1, p2, p3, buf, sems, out_sems):
     z, c = lax.axis_index("z"), lax.axis_index("c")
     copies = fetch_enc(w_enc, c, buf, sems)
     later = fetch_enc(w_enc, 1 - c, rest, sems, 4)
+    for k, out in enumerate((home, p1, p2, p3)):
+        piece = x.at[:, lanes(lax.rem(z + k, NZ) * SUB, SUB)]
+        later.append(pltpu.make_async_copy(piece, out, out_sems.at[k]))
+        later[-1].start()
     mask[...] = x[:, HALF:]
-    home[...] = x[:, lanes(z * SUB, SUB)]
-    for k, out in enumerate((p1, p2, p3)):
-        out[...] = x[:, lanes(lax.rem(z + k + 1, NZ) * SUB, SUB)]
     for i in range(0, 4, 2):
         copies[i].wait()
         copies[i + 1].wait()
@@ -156,10 +158,11 @@
         copy.wait()
 
 
-def encode_kernel(x, mask, part, bias, w_enc, w_dec, act_out, feats_out, send, home, dec, dec_sems):
+def encode_kernel(x, mask, part, bias, w_enc, w_dec, act_hbm, feats_out, send, home, act_out, dec, dec_sems, out_sems):
     z, c = lax.axis_index("z"), lax.axis_index("c")
     dec_copies = fetch_dec(w_dec, 1 - c, dec, dec_sems)
-    home[...] = x[:, lanes(z * SUB, SUB)]
+    later = [pltpu.make_async_copy(x.at[:, lanes(z * SUB, SUB)], home, out_sems.at[0])]
+    later[0].start()
     live = mask[:, 0:1].astype(f32)
     count = jnp.sum(live, axis=0, keepdims=True)
     for n in range(0, LOCAL, 256):
@@ -169,15 +172,19 @@
         act_out[:, n : n + 256] = act
         feats_out[:ROWS, n : n + 256] = feats.astype(bf16)
         fsum = jnp.sum(feats * live, axis=0, keepdims=True)
-        tail = jnp.zeros((16, 256), f32)
-        row = lax.broadcasted_iota(jnp.int32, (16, 256), 0)
+        tail = jnp.zeros((8, 256), f32)
+        row = lax.broadcasted_iota(jnp.int32, (8, 256), 0)
         for i, piece in enumerate((*split3(fsum), jnp.broadcast_to(count, (1, 256)))):
             tail = jnp.where(row == i, piece.astype(f32), tail)
         feats_out[ROWS:, n : n + 256] = tail.astype(bf16)
+    later.append(pltpu.make_async_copy(act_out, act_hbm, out_sems.at[1]))
+    later[1].start()
     feats16 = feats_out[:ROWS, :]
     for q in range(NZ):
         dec_copies[q].wait()
         send[:, q * SUB : (q + 1) * SUB] = jnp.dot(feats16, dec[q], preferred_element_type=f32).astype(bf16)
+    for copy in later:
+        copy.wait()
 
 
 def decode_own_kernel(feats, w_dec, part, buf, sems):
@@ -211,15 +218,22 @@
     fetch.wait()
 
 
-def add_kernel(own, other, out):
-    for n in range(0, HALF, SUB):
-        out[:, n : n + SUB] = (own[:, n : n + SUB] + other[:, n : n + SUB].astype(f32)).astype(bf16)
-
-
-def err_kernel(parts, mine, bias, feats, norm_row, out):
+def add_kernel(own, other, out, total, sems):
+    copies = []
+    for i in range(4):
+        rows = slice(i * 32, (i + 1) * 32)
+        total[rows, :] = (own[rows, :] + other[rows, :].astype(f32)).astype(bf16)
+        copies.append(pltpu.make_async_copy(total.at[pl.ds(i * 32, 32)], out.at[pl.ds(i * 32, 32)], sems.at[i]))
+        copies[-1].start()
+    for copy in copies:
+        copy.wait()
+
+
+def err_kernel(parts, mine, bias, feats, norm_row, out_hbm, out, sems):
     c = lax.axis_index("c")
     live = mine[:, HALF : HALF + 1].astype(f32)
     square = jnp.zeros((8, SUB), f32)
+    copies = []
     for q in range(NZ):
         cols = slice(q * SUB, (q + 1) * SUB)
         total = parts[0, :, cols].astype(f32)
@@ -231,6 +245,9 @@
         err16 = err.astype(bf16)
         for i in range(CHIPS):
             out[i, :, cols] = err16
+        piece = pl.ds(q * SUB, SUB)
+        copies.append(pltpu.make_async_copy(out.at[:, :, piece], out_hbm.at[:, :, piece], sems.at[q]))
+        copies[-1].start()
     squares = jnp.sum(jnp.sum(square, axis=0, keepdims=True), axis=1, keepdims=True)
     fsum = jnp.sum(feats[ROWS : ROWS + 3, :].astype(f32), axis=0, keepdims=True)
     nsum = norm_row[0:1, :] + norm_row[1:2, :]
@@ -242,6 +259,11 @@
         tail = jnp.where((lane == i) & (row == 0), piece.astype(f32), tail)
     for i in range(CHIPS):
         out[i, :, HALF:] = tail.astype(bf16)
+    piece = pl.ds(HALF, PAD)
+    copies.append(pltpu.make_async_copy(out.at[:, :, piece], out_hbm.at[:, :, piece], sems.at[NZ]))
+    copies[-1].start()
+    for copy in copies:
+        copy.wait()
 
 
 def slice_kernel(e, s1, s2, s3):
@@ -257,8 +279,8 @@
     fetch.start()
     both = e[:, HALF:].astype(f32) + own[:, HALF:].astype(f32)
     both = jnp.sum(jnp.sum(both, axis=0, keepdims=True), axis=1, keepdims=True)
-    lane = lax.broadcasted_iota(jnp.int32, (16, LOCAL), 1)
-    tail = jnp.zeros((16, LOCAL), f32)
+    lane = lax.broadcasted_iota(jnp.int32, (8, LOCAL), 1)
+    tail = jnp.zeros((8, LOCAL), f32)
     for i, piece in enumerate(split3(both)):
         tail = jnp.where(lane == i, piece.astype(f32), tail)
     out[ROWS:, :] = tail.astype(bf16)
@@ -299,7 +321,23 @@
     loss[...] = total / (count[...] * WIDTH)
 
 
-def grad_enc_kernel(xt, count, ds, out, done, sems):
+def dec_half(side, plane, rest, ft, scale, w, factor, done, rows):
+    z = lax.axis_index("z")
+    for m in range(0, SUB, 512):
+        part = jnp.dot(ft[rows, :ROWS], plane[:, lanes(z * SUB + m, 512)], preferred_element_type=f32)
+        part = part + jnp.dot(ft[rows, ROWS:], rest[:, m : m + 512], preferred_element_type=f32)
+        part = part * (2.0 * factor) + (scale[rows, :] * factor) * w[rows, lanes(side * SUB + m, 512)].astype(f32)
+        done[rows, m : m + 512] = part.astype(bf16)
+
+
+def copy_dec(side, done, out, sem, rows):
+    copy = pltpu.make_async_copy(done.at[rows], out.at[rows, lanes(side * SUB, SUB)], sem)
+    copy.start()
+    return copy
+
+
+def grads_kernel(xt, count, ds, e_own, own, ft, scale, w, out_enc, out_dec, done, done_dec, sems):
+    c = lax.axis_index("c")
     factor = loss_scale / count[...]
     copies = []
     for i in range(4):
@@ -308,27 +346,25 @@
             at = i % 2 * 512 + n
             part = jnp.dot(xt[i // 2, at : at + 256, :], ds[...], preferred_element_type=f32)
             done[i // 2, at : at + 256, :] = (part * factor).astype(bf16)
-        copies.append(pltpu.make_async_copy(done.at[i // 2, rows], out.at[i // 2, rows], sems.at[i]))
+        copies.append(pltpu.make_async_copy(done.at[i // 2, rows], out_enc.at[i // 2, rows], sems.at[i]))
         copies[-1].start()
-    for copy in copies:
-        copy.wait()
-
-
-def grad_dec_kernel(e_own, e_other, own, other, ft, scale, count, w, out, es, done, sems):
-    z, c = lax.axis_index("z"), lax.axis_index("c")
+    for i in range(2):
+        for n in range(i * 256, i * 256 + 256, 128):
+            dec_half(c, e_own, own, ft, scale, w, factor, done_dec, pl.ds(n, 128))
+        copies.append(copy_dec(c, done_dec, out_dec, sems.at[4 + i], pl.ds(i * 256, 256)))
+    for copy in copies:
+        copy.wait()
+
+
+def rest_kernel(e_other, other, ft, scale, count, w, half, out, done, sems):
+    del half
+    side = 1 - lax.axis_index("c")
     factor = loss_scale / count[...]
-    for side, plane, rest in ((c, e_own, own), (1 - c, e_other, other)):
-        es[:ROWS, lanes(side * SUB, SUB)] = plane[:, lanes(z * SUB, SUB)]
-        es[ROWS:, lanes(side * SUB, SUB)] = rest[...]
     copies = []
-    for i, n in enumerate(range(0, LOCAL, 128)):
-        for m in range(0, 2 * SUB, 512):
-            part = 2.0 * jnp.dot(ft[n : n + 128, :], es[:, m : m + 512], preferred_element_type=f32)
-            part = part + scale[n : n + 128, :] * w[n : n + 128, m : m + 512].astype(f32)
-            done[n : n + 128, m : m + 512] = (part * factor).astype(bf16)
-        piece = pl.ds(n, 128)
-        copies.append(pltpu.make_async_copy(done.at[piece], out.at[piece], sems.at[i]))
-        copies[-1].start()
+    for i in range(2):
+        for n in range(i * 256, i * 256 + 256, 128):
+            dec_half(side, e_other, other, ft, scale, w, factor, done, pl.ds(n, 128))
+        copies.append(copy_dec(side, done, out, sems.at[i], pl.ds(i * 256, 256)))
     for copy in copies:
         copy.wait()
 
@@ -373,33 +409,31 @@
         (keep, swap(send)),
         vmem=4 * MIB,
     )
-    norm_row, norm_col = call(
-        norm_kernel,
-        [((2, LOCAL), f32), ((LOCAL, 2), f32)],
-        (w_dec,),
-        [hbm],
-        [pltpu.VMEM((LOCAL, WIDTH), bf16), pltpu.SemaphoreType.DMA((4,))],
-        flops=4 * LOCAL * WIDTH,
-        nbytes=8 * MIB,
-    )
-    x_own, norm_row, norm_col = lax.optimization_barrier((chips(block), norm_row, norm_col))
-    x_own = x_own.reshape(ROWS, HALF + PAD)
+    x_own = chips(block).reshape(ROWS, HALF + PAD)
     x_other = swap(x_own)
     acc, w_rest, mask, home_own, *xs = call(
         encode_own_kernel,
-        [((ROWS, LOCAL), f32), ((HALF, LOCAL), bf16, pltpu.VMEM), ((ROWS, PAD), bf16)] + [((ROWS, SUB), bf16)] * 4,
+        [((ROWS, LOCAL), f32), ((HALF, LOCAL), bf16, pltpu.VMEM), ((ROWS, PAD), bf16)]
+        + [((ROWS, SUB), bf16, pltpu.HBM)] * 4,
         (x_own, w_enc),
         [VM, hbm],
-        [pltpu.VMEM((HALF, LOCAL), bf16), pltpu.SemaphoreType.DMA((8,))],
+        [pltpu.VMEM((HALF, LOCAL), bf16), pltpu.SemaphoreType.DMA((8,)), pltpu.SemaphoreType.DMA((4,))],
+        out_specs=[VM] * 3 + [hbm] * 4,
         flops=half_flops,
         nbytes=10 * MIB,
     )
     act, feats, part_send, home_other = call(
         encode_kernel,
-        [((ROWS, LOCAL), f32), ((ROWS + 16, LOCAL), bf16), ((ROWS, HALF), bf16), ((ROWS, SUB), bf16)],
+        [
+            ((ROWS, LOCAL), f32, pltpu.HBM),
+            ((ROWS + 8, LOCAL), bf16),
+            ((ROWS, HALF), bf16),
+            ((ROWS, SUB), bf16, pltpu.HBM),
+        ],
         (x_other, mask, acc, b_enc.reshape(1, LOCAL), w_rest, w_dec),
         [VM] * 5 + [hbm],
-        dec_scratch,
+        [pltpu.VMEM((ROWS, LOCAL), f32), *dec_scratch, pltpu.SemaphoreType.DMA((2,))],
+        out_specs=[hbm, VM, VM, hbm],
         flops=2 * half_flops,
         nbytes=8 * MIB,
     )
@@ -413,13 +447,31 @@
         flops=half_flops,
         nbytes=6 * MIB,
     )
-    (part,) = call(add_kernel, [((ROWS, HALF), bf16)], (part_own, part_recv), vmem=8 * MIB)
-    parts = chips(part.reshape(CHIPS, 8, HALF))
+    (part,) = call(
+        add_kernel,
+        [((ROWS, HALF), bf16, pltpu.HBM)],
+        (part_own, part_recv),
+        scratch=[pltpu.VMEM((ROWS, HALF), bf16), pltpu.SemaphoreType.DMA((4,))],
+        out_specs=[hbm],
+        vmem=8 * MIB,
+    )
+    norm_row, norm_col = call(
+        norm_kernel,
+        [((2, LOCAL), f32), ((LOCAL, 2), f32)],
+        (w_dec,),
+        [hbm],
+        [pltpu.VMEM((LOCAL, WIDTH), bf16), pltpu.SemaphoreType.DMA((4,))],
+        flops=4 * LOCAL * WIDTH,
+        nbytes=8 * MIB,
+    )
+    parts, norm_row, norm_col = lax.optimization_barrier((chips(part.reshape(CHIPS, 8, HALF)), norm_row, norm_col))
     xs = [shift(xs[k - 1], k) for k in range(1, NZ)]
     (block,) = call(
         err_kernel,
-        [((CHIPS, 8, HALF + PAD), bf16)],
+        [((CHIPS, 8, HALF + PAD), bf16, pltpu.HBM)],
         (parts, mine, b_dec, feats, norm_row),
+        scratch=[pltpu.VMEM((CHIPS, 8, HALF + PAD), bf16), pltpu.SemaphoreType.DMA((NZ + 1,))],
+        out_specs=[hbm],
     )
     block, *xs = lax.optimization_barrier((block, *xs))
     (xs,) = call(merge_kernel, [((3 * ROWS, SUB), bf16)], xs, nbytes=2 * MIB)
@@ -431,7 +483,7 @@
     es = [shift(slices[k - 1], k) for k in range(1, NZ)]
     (dpre,) = call(
         dpre_kernel,
-        [((ROWS + 16, LOCAL), bf16)],
+        [((ROWS + 8, LOCAL), bf16)],
         (e_own, e_other, mask, norm_row, at_hbm(act), w_dec),
         [VM] * 4 + [hbm] * 2,
         [
@@ -464,27 +516,29 @@
         (*ds, *es, count),
         nbytes=3 * MIB,
     )
-    (grad_enc,) = call(
-        grad_enc_kernel,
-        [((2, SUB, LOCAL), bf16)],
-        (xt, count, ds),
-        scratch=[pltpu.VMEM((2, SUB, LOCAL), bf16), pltpu.SemaphoreType.DMA((4,))],
+    grad_enc, half = call(
+        grads_kernel,
+        [((2, SUB, LOCAL), bf16), ((LOCAL, 2 * SUB), bf16)],
+        (xt, count, ds, e_own, es, ft, scale, w_slice),
+        scratch=[
+            pltpu.VMEM((2, SUB, LOCAL), bf16),
+            pltpu.VMEM((LOCAL, SUB), bf16),
+            pltpu.SemaphoreType.DMA((6,)),
+        ],
+        out_specs=[hbm, hbm],
+        flops=6 * half_flops,
+        nbytes=8 * MIB,
+    )
+    (grad_dec,) = call(
+        rest_kernel,
+        [((LOCAL, 2 * SUB), bf16)],
+        (e_other, swap(es), ft, scale, count, w_slice, half),
+        [VM] * 6 + [hbm],
+        [pltpu.VMEM((LOCAL, SUB), bf16), pltpu.SemaphoreType.DMA((2,))],
         out_specs=[hbm],
-        flops=4 * half_flops,
-        nbytes=5 * MIB,
-    )
-    (grad_dec,) = call(
-        grad_dec_kernel,
-        [((LOCAL, 2 * SUB), bf16)],
-        (e_own, e_other, es, swap(es), ft, scale, count, w_slice),
-        scratch=[
-            pltpu.VMEM((NZ * ROWS, 2 * SUB), bf16),
-            pltpu.VMEM((LOCAL, 2 * SUB), bf16),
-            pltpu.SemaphoreType.DMA((4,)),
-        ],
-        out_specs=[hbm],
-        flops=4 * half_flops,
-        nbytes=7 * MIB,
+        aliases={6: 0},
+        flops=2 * half_flops,
+        nbytes=3 * MIB,
     )
     return grad_enc, grad_dec, loss.reshape(())
 

time: 120 us -> 118 us (0.983)
  blocking collectives: 0 us -> 23.7 us
  waiting for transfers between devices: 36.3 us -> 23.8 us
  starting transfers between devices: 45.5 us -> 34.8 us
  local copies, waits for them, and re-layouts: 1.35 us -> 0.03 us
    all_to_all x0 -> x1, blocking collectives: none -> 23.7 us  [chips(): lax.all_to_all(v, ('x', 'y'), split_axis=0, concat_axis=0, tiled=True)]
    all_to_all x3 -> x2, waiting for transfers between devices: 22.6 us -> 6.43 us  [chips(): lax.all_to_all(v, ('x', 'y'), split_axis=0, concat_axis=0, tiled=True)]
    all_to_all x3 -> x2, starting transfers between devices: 16.2 us -> 9.28 us  [chips(): lax.all_to_all(v, ('x', 'y'), split_axis=0, concat_axis=0, tiled=True)]
    ppermute x12, waiting for transfers between devices: 12.7 us -> 16.3 us  [shift(): return lax.ppermute(v, 'z', [(i, (i + k) % NZ) for i in range(NZ)])]
    ppermute x6, starting transfers between devices: 10.6 us -> 8.67 us  [swap(): return lax.ppermute(v, 'c', [(0, 1), (1, 0)])]
    ppermute x12, starting transfers between devices: 18.7 us -> 16.8 us  [shift(): return lax.ppermute(v, 'z', [(i, (i + k) % NZ) for i in range(NZ)])]
    unnamed x18 -> x14, local copies, waits for them, and re-layouts: 1.35 us -> 0.03 us
  transfers between devices with their start and end apart: 21 -> 20, of which waited for: 8 -> 11; matrix products, arithmetic and copies ran while one was open for 0% -> 0% of each run, Pallas kernels for 20% -> 21%
where the time goes in v4:
time: 118 us
  starting transfers between devices  34.8 us (29%)
  Pallas kernels  33.6 us (28%)
  waiting for transfers between devices  23.8 us (20%)
  blocking collectives  23.7 us (20%)
  between operations  1.66 us (1%)
    pallas_call x15, Pallas kernels, call(): pl.pallas_call(body, out_shape=[o[2](o[0], o[1]) if len(o) == 3 else jax....  33.6 us
    all_to_all x1, blocking collectives, chips(): lax.all_to_all(v, ('x', 'y'), split_axis=0, concat_axis=0, tiled=True)  23.7 us
    ppermute x12, starting transfers between devices, shift(): return lax.ppermute(v, 'z', [(i, (i + k) % NZ) for i in range(NZ)])  16.8 us
    ppermute x12, waiting for transfers between devices, shift(): return lax.ppermute(v, 'z', [(i, (i + k) % NZ) for i in range(NZ)])  16.3 us
    all_to_all x2, starting transfers between devices, chips(): lax.all_to_all(v, ('x', 'y'), split_axis=0, concat_axis=0, tiled=True)  9.28 us
    ppermute x6, starting transfers between devices, swap(): return lax.ppermute(v, 'c', [(0, 1), (1, 0)])  8.67 us
    all_to_all x2, waiting for transfers between devices, chips(): lax.all_to_all(v, ('x', 'y'), split_axis=0, concat_axis=0, tiled=True)  6.43 us
  transfers between devices with their start and end apart: 20, of which 11 were waited for; matrix products, arithmetic and copies ran while one was open for 0% of the time, Pallas kernels for 21%

profile of v4, /device:TPU:1, one launch (start us, length us, event | category | flops | bytes accessed | tf_op | source)
XLA Modules:
  0.0 117.6 jit_solution(16714595041063847398)
XLA Ops:
  4.9 23.7 %all_to_all.15 = bf16[16,8,4224]{2,1,0:T(8,128)(2,1)S(1)} all-to-all(bf16[16,8,4224]{2,1,0:T(8,128)(2,1)S(1)} %get-tuple-element.49), channel_id=1, replica_groups=mesh['z'=4,'x'=4,'y'=4,'c'=2] {'x','y'}, dimensions={0} | all-to-all | bytes 2162688 | tf_op jit(solution)/shard_map/all_to_all | solution.py:377
  30.1 3.9 %shard_map.96 = (f32[128,512]{1,0:T(8,128)S(1)}, bf16[4096,512]{1,0:T(8,128)(2,1)S(1)}, bf16[128,128]{1,0:T(8,128)(2,1)S(1)}, bf16[128,1024]{1,0:T(8,128)(2,1)},...) custom-call(bf16[128,4224]{1,0:T(8,128)(2,1)S(1)} %bitcast.11, ...), custom_call_target="tpu_custom_call" | custom-call | flops 536870912 | bytes 10485760 | tf_op jit(solution)/shard_map/pallas_call | solution.py:34
  34.0 3.3 %shard_map.97 = (f32[128,512]{1,0:T(8,128)}, bf16[136,512]{1,0:T(8,128)(2,1)S(1)}, bf16[128,4096]{1,0:T(8,128)(2,1)S(1)}, bf16[128,1024]{1,0:T(8,128)(2,1)}) custom-call(bf16[128,4224]{1,0:T(8,128)(2,1)S(1)} %collective-permute-done.1.x, bf16[128,128]{1,0:T(8,128)(2,1)S(1)} %get-tuple-element.51.mask, f32[128,512]{1,0:T(8,128)S(1)} %get-tuple-element.52.part, ...), custom_call_target="tpu_custom_call" | custom-call | flops 1073741824 | bytes 8388608 | tf_op jit(solution)/shard_map/pallas_call | solution.py:34
  37.4 2.5 %shard_map.98.own = f32[128,4096]{1,0:T(8,128)S(1)} custom-call(bf16[136,512]{1,0:T(8,128)(2,1)S(1)} %get-tuple-element.71.feats.refs_0_, bf16[512,8192]{1,0:T(8,128)(2,1)} %refs_5_.1), custom_call_target="tpu_custom_call" | custom-call | flops 536870912 | bytes 6291456 | tf_op jit(solution)/shard_map/pallas_call | solution.py:34
  41.1 3.8 %all-to-all-start.1 = ((bf16[16,8,4096]{2,1,0:T(8,128)(2,1)}), bf16[16,8,4096]{2,1,0:T(8,128)(2,1)S(1)}, u32[]{:S(2)}, u32[]{:S(2)}) async-start(bf16[16,8,4096]{2,1,0:T(8,128)(2,1)} %bitcast.13), calls=%async_computation.1 | async-start | bytes 2097152 | tf_op jit(solution)/shard_map/all_to_all | solution.py:377
  44.9 1.7 %collective-permute-start.3 = (bf16[128,1024]{1,0:T(8,128)(2,1)S(1)}, bf16[128,1024]{1,0:T(8,128)(2,1)S(1)}, u32[]{:S(2)}, u32[]{:S(2)}) collective-permute-start(bf16[128,1024]{1,0:T(8,128)(2,1)S(1)} %copy-done.6), channel_id=1, source_target_pairs={{0,32},{32,64},{64,96},{96,0},{1,33},{33,65},{65,97},{97,1},{2,34}... | collective-permute-start | bytes 786440 | tf_op jit(solution)/shard_map/ppermute | solution.py:385
  46.6 3.3 %collective-permute-start.4 = (bf16[128,1024]{1,0:T(8,128)(2,1)S(1)}, bf16[128,1024]{1,0:T(8,128)(2,1)S(1)}, u32[]{:S(2)}, u32[]{:S(2)}) collective-permute-start(bf16[128,1024]{1,0:T(8,128)(2,1)S(1)} %copy-done.5), channel_id=1, source_target_pairs={{0,64},{32,96},{64,0},{96,32},{1,65},{33,97},{65,1},{97,33},{2,66}... | collective-permute-start | bytes 786440 | tf_op jit(solution)/shard_map/ppermute | solution.py:385
  50.7 5.0 %shard_map.100 = (f32[2,512]{1,0:T(2,128)S(1)}, f32[512,2]{1,0:T(8,128)S(1)}) custom-call(bf16[512,8192]{1,0:T(8,128)(2,1)} %refs_5_.1), custom_call_target="tpu_custom_call" | custom-call | flops 16777216 | bytes 8388608 | tf_op jit(solution)/shard_map/pallas_call | solution.py:34
  55.7 5.5 %all-to-all-done.1.parts = bf16[16,8,4096]{2,1,0:T(8,128)(2,1)S(1)} async-done(((bf16[16,8,4096]{2,1,0:T(8,128)(2,1)}), bf16[16,8,4096]{2,1,0:T(8,128)(2,1)S(1)}, u32[]{:S(2)}, u32[]{:S(2)}) %all-to-all-start.1) | async-done | bytes 1048608 | tf_op jit(solution)/shard_map/all_to_all | solution.py:377
  62.4 5.5 %all-to-all-start.2 = ((bf16[16,8,4224]{2,1,0:T(8,128)(2,1)}), bf16[16,8,4224]{2,1,0:T(8,128)(2,1)S(1)}, u32[]{:S(2)}, u32[]{:S(2)}) async-start(bf16[16,8,4224]{2,1,0:T(8,128)(2,1)} %shard_map.101), calls=%async_computation.2 | async-start | bytes 2162688 | tf_op jit(solution)/shard_map/all_to_all | solution.py:377
  67.9 1.9 %collective-permute-start.6 = (bf16[384,1024]{1,0:T(8,128)(2,1)S(1)}, bf16[384,1024]{1,0:T(8,128)(2,1)S(1)}, u32[]{:S(2)}, u32[]{:S(2)}) collective-permute-start(bf16[384,1024]{1,0:T(8,128)(2,1)S(1)} %shard_map.102.own), channel_id=1, source_target_pairs={{0,1},{1,0},{2,3},{3,2},{4,5},{5,4},{6,7},{7,6},{8,9},{9,8},{10,11... | collective-permute-start | bytes 2359304 | tf_op jit(solution)/shard_map/ppermute | solution.py:373
  69.8 2.6 %collective-permute-start.9 = (bf16[136,512]{1,0:T(8,128)(2,1)S(1)}, bf16[136,512]{1,0:T(8,128)(2,1)S(1)}, u32[]{:S(2)}, u32[]{:S(2)}) collective-permute-start(bf16[136,512]{1,0:T(8,128)(2,1)S(1)} %get-tuple-element.71.feats.refs_0_), channel_id=1, source_target_pairs={{0,96},{32,0},{64,32},{96,64},{1,97},{33,1},{65,33},{97,65},{2,98}... | collective-permute-start | bytes 417800 | tf_op jit(solution)/shard_map/ppermute | solution.py:385
  73.1 5.2 %collective-permute-done.9.refs_3_ = bf16[136,512]{1,0:T(8,128)(2,1)S(1)} collective-permute-done((bf16[136,512]{1,0:T(8,128)(2,1)S(1)}, bf16[136,512]{1,0:T(8,128)(2,1)S(1)}, u32[]{:S(2)}, u32[]{:S(2)}) %collective-permute-start.9) | collective-permute-done | bytes 139296 | tf_op jit(solution)/shard_map/ppermute | solution.py:385
  78.9 3.5 %collective-permute-done.7.refs_1_ = bf16[136,512]{1,0:T(8,128)(2,1)S(1)} collective-permute-done((bf16[136,512]{1,0:T(8,128)(2,1)S(1)}, bf16[136,512]{1,0:T(8,128)(2,1)S(1)}, u32[]{:S(2)}, u32[]{:S(2)}) %collective-permute-start.7) | collective-permute-done | bytes 139296 | tf_op jit(solution)/shard_map/ppermute | solution.py:385
  83.2 3.2 %collective-permute-start.10 = (bf16[128,4224]{1,0:T(8,128)(2,1)S(1)}, bf16[128,4224]{1,0:T(8,128)(2,1)S(1)}, u32[]{:S(2)}, u32[]{:S(2)}) collective-permute-start(bf16[128,4224]{1,0:T(8,128)(2,1)S(1)} %bitcast.6), channel_id=1, source_target_pairs={{0,1},{1,0},{2,3},{3,2},{4,5},{5,4},{6,7},{7,6},{8,9},{9,8},{10,11... | collective-permute-start | bytes 3244040 | tf_op jit(solution)/shard_map/ppermute | solution.py:373
  86.5 2.1 %collective-permute-start.14 = (bf16[128,1024]{1,0:T(8,128)(2,1)S(1)}, bf16[128,1024]{1,0:T(8,128)(2,1)S(1)}, u32[]{:S(2)}, u32[]{:S(2)}) collective-permute-start(bf16[128,1024]{1,0:T(8,128)(2,1)S(1)} %get-tuple-element.80), channel_id=1, source_target_pairs={{0,32},{32,64},{64,96},{96,0},{1,33},{33,65},{65,97},{97,1},{2,34}... | collective-permute-start | bytes 786440 | tf_op jit(solution)/shard_map/ppermute | solution.py:385
  88.6 2.4 %collective-permute-start.15 = (bf16[128,1024]{1,0:T(8,128)(2,1)S(1)}, bf16[128,1024]{1,0:T(8,128)(2,1)S(1)}, u32[]{:S(2)}, u32[]{:S(2)}) collective-permute-start(bf16[128,1024]{1,0:T(8,128)(2,1)S(1)} %get-tuple-element.81), channel_id=1, source_target_pairs={{0,64},{32,96},{64,0},{96,32},{1,65},{33,97},{65,1},{97,33},{2,66}... | collective-permute-start | bytes 786440 | tf_op jit(solution)/shard_map/ppermute | solution.py:385
  91.1 4.9 %shard_map.103.refs_6_.refs_0_ = bf16[136,512]{1,0:T(8,128)(2,1)S(1)} custom-call(bf16[128,4224]{1,0:T(8,128)(2,1)S(1)} %bitcast.8, bf16[128,4224]{1,0:T(8,128)(2,1)S(1)} %collective-permute-done.10.e.e_other, bf16[128,128]{1,0:T(8,128)(2,1)S(1)} %get-tuple-element.51.mask, f32[2,512]{1,0:T(2,128)S(1)} %get-tuple-element.61.norm_row, ...), custom_call_target="tpu_custom_call" | custom-call | flops 1073741824 | bytes 10485760 | tf_op jit(solution)/shard_map/pallas_call | solution.py:34
  96.9 2.2 %collective-permute-start.12 = (bf16[136,512]{1,0:T(8,128)(2,1)S(1)}, bf16[136,512]{1,0:T(8,128)(2,1)S(1)}, u32[]{:S(2)}, u32[]{:S(2)}) collective-permute-start(bf16[136,512]{1,0:T(8,128)(2,1)S(1)} %shard_map.103.refs_6_.refs_0_), channel_id=1, source_target_pairs={{0,64},{32,96},{64,0},{96,32},{1,65},{33,97},{65,1},{97,33},{2,66}... | collective-permute-start | bytes 417800 | tf_op jit(solution)/shard_map/ppermute | solution.py:385
  99.2 3.0 %shard_map.104 = (bf16[2,1024,512]{2,1,0:T(8,128)(2,1)S(1)}, bf16[512,512]{1,0:T(8,128)(2,1)S(1)}, f32[512,1]{1,0:T(8,128)S(1)}, f32[1,1]{1,0:T(1,128)}, bf16[512,2048]{1,0:T(8,128)(2,1)S(1)}) custom-call(bf16[128,1024]{1,0:T(8,128)(2,1)S(1)} %copy-done, bf16[128,1024]{1,0:T(8,128)(2,1)S(1)} %copy-done.1, bf16[384,1024]{1,0:T(8,128)(2,1)S(1)} %shard_map.102.own, ...), custom_call_target="tpu_custom_call" | custom-call | bytes 6291456 | tf_op jit(solution)/shard_map/pallas_call | solution.py:34
  103.1 2.5 %collective-permute-done.13.refs_3_ = bf16[136,512]{1,0:T(8,128)(2,1)S(1)} collective-permute-done((bf16[136,512]{1,0:T(8,128)(2,1)S(1)}, bf16[136,512]{1,0:T(8,128)(2,1)S(1)}, u32[]{:S(2)}, u32[]{:S(2)}) %collective-permute-start.13) | collective-permute-done | bytes 139296 | tf_op jit(solution)/shard_map/ppermute | solution.py:385
  106.1 3.2 %collective-permute-done.11.refs_1_ = bf16[136,512]{1,0:T(8,128)(2,1)S(1)} collective-permute-done((bf16[136,512]{1,0:T(8,128)(2,1)S(1)}, bf16[136,512]{1,0:T(8,128)(2,1)S(1)}, u32[]{:S(2)}, u32[]{:S(2)}) %collective-permute-start.11) | collective-permute-done | bytes 139296 | tf_op jit(solution)/shard_map/ppermute | solution.py:385
  111.1 3.7 %shard_map.107 = (bf16[2,1024,512]{2,1,0:T(8,128)(2,1)}, bf16[512,2048]{1,0:T(8,128)(2,1)}) custom-call(bf16[2,1024,512]{2,1,0:T(8,128)(2,1)S(1)} %get-tuple-element.78.xt, f32[1,1]{1,0:T(1,128)} %get-tuple-element.79.refs_7_.count, bf16[512,512]{1,0:T(8,128)(2,1)S(1)} %get-tuple-element.83.ds, bf16[128,4224]{1,0:T(8,128)(2,1)S(1)} %bitcast.9, ...), custom_call_target="tpu_custom_call" | custom-call | flops 3221225472 | bytes 8388608 | tf_op jit(solution)/shard_map/pallas_call | solution.py:34
  114.8 2.6 %shard_map.108 = bf16[512,2048]{1,0:T(8,128)(2,1)} custom-call(bf16[128,4224]{1,0:T(8,128)(2,1)S(1)} %collective-permute-done.10.e.e_other, bf16[384,1024]{1,0:T(8,128)(2,1)S(1)} %collective-permute-done.17.other, bf16[512,512]{1,0:T(8,128)(2,1)S(1)} %get-tuple-element.85.ft, f32[512,1]{1,0:T(8,128)S(1)} %get-tuple-element.86.scale, ...), custom_call_target="tpu_custom_call", output_to_operand_aliasing={{}: (6, {})} | custom-call | flops 1073741824 | bytes 3145728 | tf_op jit(solution)/shard_map/pallas_call | solution.py:34
  (46 shorter events, 14.7 us)
Async XLA Ops:
  2.4 2.4 %collective-permute-start = (bf16[4,8320]{1,0:T(4,128)(2,1)S(1)}, bf16[4,8320]{1,0:T(4,128)(2,1)S(1)}, u32[]{:S(2)}, u32[]{:S(2)}) collective-permute-start(bf16[4,8320]{1,0:T(4,128)(2,1)S(1)} %get-tuple-element.48), channel_id=1, source_target_pairs={{0,1},{1,0},{2,3},{3,2},{4,5},{5,4},{6,7},{7,6},{8,9},{9,8},{10,11... | collective-permute-start | bytes 199688 | tf_op jit(solution)/shard_map/ppermute | solution.py:373
  28.6 5.4 %collective-permute-start.1 = (bf16[128,4224]{1,0:T(8,128)(2,1)S(1)}, bf16[128,4224]{1,0:T(8,128)(2,1)S(1)}, u32[]{:S(2)}, u32[]{:S(2)}) collective-permute-start(bf16[128,4224]{1,0:T(8,128)(2,1)S(1)} %bitcast.10), channel_id=1, source_target_pairs={{0,1},{1,0},{2,3},{3,2},{4,5},{5,4},{6,7},{7,6},{8,9},{9,8},{10,11... | collective-permute-start | bytes 3244040 | tf_op jit(solution)/shard_map/ppermute | solution.py:373
  37.3 2.7 %collective-permute-start.2 = (bf16[128,4096]{1,0:T(8,128)(2,1)S(1)}, bf16[128,4096]{1,0:T(8,128)(2,1)S(1)}, u32[]{:S(2)}, u32[]{:S(2)}) collective-permute-start(bf16[128,4096]{1,0:T(8,128)(2,1)S(1)} %get-tuple-element.56), channel_id=1, source_target_pairs={{0,1},{1,0},{2,3},{3,2},{4,5},{5,4},{6,7},{7,6},{8,9},{9,8},{10,11... | collective-permute-start | bytes 3145736 | tf_op jit(solution)/shard_map/ppermute | solution.py:373
  41.1 8.8 %copy-start.4 = (bf16[128,1024]{1,0:T(8,128)(2,1)S(1)}, bf16[128,1024]{1,0:T(8,128)(2,1)}, u32[]{:S(2)}) copy-start(bf16[128,1024]{1,0:T(8,128)(2,1)} %get-tuple-element.64) | copy-start | bytes 786436
  41.1 20.1 %all-to-all-start.1 = ((bf16[16,8,4096]{2,1,0:T(8,128)(2,1)}), bf16[16,8,4096]{2,1,0:T(8,128)(2,1)S(1)}, u32[]{:S(2)}, u32[]{:S(2)}) async-start(bf16[16,8,4096]{2,1,0:T(8,128)(2,1)} %bitcast.13), calls=%async_computation.1 | async-start | bytes 2097152 | tf_op jit(solution)/shard_map/all_to_all | solution.py:377
  44.9 17.4 %collective-permute-start.3 = (bf16[128,1024]{1,0:T(8,128)(2,1)S(1)}, bf16[128,1024]{1,0:T(8,128)(2,1)S(1)}, u32[]{:S(2)}, u32[]{:S(2)}) collective-permute-start(bf16[128,1024]{1,0:T(8,128)(2,1)S(1)} %copy-done.6), channel_id=1, source_target_pairs={{0,32},{32,64},{64,96},{96,0},{1,33},{33,65},{65,97},{97,1},{2,34}... | collective-permute-start | bytes 786440 | tf_op jit(solution)/shard_map/ppermute | solution.py:385
  46.6 15.7 %collective-permute-start.4 = (bf16[128,1024]{1,0:T(8,128)(2,1)S(1)}, bf16[128,1024]{1,0:T(8,128)(2,1)S(1)}, u32[]{:S(2)}, u32[]{:S(2)}) collective-permute-start(bf16[128,1024]{1,0:T(8,128)(2,1)S(1)} %copy-done.5), channel_id=1, source_target_pairs={{0,64},{32,96},{64,0},{96,32},{1,65},{33,97},{65,1},{97,33},{2,66}... | collective-permute-start | bytes 786440 | tf_op jit(solution)/shard_map/ppermute | solution.py:385
  50.0 11.3 %copy-start.2 = (f32[2,4096]{1,0:T(2,128)S(1)}, f32[2,4096]{1,0:T(2,128)}, u32[]{:S(2)}) copy-start(f32[2,4096]{1,0:T(2,128)} %bias.1) | copy-start | bytes 98308
  50.0 12.4 %collective-permute-start.5 = (bf16[128,1024]{1,0:T(8,128)(2,1)S(1)}, bf16[128,1024]{1,0:T(8,128)(2,1)S(1)}, u32[]{:S(2)}, u32[]{:S(2)}) collective-permute-start(bf16[128,1024]{1,0:T(8,128)(2,1)S(1)} %copy-done.4), channel_id=1, source_target_pairs={{0,96},{32,0},{64,32},{96,64},{1,97},{33,1},{65,33},{97,65},{2,98}... | collective-permute-start | bytes 786440 | tf_op jit(solution)/shard_map/ppermute | solution.py:385
  62.4 20.8 %all-to-all-start.2 = ((bf16[16,8,4224]{2,1,0:T(8,128)(2,1)}), bf16[16,8,4224]{2,1,0:T(8,128)(2,1)S(1)}, u32[]{:S(2)}, u32[]{:S(2)}) async-start(bf16[16,8,4224]{2,1,0:T(8,128)(2,1)} %shard_map.101), calls=%async_computation.2 | async-start | bytes 2162688 | tf_op jit(solution)/shard_map/all_to_all | solution.py:377
  67.9 14.4 %collective-permute-start.6 = (bf16[384,1024]{1,0:T(8,128)(2,1)S(1)}, bf16[384,1024]{1,0:T(8,128)(2,1)S(1)}, u32[]{:S(2)}, u32[]{:S(2)}) collective-permute-start(bf16[384,1024]{1,0:T(8,128)(2,1)S(1)} %shard_map.102.own), channel_id=1, source_target_pairs={{0,1},{1,0},{2,3},{3,2},{4,5},{5,4},{6,7},{7,6},{8,9},{9,8},{10,11... | collective-permute-start | bytes 2359304 | tf_op jit(solution)/shard_map/ppermute | solution.py:373
  69.8 8.4 %collective-permute-start.9 = (bf16[136,512]{1,0:T(8,128)(2,1)S(1)}, bf16[136,512]{1,0:T(8,128)(2,1)S(1)}, u32[]{:S(2)}, u32[]{:S(2)}) collective-permute-start(bf16[136,512]{1,0:T(8,128)(2,1)S(1)} %get-tuple-element.71.feats.refs_0_), channel_id=1, source_target_pairs={{0,96},{32,0},{64,32},{96,64},{1,97},{33,1},{65,33},{97,65},{2,98}... | collective-permute-start | bytes 417800 | tf_op jit(solution)/shard_map/ppermute | solution.py:385
  72.4 6.5 %collective-permute-start.8 = (bf16[136,512]{1,0:T(8,128)(2,1)S(1)}, bf16[136,512]{1,0:T(8,128)(2,1)S(1)}, u32[]{:S(2)}, u32[]{:S(2)}) collective-permute-start(bf16[136,512]{1,0:T(8,128)(2,1)S(1)} %get-tuple-element.71.feats.refs_0_), channel_id=1, source_target_pairs={{0,64},{32,96},{64,0},{96,32},{1,65},{33,97},{65,1},{97,33},{2,66}... | collective-permute-start | bytes 417800 | tf_op jit(solution)/shard_map/ppermute | solution.py:385
  72.6 9.7 %collective-permute-start.7 = (bf16[136,512]{1,0:T(8,128)(2,1)S(1)}, bf16[136,512]{1,0:T(8,128)(2,1)S(1)}, u32[]{:S(2)}, u32[]{:S(2)}) collective-permute-start(bf16[136,512]{1,0:T(8,128)(2,1)S(1)} %get-tuple-element.71.feats.refs_0_), channel_id=1, source_target_pairs={{0,32},{32,64},{64,96},{96,0},{1,33},{33,65},{65,97},{97,1},{2,34}... | collective-permute-start | bytes 417800 | tf_op jit(solution)/shard_map/ppermute | solution.py:385
  83.2 7.8 %collective-permute-start.10 = (bf16[128,4224]{1,0:T(8,128)(2,1)S(1)}, bf16[128,4224]{1,0:T(8,128)(2,1)S(1)}, u32[]{:S(2)}, u32[]{:S(2)}) collective-permute-start(bf16[128,4224]{1,0:T(8,128)(2,1)S(1)} %bitcast.6), channel_id=1, source_target_pairs={{0,1},{1,0},{2,3},{3,2},{4,5},{5,4},{6,7},{7,6},{8,9},{9,8},{10,11... | collective-permute-start | bytes 3244040 | tf_op jit(solution)/shard_map/ppermute | solution.py:373
  86.5 12.7 %collective-permute-start.14 = (bf16[128,1024]{1,0:T(8,128)(2,1)S(1)}, bf16[128,1024]{1,0:T(8,128)(2,1)S(1)}, u32[]{:S(2)}, u32[]{:S(2)}) collective-permute-start(bf16[128,1024]{1,0:T(8,128)(2,1)S(1)} %get-tuple-element.80), channel_id=1, source_target_pairs={{0,32},{32,64},{64,96},{96,0},{1,33},{33,65},{65,97},{97,1},{2,34}... | collective-permute-start | bytes 786440 | tf_op jit(solution)/shard_map/ppermute | solution.py:385
  88.6 14.5 %collective-permute-start.15 = (bf16[128,1024]{1,0:T(8,128)(2,1)S(1)}, bf16[128,1024]{1,0:T(8,128)(2,1)S(1)}, u32[]{:S(2)}, u32[]{:S(2)}) collective-permute-start(bf16[128,1024]{1,0:T(8,128)(2,1)S(1)} %get-tuple-element.81), channel_id=1, source_target_pairs={{0,64},{32,96},{64,0},{96,32},{1,65},{33,97},{65,1},{97,33},{2,66}... | collective-permute-start | bytes 786440 | tf_op jit(solution)/shard_map/ppermute | solution.py:385
  91.0 12.1 %collective-permute-start.16 = (bf16[128,1024]{1,0:T(8,128)(2,1)S(1)}, bf16[128,1024]{1,0:T(8,128)(2,1)S(1)}, u32[]{:S(2)}, u32[]{:S(2)}) collective-permute-start(bf16[128,1024]{1,0:T(8,128)(2,1)S(1)} %get-tuple-element.82), channel_id=1, source_target_pairs={{0,96},{32,0},{64,32},{96,64},{1,97},{33,1},{65,33},{97,65},{2,98}... | collective-permute-start | bytes 786440 | tf_op jit(solution)/shard_map/ppermute | solution.py:385
  91.1 8.1 %copy-start = (bf16[128,1024]{1,0:T(8,128)(2,1)S(1)}, bf16[128,1024]{1,0:T(8,128)(2,1)}, u32[]{:S(2)}) copy-start(bf16[128,1024]{1,0:T(8,128)(2,1)} %get-tuple-element.50.home_own) | copy-start | bytes 786436
  91.1 8.1 %copy-start.1 = (bf16[128,1024]{1,0:T(8,128)(2,1)S(1)}, bf16[128,1024]{1,0:T(8,128)(2,1)}, u32[]{:S(2)}) copy-start(bf16[128,1024]{1,0:T(8,128)(2,1)} %get-tuple-element.54.home_other) | copy-start | bytes 786436
  95.9 9.7 %collective-permute-start.13 = (bf16[136,512]{1,0:T(8,128)(2,1)S(1)}, bf16[136,512]{1,0:T(8,128)(2,1)S(1)}, u32[]{:S(2)}, u32[]{:S(2)}) collective-permute-start(bf16[136,512]{1,0:T(8,128)(2,1)S(1)} %shard_map.103.refs_6_.refs_0_), channel_id=1, source_target_pairs={{0,96},{32,0},{64,32},{96,64},{1,97},{33,1},{65,33},{97,65},{2,98}... | collective-permute-start | bytes 417800 | tf_op jit(solution)/shard_map/ppermute | solution.py:385
  96.9 9.2 %collective-permute-start.12 = (bf16[136,512]{1,0:T(8,128)(2,1)S(1)}, bf16[136,512]{1,0:T(8,128)(2,1)S(1)}, u32[]{:S(2)}, u32[]{:S(2)}) collective-permute-start(bf16[136,512]{1,0:T(8,128)(2,1)S(1)} %shard_map.103.refs_6_.refs_0_), channel_id=1, source_target_pairs={{0,64},{32,96},{64,0},{96,32},{1,65},{33,97},{65,1},{97,33},{2,66}... | collective-permute-start | bytes 417800 | tf_op jit(solution)/shard_map/ppermute | solution.py:385
  99.2 10.2 %collective-permute-start.11 = (bf16[136,512]{1,0:T(8,128)(2,1)S(1)}, bf16[136,512]{1,0:T(8,128)(2,1)S(1)}, u32[]{:S(2)}, u32[]{:S(2)}) collective-permute-start(bf16[136,512]{1,0:T(8,128)(2,1)S(1)} %shard_map.103.refs_6_.refs_0_), channel_id=1, source_target_pairs={{0,32},{32,64},{64,96},{96,0},{1,33},{33,65},{65,97},{97,1},{2,34}... | collective-permute-start | bytes 417800 | tf_op jit(solution)/shard_map/ppermute | solution.py:385
  110.6 4.2 %collective-permute-start.17 = (bf16[384,1024]{1,0:T(8,128)(2,1)S(1)}, bf16[384,1024]{1,0:T(8,128)(2,1)S(1)}, u32[]{:S(2)}, u32[]{:S(2)}) collective-permute-start(bf16[384,1024]{1,0:T(8,128)(2,1)S(1)} %get-tuple-element.84.own), channel_id=1, source_target_pairs={{0,1},{1,0},{2,3},{3,2},{4,5},{5,4},{6,7},{7,6},{8,9},{9,8},{10,11... | collective-permute-start | bytes 2359304 | tf_op jit(solution)/shard_map/ppermute | solution.py:373
  (3 other events, 14.8 us)

commit v5 on v4

--- a/solution.py
+++ b/solution.py
@@ -211,7 +211,7 @@
         ft[:, k * ROWS : (k + 1) * ROWS] = feats[k][:ROWS, :].T
         fsum = fsum + jnp.sum(feats[k][ROWS : ROWS + 3, :].astype(f32), axis=0, keepdims=True)
         total = total + feats[k][ROWS + 3 : ROWS + 4, 0:1].astype(f32)
-    count[...] = total
+    count[...] = jnp.broadcast_to(total, (8, PAD))
     fsum = jnp.broadcast_to(fsum, (128, LOCAL)).T[:, 0:1]
     norm = jnp.where(z < 2, norm_col[:, 0:1], norm_col[:, 1:2])
     scale[...] = sparsity_weight * fsum / norm
@@ -311,47 +311,43 @@
 
 def part_kernel(*refs):
     pres, slices, count = refs[0:4], refs[4:7], refs[7]
-    es, ds, loss = refs[8:]
+    es, loss = refs[8:]
     total = jnp.zeros((1, 1), f32)
-    for k, p in enumerate(pres):
+    for p in pres:
         total = total + jnp.sum(p[ROWS : ROWS + 1, 0:3].astype(f32), axis=1, keepdims=True)
-        ds[k * ROWS : (k + 1) * ROWS, :] = p[:ROWS, :]
     for k, p in enumerate(slices):
         es[k * ROWS : (k + 1) * ROWS, :] = p[...]
-    loss[...] = total / (count[...] * WIDTH)
-
-
-def dec_half(side, plane, rest, ft, scale, w, factor, done, rows):
+    loss[...] = total / (count[0:1, 0:1] * WIDTH)
+
+
+def dec_half(side, plane, rest, ft, scale, w, factor, done, out, sems):
     z = lax.axis_index("z")
-    for m in range(0, SUB, 512):
-        part = jnp.dot(ft[rows, :ROWS], plane[:, lanes(z * SUB + m, 512)], preferred_element_type=f32)
-        part = part + jnp.dot(ft[rows, ROWS:], rest[:, m : m + 512], preferred_element_type=f32)
-        part = part * (2.0 * factor) + (scale[rows, :] * factor) * w[rows, lanes(side * SUB + m, 512)].astype(f32)
-        done[rows, m : m + 512] = part.astype(bf16)
-
-
-def copy_dec(side, done, out, sem, rows):
-    copy = pltpu.make_async_copy(done.at[rows], out.at[rows, lanes(side * SUB, SUB)], sem)
-    copy.start()
-    return copy
-
-
-def grads_kernel(xt, count, ds, e_own, own, ft, scale, w, out_enc, out_dec, done, done_dec, sems):
-    c = lax.axis_index("c")
-    factor = loss_scale / count[...]
+    copies = []
+    for i, m in enumerate(range(0, SUB, 512)):
+        cols = lanes(side * SUB + m, 512)
+        part = jnp.dot(ft[:, :ROWS], plane[:, lanes(z * SUB + m, 512)], preferred_element_type=f32)
+        part = part + jnp.dot(ft[:, ROWS:], rest[:, m : m + 512], preferred_element_type=f32)
+        part = part * (2.0 * factor) + (scale[...] * factor) * w[:, cols].astype(f32)
+        done[i] = part.astype(bf16)
+        copies.append(pltpu.make_async_copy(done.at[i], out.at[:, cols], sems[i]))
+        copies[-1].start()
+    return copies
+
+
+def grads_kernel(xt, count, p0, p1, p2, p3, e_own, own, ft, scale, w, out_enc, out_dec, ds, done, done_dec, sems):
+    for k, p in enumerate((p0, p1, p2, p3)):
+        ds[k * ROWS : (k + 1) * ROWS, :] = p[:ROWS, :]
+    factor = loss_scale / count[0:1, 0:1]
     copies = []
     for i in range(4):
         rows = pl.ds(i % 2 * 512, 512)
-        for n in range(0, 512, 256):
-            at = i % 2 * 512 + n
-            part = jnp.dot(xt[i // 2, at : at + 256, :], ds[...], preferred_element_type=f32)
-            done[i // 2, at : at + 256, :] = (part * factor).astype(bf16)
+        part = jnp.dot(xt[i // 2, rows, :], ds[...], preferred_element_type=f32)
+        done[i // 2, rows, :] = (part * factor).astype(bf16)
         copies.append(pltpu.make_async_copy(done.at[i // 2, rows], out_enc.at[i // 2, rows], sems.at[i]))
         copies[-1].start()
-    for i in range(2):
-        for n in range(i * 256, i * 256 + 256, 128):
-            dec_half(c, e_own, own, ft, scale, w, factor, done_dec, pl.ds(n, 128))
-        copies.append(copy_dec(c, done_dec, out_dec, sems.at[4 + i], pl.ds(i * 256, 256)))
+    copies += dec_half(
+        lax.axis_index("c"), e_own, own, ft, scale, w, factor, done_dec, out_dec, [sems.at[4], sems.at[5]]
+    )
     for copy in copies:
         copy.wait()
 
@@ -359,13 +355,8 @@
 def rest_kernel(e_other, other, ft, scale, count, w, half, out, done, sems):
     del half
     side = 1 - lax.axis_index("c")
-    factor = loss_scale / count[...]
-    copies = []
-    for i in range(2):
-        for n in range(i * 256, i * 256 + 256, 128):
-            dec_half(side, e_other, other, ft, scale, w, factor, done, pl.ds(n, 128))
-        copies.append(copy_dec(side, done, out, sems.at[i], pl.ds(i * 256, 256)))
-    for copy in copies:
+    factor = loss_scale / count[0:1, 0:1]
+    for copy in dec_half(side, e_other, other, ft, scale, w, factor, done, out, [sems.at[0], sems.at[1]]):
         copy.wait()
 
 
@@ -502,7 +493,7 @@
             ((2, SUB, NZ * ROWS), bf16),
             ((LOCAL, NZ * ROWS), bf16),
             ((LOCAL, 1), f32),
-            ((1, 1), f32),
+            ((8, PAD), f32, pltpu.VMEM),
             ((LOCAL, 2 * SUB), bf16),
         ],
         (home_own, home_other, xs, xs_other, *fs, norm_col, w_dec, dpre),
@@ -510,19 +501,20 @@
         [pltpu.SemaphoreType.DMA],
         nbytes=6 * MIB,
     )
-    es, ds, loss = call(
+    es, loss = call(
         part_kernel,
-        [((3 * ROWS, SUB), bf16), ((NZ * ROWS, LOCAL), bf16), ((1, 1), f32)],
+        [((3 * ROWS, SUB), bf16), ((1, 1), f32)],
         (*ds, *es, count),
         nbytes=3 * MIB,
     )
     grad_enc, half = call(
         grads_kernel,
         [((2, SUB, LOCAL), bf16), ((LOCAL, 2 * SUB), bf16)],
-        (xt, count, ds, e_own, es, ft, scale, w_slice),
+        (xt, count, *ds, e_own, es, ft, scale, w_slice),
         scratch=[
+            pltpu.VMEM((NZ * ROWS, LOCAL), bf16),
             pltpu.VMEM((2, SUB, LOCAL), bf16),
-            pltpu.VMEM((LOCAL, SUB), bf16),
+            pltpu.VMEM((2, LOCAL, 512), bf16),
             pltpu.SemaphoreType.DMA((6,)),
         ],
         out_specs=[hbm, hbm],
@@ -534,7 +526,7 @@
         [((LOCAL, 2 * SUB), bf16)],
         (e_other, swap(es), ft, scale, count, w_slice, half),
         [VM] * 6 + [hbm],
-        [pltpu.VMEM((LOCAL, SUB), bf16), pltpu.SemaphoreType.DMA((2,))],
+        [pltpu.VMEM((2, LOCAL, 512), bf16), pltpu.SemaphoreType.DMA((2,))],
         out_specs=[hbm],
         aliases={6: 0},
         flops=2 * half_flops,

time: 118 us -> 116 us (0.983)
  Pallas kernels: 33.6 us -> 30.8 us
    pallas_call x15, Pallas kernels: 33.6 us -> 30.8 us  [call(): pl.pallas_call(body, out_shape=[o[2](o[0], o[1]) if len(o) == 3 else jax....]
  transfers between devices with their start and end apart: 20 -> 20, of which waited for: 11 -> 11; matrix products, arithmetic and copies ran while one was open for 0% -> 0% of each run, Pallas kernels for 21% -> 20%
where the time goes in v5:
time: 116 us; the launch traced here: 115 us
  starting transfers between devices  34.8 us (30%)
  Pallas kernels  30.8 us (27%)
  waiting for transfers between devices  24.4 us (21%)
  blocking collectives  23.7 us (20%)
  between operations  1.66 us (1%)
    pallas_call x15, Pallas kernels, call(): pl.pallas_call(body, out_shape=[o[2](o[0], o[1]) if len(o) == 3 else jax....  30.8 us
    all_to_all x1, blocking collectives, chips(): lax.all_to_all(v, ('x', 'y'), split_axis=0, concat_axis=0, tiled=True)  23.7 us
    ppermute x12, waiting for transfers between devices, shift(): return lax.ppermute(v, 'z', [(i, (i + k) % NZ) for i in range(NZ)])  16.9 us
    ppermute x12, starting transfers between devices, shift(): return lax.ppermute(v, 'z', [(i, (i + k) % NZ) for i in range(NZ)])  16.8 us
    all_to_all x2, starting transfers between devices, chips(): lax.all_to_all(v, ('x', 'y'), split_axis=0, concat_axis=0, tiled=True)  9.28 us
    ppermute x6, starting transfers between devices, swap(): return lax.ppermute(v, 'c', [(0, 1), (1, 0)])  8.67 us
    all_to_all x2, waiting for transfers between devices, chips(): lax.all_to_all(v, ('x', 'y'), split_axis=0, concat_axis=0, tiled=True)  6.43 us
  transfers between devices with their start and end apart: 20, of which 11 were waited for; matrix products, arithmetic and copies ran while one was open for 0% of the time, Pallas kernels for 20%

profile of v5, /device:TPU:1, one launch (start us, length us, event | category | flops | bytes accessed | tf_op | source)
XLA Modules:
  0.0 115.4 jit_solution(6035346678211676216)
XLA Ops:
  4.9 23.7 %all_to_all.15 = bf16[16,8,4224]{2,1,0:T(8,128)(2,1)S(1)} all-to-all(bf16[16,8,4224]{2,1,0:T(8,128)(2,1)S(1)} %get-tuple-element.48), channel_id=1, replica_groups=mesh['z'=4,'x'=4,'y'=4,'c'=2] {'x','y'}, dimensions={0} | all-to-all | bytes 2162688 | tf_op jit(solution)/shard_map/all_to_all | solution.py:368
  30.1 3.9 %shard_map.96 = (f32[128,512]{1,0:T(8,128)S(1)}, bf16[4096,512]{1,0:T(8,128)(2,1)S(1)}, bf16[128,128]{1,0:T(8,128)(2,1)S(1)}, bf16[128,1024]{1,0:T(8,128)(2,1)},...) custom-call(bf16[128,4224]{1,0:T(8,128)(2,1)S(1)} %bitcast.11, ...), custom_call_target="tpu_custom_call" | custom-call | flops 536870912 | bytes 10485760 | tf_op jit(solution)/shard_map/pallas_call | solution.py:34
  34.0 3.3 %shard_map.97 = (f32[128,512]{1,0:T(8,128)}, bf16[136,512]{1,0:T(8,128)(2,1)S(1)}, bf16[128,4096]{1,0:T(8,128)(2,1)S(1)}, bf16[128,1024]{1,0:T(8,128)(2,1)}) custom-call(bf16[128,4224]{1,0:T(8,128)(2,1)S(1)} %collective-permute-done.1.x, bf16[128,128]{1,0:T(8,128)(2,1)S(1)} %get-tuple-element.50.mask, f32[128,512]{1,0:T(8,128)S(1)} %get-tuple-element.51.part, ...), custom_call_target="tpu_custom_call" | custom-call | flops 1073741824 | bytes 8388608 | tf_op jit(solution)/shard_map/pallas_call | solution.py:34
  37.4 2.5 %shard_map.98.own = f32[128,4096]{1,0:T(8,128)S(1)} custom-call(bf16[136,512]{1,0:T(8,128)(2,1)S(1)} %get-tuple-element.70.feats.refs_0_, bf16[512,8192]{1,0:T(8,128)(2,1)} %refs_5_.1), custom_call_target="tpu_custom_call" | custom-call | flops 536870912 | bytes 6291456 | tf_op jit(solution)/shard_map/pallas_call | solution.py:34
  41.1 3.8 %all-to-all-start.1 = ((bf16[16,8,4096]{2,1,0:T(8,128)(2,1)}), bf16[16,8,4096]{2,1,0:T(8,128)(2,1)S(1)}, u32[]{:S(2)}, u32[]{:S(2)}) async-start(bf16[16,8,4096]{2,1,0:T(8,128)(2,1)} %bitcast.13), calls=%async_computation.1 | async-start | bytes 2097152 | tf_op jit(solution)/shard_map/all_to_all | solution.py:368
  44.9 1.7 %collective-permute-start.3 = (bf16[128,1024]{1,0:T(8,128)(2,1)S(1)}, bf16[128,1024]{1,0:T(8,128)(2,1)S(1)}, u32[]{:S(2)}, u32[]{:S(2)}) collective-permute-start(bf16[128,1024]{1,0:T(8,128)(2,1)S(1)} %copy-done.6), channel_id=1, source_target_pairs={{0,32},{32,64},{64,96},{96,0},{1,33},{33,65},{65,97},{97,1},{2,34}... | collective-permute-start | bytes 786440 | tf_op jit(solution)/shard_map/ppermute | solution.py:376
  46.6 3.3 %collective-permute-start.4 = (bf16[128,1024]{1,0:T(8,128)(2,1)S(1)}, bf16[128,1024]{1,0:T(8,128)(2,1)S(1)}, u32[]{:S(2)}, u32[]{:S(2)}) collective-permute-start(bf16[128,1024]{1,0:T(8,128)(2,1)S(1)} %copy-done.5), channel_id=1, source_target_pairs={{0,64},{32,96},{64,0},{96,32},{1,65},{33,97},{65,1},{97,33},{2,66}... | collective-permute-start | bytes 786440 | tf_op jit(solution)/shard_map/ppermute | solution.py:376
  50.7 5.0 %shard_map.100 = (f32[2,512]{1,0:T(2,128)S(1)}, f32[512,2]{1,0:T(8,128)S(1)}) custom-call(bf16[512,8192]{1,0:T(8,128)(2,1)} %refs_5_.1), custom_call_target="tpu_custom_call" | custom-call | flops 16777216 | bytes 8388608 | tf_op jit(solution)/shard_map/pallas_call | solution.py:34
  55.7 5.5 %all-to-all-done.1.parts = bf16[16,8,4096]{2,1,0:T(8,128)(2,1)S(1)} async-done(((bf16[16,8,4096]{2,1,0:T(8,128)(2,1)}), bf16[16,8,4096]{2,1,0:T(8,128)(2,1)S(1)}, u32[]{:S(2)}, u32[]{:S(2)}) %all-to-all-start.1) | async-done | bytes 1048608 | tf_op jit(solution)/shard_map/all_to_all | solution.py:368
  62.4 5.5 %all-to-all-start.2 = ((bf16[16,8,4224]{2,1,0:T(8,128)(2,1)}), bf16[16,8,4224]{2,1,0:T(8,128)(2,1)S(1)}, u32[]{:S(2)}, u32[]{:S(2)}) async-start(bf16[16,8,4224]{2,1,0:T(8,128)(2,1)} %shard_map.101), calls=%async_computation.2 | async-start | bytes 2162688 | tf_op jit(solution)/shard_map/all_to_all | solution.py:368
  67.9 1.9 %collective-permute-start.6 = (bf16[384,1024]{1,0:T(8,128)(2,1)S(1)}, bf16[384,1024]{1,0:T(8,128)(2,1)S(1)}, u32[]{:S(2)}, u32[]{:S(2)}) collective-permute-start(bf16[384,1024]{1,0:T(8,128)(2,1)S(1)} %shard_map.102.own), channel_id=1, source_target_pairs={{0,1},{1,0},{2,3},{3,2},{4,5},{5,4},{6,7},{7,6},{8,9},{9,8},{10,11... | collective-permute-start | bytes 2359304 | tf_op jit(solution)/shard_map/ppermute | solution.py:364
  69.8 2.6 %collective-permute-start.9 = (bf16[136,512]{1,0:T(8,128)(2,1)S(1)}, bf16[136,512]{1,0:T(8,128)(2,1)S(1)}, u32[]{:S(2)}, u32[]{:S(2)}) collective-permute-start(bf16[136,512]{1,0:T(8,128)(2,1)S(1)} %get-tuple-element.70.feats.refs_0_), channel_id=1, source_target_pairs={{0,96},{32,0},{64,32},{96,64},{1,97},{33,1},{65,33},{97,65},{2,98}... | collective-permute-start | bytes 417800 | tf_op jit(solution)/shard_map/ppermute | solution.py:376
  73.1 5.2 %collective-permute-done.9.refs_3_ = bf16[136,512]{1,0:T(8,128)(2,1)S(1)} collective-permute-done((bf16[136,512]{1,0:T(8,128)(2,1)S(1)}, bf16[136,512]{1,0:T(8,128)(2,1)S(1)}, u32[]{:S(2)}, u32[]{:S(2)}) %collective-permute-start.9) | collective-permute-done | bytes 139296 | tf_op jit(solution)/shard_map/ppermute | solution.py:376
  78.9 3.5 %collective-permute-done.7.refs_1_ = bf16[136,512]{1,0:T(8,128)(2,1)S(1)} collective-permute-done((bf16[136,512]{1,0:T(8,128)(2,1)S(1)}, bf16[136,512]{1,0:T(8,128)(2,1)S(1)}, u32[]{:S(2)}, u32[]{:S(2)}) %collective-permute-start.7) | collective-permute-done | bytes 139296 | tf_op jit(solution)/shard_map/ppermute | solution.py:376
  83.2 3.2 %collective-permute-start.10 = (bf16[128,4224]{1,0:T(8,128)(2,1)S(1)}, bf16[128,4224]{1,0:T(8,128)(2,1)S(1)}, u32[]{:S(2)}, u32[]{:S(2)}) collective-permute-start(bf16[128,4224]{1,0:T(8,128)(2,1)S(1)} %bitcast.6), channel_id=1, source_target_pairs={{0,1},{1,0},{2,3},{3,2},{4,5},{5,4},{6,7},{7,6},{8,9},{9,8},{10,11... | collective-permute-start | bytes 3244040 | tf_op jit(solution)/shard_map/ppermute | solution.py:364
  86.5 2.1 %collective-permute-start.14 = (bf16[128,1024]{1,0:T(8,128)(2,1)S(1)}, bf16[128,1024]{1,0:T(8,128)(2,1)S(1)}, u32[]{:S(2)}, u32[]{:S(2)}) collective-permute-start(bf16[128,1024]{1,0:T(8,128)(2,1)S(1)} %get-tuple-element.79), channel_id=1, source_target_pairs={{0,32},{32,64},{64,96},{96,0},{1,33},{33,65},{65,97},{97,1},{2,34}... | collective-permute-start | bytes 786440 | tf_op jit(solution)/shard_map/ppermute | solution.py:376
  88.6 2.4 %collective-permute-start.15 = (bf16[128,1024]{1,0:T(8,128)(2,1)S(1)}, bf16[128,1024]{1,0:T(8,128)(2,1)S(1)}, u32[]{:S(2)}, u32[]{:S(2)}) collective-permute-start(bf16[128,1024]{1,0:T(8,128)(2,1)S(1)} %get-tuple-element.80), channel_id=1, source_target_pairs={{0,64},{32,96},{64,0},{96,32},{1,65},{33,97},{65,1},{97,33},{2,66}... | collective-permute-start | bytes 786440 | tf_op jit(solution)/shard_map/ppermute | solution.py:376
  91.1 4.9 %shard_map.103.refs_6_.refs_0_.p0 = bf16[136,512]{1,0:T(8,128)(2,1)S(1)} custom-call(bf16[128,4224]{1,0:T(8,128)(2,1)S(1)} %bitcast.8, bf16[128,4224]{1,0:T(8,128)(2,1)S(1)} %collective-permute-done.10.e.e_other, bf16[128,128]{1,0:T(8,128)(2,1)S(1)} %get-tuple-element.50.mask, f32[2,512]{1,0:T(2,128)S(1)} %get-tuple-element.60.norm_row, ...), custom_call_target="tpu_custom_call" | custom-call | flops 1073741824 | bytes 10485760 | tf_op jit(solution)/shard_map/pallas_call | solution.py:34
  96.9 2.2 %collective-permute-start.12 = (bf16[136,512]{1,0:T(8,128)(2,1)S(1)}, bf16[136,512]{1,0:T(8,128)(2,1)S(1)}, u32[]{:S(2)}, u32[]{:S(2)}) collective-permute-start(bf16[136,512]{1,0:T(8,128)(2,1)S(1)} %shard_map.103.refs_6_.refs_0_.p0), channel_id=1, source_target_pairs={{0,64},{32,96},{64,0},{96,32},{1,65},{33,97},{65,1},{97,33},{2,66}... | collective-permute-start | bytes 417800 | tf_op jit(solution)/shard_map/ppermute | solution.py:376
  99.2 2.4 %shard_map.104 = (bf16[2,1024,512]{2,1,0:T(8,128)(2,1)S(1)}, bf16[512,512]{1,0:T(8,128)(2,1)S(1)}, f32[512,1]{1,0:T(8,128)S(1)}, f32[8,128]{1,0:T(8,128)S(1)}, bf16[512,2048]{1,0:T(8,128)(2,1)S(1)}) custom-call(bf16[128,1024]{1,0:T(8,128)(2,1)S(1)} %copy-done, bf16[128,1024]{1,0:T(8,128)(2,1)S(1)} %copy-done.1, bf16[384,1024]{1,0:T(8,128)(2,1)S(1)} %shard_map.102.own, ...), custom_call_target="tpu_custom_call" | custom-call | bytes 6291456 | tf_op jit(solution)/shard_map/pallas_call | solution.py:34
  103.1 2.5 %collective-permute-done.13.refs_3_.p3 = bf16[136,512]{1,0:T(8,128)(2,1)S(1)} collective-permute-done((bf16[136,512]{1,0:T(8,128)(2,1)S(1)}, bf16[136,512]{1,0:T(8,128)(2,1)S(1)}, u32[]{:S(2)}, u32[]{:S(2)}) %collective-permute-start.13) | collective-permute-done | bytes 139296 | tf_op jit(solution)/shard_map/ppermute | solution.py:376
  106.1 3.2 %collective-permute-done.11.refs_1_.p1 = bf16[136,512]{1,0:T(8,128)(2,1)S(1)} collective-permute-done((bf16[136,512]{1,0:T(8,128)(2,1)S(1)}, bf16[136,512]{1,0:T(8,128)(2,1)S(1)}, u32[]{:S(2)}, u32[]{:S(2)}) %collective-permute-start.11) | collective-permute-done | bytes 139296 | tf_op jit(solution)/shard_map/ppermute | solution.py:376
  110.4 3.0 %shard_map.107 = (bf16[2,1024,512]{2,1,0:T(8,128)(2,1)}, bf16[512,2048]{1,0:T(8,128)(2,1)}) custom-call(bf16[2,1024,512]{2,1,0:T(8,128)(2,1)S(1)} %get-tuple-element.77.xt, f32[8,128]{1,0:T(8,128)S(1)} %get-tuple-element.78.refs_7_.count, bf16[136,512]{1,0:T(8,128)(2,1)S(1)} %shard_map.103.refs_6_.refs_0_.p0, ...), custom_call_target="tpu_custom_call" | custom-call | flops 3221225472 | bytes 8388608 | tf_op jit(solution)/shard_map/pallas_call | solution.py:34
  113.4 1.8 %shard_map.108 = bf16[512,2048]{1,0:T(8,128)(2,1)} custom-call(bf16[128,4224]{1,0:T(8,128)(2,1)S(1)} %collective-permute-done.10.e.e_other, bf16[384,1024]{1,0:T(8,128)(2,1)S(1)} %collective-permute-done.17.other, bf16[512,512]{1,0:T(8,128)(2,1)S(1)} %get-tuple-element.83.ft, f32[512,1]{1,0:T(8,128)S(1)} %get-tuple-element.84.scale, ...), custom_call_target="tpu_custom_call", output_to_operand_aliasing={{}: (6, {})} | custom-call | flops 1073741824 | bytes 3145728 | tf_op jit(solution)/shard_map/pallas_call | solution.py:34
  (46 shorter events, 14.6 us)
Async XLA Ops:
  2.4 2.4 %collective-permute-start = (bf16[4,8320]{1,0:T(4,128)(2,1)S(1)}, bf16[4,8320]{1,0:T(4,128)(2,1)S(1)}, u32[]{:S(2)}, u32[]{:S(2)}) collective-permute-start(bf16[4,8320]{1,0:T(4,128)(2,1)S(1)} %get-tuple-element.47), channel_id=1, source_target_pairs={{0,1},{1,0},{2,3},{3,2},{4,5},{5,4},{6,7},{7,6},{8,9},{9,8},{10,11... | collective-permute-start | bytes 199688 | tf_op jit(solution)/shard_map/ppermute | solution.py:364
  28.6 5.4 %collective-permute-start.1 = (bf16[128,4224]{1,0:T(8,128)(2,1)S(1)}, bf16[128,4224]{1,0:T(8,128)(2,1)S(1)}, u32[]{:S(2)}, u32[]{:S(2)}) collective-permute-start(bf16[128,4224]{1,0:T(8,128)(2,1)S(1)} %bitcast.10), channel_id=1, source_target_pairs={{0,1},{1,0},{2,3},{3,2},{4,5},{5,4},{6,7},{7,6},{8,9},{9,8},{10,11... | collective-permute-start | bytes 3244040 | tf_op jit(solution)/shard_map/ppermute | solution.py:364
  37.3 2.7 %collective-permute-start.2 = (bf16[128,4096]{1,0:T(8,128)(2,1)S(1)}, bf16[128,4096]{1,0:T(8,128)(2,1)S(1)}, u32[]{:S(2)}, u32[]{:S(2)}) collective-permute-start(bf16[128,4096]{1,0:T(8,128)(2,1)S(1)} %get-tuple-element.55), channel_id=1, source_target_pairs={{0,1},{1,0},{2,3},{3,2},{4,5},{5,4},{6,7},{7,6},{8,9},{9,8},{10,11... | collective-permute-start | bytes 3145736 | tf_op jit(solution)/shard_map/ppermute | solution.py:364
  41.1 8.8 %copy-start.4 = (bf16[128,1024]{1,0:T(8,128)(2,1)S(1)}, bf16[128,1024]{1,0:T(8,128)(2,1)}, u32[]{:S(2)}) copy-start(bf16[128,1024]{1,0:T(8,128)(2,1)} %get-tuple-element.63) | copy-start | bytes 786436
  41.1 20.1 %all-to-all-start.1 = ((bf16[16,8,4096]{2,1,0:T(8,128)(2,1)}), bf16[16,8,4096]{2,1,0:T(8,128)(2,1)S(1)}, u32[]{:S(2)}, u32[]{:S(2)}) async-start(bf16[16,8,4096]{2,1,0:T(8,128)(2,1)} %bitcast.13), calls=%async_computation.1 | async-start | bytes 2097152 | tf_op jit(solution)/shard_map/all_to_all | solution.py:368
  44.9 17.4 %collective-permute-start.3 = (bf16[128,1024]{1,0:T(8,128)(2,1)S(1)}, bf16[128,1024]{1,0:T(8,128)(2,1)S(1)}, u32[]{:S(2)}, u32[]{:S(2)}) collective-permute-start(bf16[128,1024]{1,0:T(8,128)(2,1)S(1)} %copy-done.6), channel_id=1, source_target_pairs={{0,32},{32,64},{64,96},{96,0},{1,33},{33,65},{65,97},{97,1},{2,34}... | collective-permute-start | bytes 786440 | tf_op jit(solution)/shard_map/ppermute | solution.py:376
  46.6 15.7 %collective-permute-start.4 = (bf16[128,1024]{1,0:T(8,128)(2,1)S(1)}, bf16[128,1024]{1,0:T(8,128)(2,1)S(1)}, u32[]{:S(2)}, u32[]{:S(2)}) collective-permute-start(bf16[128,1024]{1,0:T(8,128)(2,1)S(1)} %copy-done.5), channel_id=1, source_target_pairs={{0,64},{32,96},{64,0},{96,32},{1,65},{33,97},{65,1},{97,33},{2,66}... | collective-permute-start | bytes 786440 | tf_op jit(solution)/shard_map/ppermute | solution.py:376
  50.0 11.3 %copy-start.2 = (f32[2,4096]{1,0:T(2,128)S(1)}, f32[2,4096]{1,0:T(2,128)}, u32[]{:S(2)}) copy-start(f32[2,4096]{1,0:T(2,128)} %bias.1) | copy-start | bytes 98308
  50.0 12.4 %collective-permute-start.5 = (bf16[128,1024]{1,0:T(8,128)(2,1)S(1)}, bf16[128,1024]{1,0:T(8,128)(2,1)S(1)}, u32[]{:S(2)}, u32[]{:S(2)}) collective-permute-start(bf16[128,1024]{1,0:T(8,128)(2,1)S(1)} %copy-done.4), channel_id=1, source_target_pairs={{0,96},{32,0},{64,32},{96,64},{1,97},{33,1},{65,33},{97,65},{2,98}... | collective-permute-start | bytes 786440 | tf_op jit(solution)/shard_map/ppermute | solution.py:376
  62.4 20.8 %all-to-all-start.2 = ((bf16[16,8,4224]{2,1,0:T(8,128)(2,1)}), bf16[16,8,4224]{2,1,0:T(8,128)(2,1)S(1)}, u32[]{:S(2)}, u32[]{:S(2)}) async-start(bf16[16,8,4224]{2,1,0:T(8,128)(2,1)} %shard_map.101), calls=%async_computation.2 | async-start | bytes 2162688 | tf_op jit(solution)/shard_map/all_to_all | solution.py:368
  67.9 14.4 %collective-permute-start.6 = (bf16[384,1024]{1,0:T(8,128)(2,1)S(1)}, bf16[384,1024]{1,0:T(8,128)(2,1)S(1)}, u32[]{:S(2)}, u32[]{:S(2)}) collective-permute-start(bf16[384,1024]{1,0:T(8,128)(2,1)S(1)} %shard_map.102.own), channel_id=1, source_target_pairs={{0,1},{1,0},{2,3},{3,2},{4,5},{5,4},{6,7},{7,6},{8,9},{9,8},{10,11... | collective-permute-start | bytes 2359304 | tf_op jit(solution)/shard_map/ppermute | solution.py:364
  69.8 8.4 %collective-permute-start.9 = (bf16[136,512]{1,0:T(8,128)(2,1)S(1)}, bf16[136,512]{1,0:T(8,128)(2,1)S(1)}, u32[]{:S(2)}, u32[]{:S(2)}) collective-permute-start(bf16[136,512]{1,0:T(8,128)(2,1)S(1)} %get-tuple-element.70.feats.refs_0_), channel_id=1, source_target_pairs={{0,96},{32,0},{64,32},{96,64},{1,97},{33,1},{65,33},{97,65},{2,98}... | collective-permute-start | bytes 417800 | tf_op jit(solution)/shard_map/ppermute | solution.py:376
  72.4 6.5 %collective-permute-start.8 = (bf16[136,512]{1,0:T(8,128)(2,1)S(1)}, bf16[136,512]{1,0:T(8,128)(2,1)S(1)}, u32[]{:S(2)}, u32[]{:S(2)}) collective-permute-start(bf16[136,512]{1,0:T(8,128)(2,1)S(1)} %get-tuple-element.70.feats.refs_0_), channel_id=1, source_target_pairs={{0,64},{32,96},{64,0},{96,32},{1,65},{33,97},{65,1},{97,33},{2,66}... | collective-permute-start | bytes 417800 | tf_op jit(solution)/shard_map/ppermute | solution.py:376
  72.6 9.7 %collective-permute-start.7 = (bf16[136,512]{1,0:T(8,128)(2,1)S(1)}, bf16[136,512]{1,0:T(8,128)(2,1)S(1)}, u32[]{:S(2)}, u32[]{:S(2)}) collective-permute-start(bf16[136,512]{1,0:T(8,128)(2,1)S(1)} %get-tuple-element.70.feats.refs_0_), channel_id=1, source_target_pairs={{0,32},{32,64},{64,96},{96,0},{1,33},{33,65},{65,97},{97,1},{2,34}... | collective-permute-start | bytes 417800 | tf_op jit(solution)/shard_map/ppermute | solution.py:376
  83.2 7.8 %collective-permute-start.10 = (bf16[128,4224]{1,0:T(8,128)(2,1)S(1)}, bf16[128,4224]{1,0:T(8,128)(2,1)S(1)}, u32[]{:S(2)}, u32[]{:S(2)}) collective-permute-start(bf16[128,4224]{1,0:T(8,128)(2,1)S(1)} %bitcast.6), channel_id=1, source_target_pairs={{0,1},{1,0},{2,3},{3,2},{4,5},{5,4},{6,7},{7,6},{8,9},{9,8},{10,11... | collective-permute-start | bytes 3244040 | tf_op jit(solution)/shard_map/ppermute | solution.py:364
  86.5 12.7 %collective-permute-start.14 = (bf16[128,1024]{1,0:T(8,128)(2,1)S(1)}, bf16[128,1024]{1,0:T(8,128)(2,1)S(1)}, u32[]{:S(2)}, u32[]{:S(2)}) collective-permute-start(bf16[128,1024]{1,0:T(8,128)(2,1)S(1)} %get-tuple-element.79), channel_id=1, source_target_pairs={{0,32},{32,64},{64,96},{96,0},{1,33},{33,65},{65,97},{97,1},{2,34}... | collective-permute-start | bytes 786440 | tf_op jit(solution)/shard_map/ppermute | solution.py:376
  88.6 14.5 %collective-permute-start.15 = (bf16[128,1024]{1,0:T(8,128)(2,1)S(1)}, bf16[128,1024]{1,0:T(8,128)(2,1)S(1)}, u32[]{:S(2)}, u32[]{:S(2)}) collective-permute-start(bf16[128,1024]{1,0:T(8,128)(2,1)S(1)} %get-tuple-element.80), channel_id=1, source_target_pairs={{0,64},{32,96},{64,0},{96,32},{1,65},{33,97},{65,1},{97,33},{2,66}... | collective-permute-start | bytes 786440 | tf_op jit(solution)/shard_map/ppermute | solution.py:376
  91.0 12.1 %collective-permute-start.16 = (bf16[128,1024]{1,0:T(8,128)(2,1)S(1)}, bf16[128,1024]{1,0:T(8,128)(2,1)S(1)}, u32[]{:S(2)}, u32[]{:S(2)}) collective-permute-start(bf16[128,1024]{1,0:T(8,128)(2,1)S(1)} %get-tuple-element.81), channel_id=1, source_target_pairs={{0,96},{32,0},{64,32},{96,64},{1,97},{33,1},{65,33},{97,65},{2,98}... | collective-permute-start | bytes 786440 | tf_op jit(solution)/shard_map/ppermute | solution.py:376
  91.1 8.1 %copy-start = (bf16[128,1024]{1,0:T(8,128)(2,1)S(1)}, bf16[128,1024]{1,0:T(8,128)(2,1)}, u32[]{:S(2)}) copy-start(bf16[128,1024]{1,0:T(8,128)(2,1)} %get-tuple-element.49.home_own) | copy-start | bytes 786436
  91.1 8.1 %copy-start.1 = (bf16[128,1024]{1,0:T(8,128)(2,1)S(1)}, bf16[128,1024]{1,0:T(8,128)(2,1)}, u32[]{:S(2)}) copy-start(bf16[128,1024]{1,0:T(8,128)(2,1)} %get-tuple-element.53.home_other) | copy-start | bytes 786436
  95.9 9.7 %collective-permute-start.13 = (bf16[136,512]{1,0:T(8,128)(2,1)S(1)}, bf16[136,512]{1,0:T(8,128)(2,1)S(1)}, u32[]{:S(2)}, u32[]{:S(2)}) collective-permute-start(bf16[136,512]{1,0:T(8,128)(2,1)S(1)} %shard_map.103.refs_6_.refs_0_.p0), channel_id=1, source_target_pairs={{0,96},{32,0},{64,32},{96,64},{1,97},{33,1},{65,33},{97,65},{2,98}... | collective-permute-start | bytes 417800 | tf_op jit(solution)/shard_map/ppermute | solution.py:376
  96.9 9.2 %collective-permute-start.12 = (bf16[136,512]{1,0:T(8,128)(2,1)S(1)}, bf16[136,512]{1,0:T(8,128)(2,1)S(1)}, u32[]{:S(2)}, u32[]{:S(2)}) collective-permute-start(bf16[136,512]{1,0:T(8,128)(2,1)S(1)} %shard_map.103.refs_6_.refs_0_.p0), channel_id=1, source_target_pairs={{0,64},{32,96},{64,0},{96,32},{1,65},{33,97},{65,1},{97,33},{2,66}... | collective-permute-start | bytes 417800 | tf_op jit(solution)/shard_map/ppermute | solution.py:376
  99.2 10.2 %collective-permute-start.11 = (bf16[136,512]{1,0:T(8,128)(2,1)S(1)}, bf16[136,512]{1,0:T(8,128)(2,1)S(1)}, u32[]{:S(2)}, u32[]{:S(2)}) collective-permute-start(bf16[136,512]{1,0:T(8,128)(2,1)S(1)} %shard_map.103.refs_6_.refs_0_.p0), channel_id=1, source_target_pairs={{0,32},{32,64},{64,96},{96,0},{1,33},{33,65},{65,97},{97,1},{2,34}... | collective-permute-start | bytes 417800 | tf_op jit(solution)/shard_map/ppermute | solution.py:376
  109.9 3.5 %collective-permute-start.17 = (bf16[384,1024]{1,0:T(8,128)(2,1)S(1)}, bf16[384,1024]{1,0:T(8,128)(2,1)S(1)}, u32[]{:S(2)}, u32[]{:S(2)}) collective-permute-start(bf16[384,1024]{1,0:T(8,128)(2,1)S(1)} %get-tuple-element.82.own), channel_id=1, source_target_pairs={{0,1},{1,0},{2,3},{3,2},{4,5},{5,4},{6,7},{7,6},{8,9},{9,8},{10,11... | collective-permute-start | bytes 2359304 | tf_op jit(solution)/shard_map/ppermute | solution.py:364
  (3 other events, 14.8 us)

commit v6 on v5

--- a/solution.py
+++ b/solution.py
@@ -304,20 +304,10 @@
         out[:ROWS, n] = (grad * 2.0 * act[:, n]).astype(bf16)
 
 
-def merge_kernel(a, b, d, out):
+def merge_kernel(a, b, d, *refs):
+    out = refs[-1]
     for k, v in enumerate((a, b, d)):
         out[k * ROWS : (k + 1) * ROWS, :] = v[...]
-
-
-def part_kernel(*refs):
-    pres, slices, count = refs[0:4], refs[4:7], refs[7]
-    es, loss = refs[8:]
-    total = jnp.zeros((1, 1), f32)
-    for p in pres:
-        total = total + jnp.sum(p[ROWS : ROWS + 1, 0:3].astype(f32), axis=1, keepdims=True)
-    for k, p in enumerate(slices):
-        es[k * ROWS : (k + 1) * ROWS, :] = p[...]
-    loss[...] = total / (count[0:1, 0:1] * WIDTH)
 
 
 def dec_half(side, plane, rest, ft, scale, w, factor, done, out, sems):
@@ -334,11 +324,17 @@
     return copies
 
 
-def grads_kernel(xt, count, p0, p1, p2, p3, e_own, own, ft, scale, w, out_enc, out_dec, ds, done, done_dec, sems):
+def grads_kernel(
+    xt, count, p0, p1, p2, p3, e_own, own, ft, scale, w, out_enc, out_dec, loss, ds, done, done_dec, total, sems
+):
+    loss_sum = jnp.zeros((1, 1), f32)
     for k, p in enumerate((p0, p1, p2, p3)):
         ds[k * ROWS : (k + 1) * ROWS, :] = p[:ROWS, :]
+        loss_sum = loss_sum + jnp.sum(p[ROWS : ROWS + 1, 0:3].astype(f32), axis=1, keepdims=True)
+    total[...] = loss_sum / (count[0:1, 0:1] * WIDTH)
+    copies = [pltpu.make_async_copy(total, loss, sems.at[6])]
+    copies[0].start()
     factor = loss_scale / count[0:1, 0:1]
-    copies = []
     for i in range(4):
         rows = pl.ds(i % 2 * 512, 512)
         part = jnp.dot(xt[i // 2, rows, :], ds[...], preferred_element_type=f32)
@@ -501,23 +497,19 @@
         [pltpu.SemaphoreType.DMA],
         nbytes=6 * MIB,
     )
-    es, loss = call(
-        part_kernel,
-        [((3 * ROWS, SUB), bf16), ((1, 1), f32)],
-        (*ds, *es, count),
-        nbytes=3 * MIB,
-    )
-    grad_enc, half = call(
+    (es,) = call(merge_kernel, [((3 * ROWS, SUB), bf16)], (*es, count, *ds[1:]), [VM] * 4 + [anywhere] * 3)
+    grad_enc, half, loss = call(
         grads_kernel,
-        [((2, SUB, LOCAL), bf16), ((LOCAL, 2 * SUB), bf16)],
+        [((2, SUB, LOCAL), bf16), ((LOCAL, 2 * SUB), bf16), ((1, 1), f32, pltpu.HBM)],
         (xt, count, *ds, e_own, es, ft, scale, w_slice),
         scratch=[
             pltpu.VMEM((NZ * ROWS, LOCAL), bf16),
             pltpu.VMEM((2, SUB, LOCAL), bf16),
             pltpu.VMEM((2, LOCAL, 512), bf16),
-            pltpu.SemaphoreType.DMA((6,)),
+            pltpu.VMEM((1, 1), f32),
+            pltpu.SemaphoreType.DMA((7,)),
         ],
-        out_specs=[hbm, hbm],
+        out_specs=[hbm] * 3,
         flops=6 * half_flops,
         nbytes=8 * MIB,
     )

time: 116 us -> 115 us (level)
  no operation moved by 1% of the time
where the time goes in v6:
time: 115 us
  starting transfers between devices  34.9 us (30%)
  Pallas kernels  30.3 us (26%)
  waiting for transfers between devices  24.4 us (21%)
  blocking collectives  23.7 us (21%)
  between operations  1.67 us (1%)
    pallas_call x15, Pallas kernels, call(): pl.pallas_call(body, out_shape=[o[2](o[0], o[1]) if len(o) == 3 else jax....  30.3 us
    all_to_all x1, blocking collectives, chips(): lax.all_to_all(v, ('x', 'y'), split_axis=0, concat_axis=0, tiled=True)  23.7 us
    ppermute x12, waiting for transfers between devices, shift(): return lax.ppermute(v, 'z', [(i, (i + k) % NZ) for i in range(NZ)])  16.9 us
    ppermute x12, starting transfers between devices, shift(): return lax.ppermute(v, 'z', [(i, (i + k) % NZ) for i in range(NZ)])  16.8 us
    all_to_all x2, starting transfers between devices, chips(): lax.all_to_all(v, ('x', 'y'), split_axis=0, concat_axis=0, tiled=True)  9.28 us
    ppermute x6, starting transfers between devices, swap(): return lax.ppermute(v, 'c', [(0, 1), (1, 0)])  8.75 us
    all_to_all x2, waiting for transfers between devices, chips(): lax.all_to_all(v, ('x', 'y'), split_axis=0, concat_axis=0, tiled=True)  6.43 us
  transfers between devices with their start and end apart: 20, of which 11 were waited for; matrix products, arithmetic and copies ran while one was open for 0% of the time, Pallas kernels for 20%

profile of v6, /device:TPU:1, one launch (start us, length us, event | category | flops | bytes accessed | tf_op | source)
XLA Modules:
  0.0 114.9 jit_solution(17144054529343562055)
XLA Ops:
  4.9 23.7 %all_to_all.15 = bf16[16,8,4224]{2,1,0:T(8,128)(2,1)S(1)} all-to-all(bf16[16,8,4224]{2,1,0:T(8,128)(2,1)S(1)} %get-tuple-element.47), channel_id=1, replica_groups=mesh['z'=4,'x'=4,'y'=4,'c'=2] {'x','y'}, dimensions={0} | all-to-all | bytes 2162688 | tf_op jit(solution)/shard_map/all_to_all | solution.py:364
  30.1 3.9 %shard_map.96 = (f32[128,512]{1,0:T(8,128)S(1)}, bf16[4096,512]{1,0:T(8,128)(2,1)S(1)}, bf16[128,128]{1,0:T(8,128)(2,1)S(1)}, bf16[128,1024]{1,0:T(8,128)(2,1)},...) custom-call(bf16[128,4224]{1,0:T(8,128)(2,1)S(1)} %bitcast.11, ...), custom_call_target="tpu_custom_call" | custom-call | flops 536870912 | bytes 10485760 | tf_op jit(solution)/shard_map/pallas_call | solution.py:34
  34.0 3.3 %shard_map.97 = (f32[128,512]{1,0:T(8,128)}, bf16[136,512]{1,0:T(8,128)(2,1)S(1)}, bf16[128,4096]{1,0:T(8,128)(2,1)S(1)}, bf16[128,1024]{1,0:T(8,128)(2,1)}) custom-call(bf16[128,4224]{1,0:T(8,128)(2,1)S(1)} %collective-permute-done.1.x, bf16[128,128]{1,0:T(8,128)(2,1)S(1)} %get-tuple-element.49.mask, f32[128,512]{1,0:T(8,128)S(1)} %get-tuple-element.50.part, ...), custom_call_target="tpu_custom_call" | custom-call | flops 1073741824 | bytes 8388608 | tf_op jit(solution)/shard_map/pallas_call | solution.py:34
  37.4 2.5 %shard_map.98.own = f32[128,4096]{1,0:T(8,128)S(1)} custom-call(bf16[136,512]{1,0:T(8,128)(2,1)S(1)} %get-tuple-element.69.feats.refs_0_, bf16[512,8192]{1,0:T(8,128)(2,1)} %refs_5_.1), custom_call_target="tpu_custom_call" | custom-call | flops 536870912 | bytes 6291456 | tf_op jit(solution)/shard_map/pallas_call | solution.py:34
  41.1 3.8 %all-to-all-start.1 = ((bf16[16,8,4096]{2,1,0:T(8,128)(2,1)}), bf16[16,8,4096]{2,1,0:T(8,128)(2,1)S(1)}, u32[]{:S(2)}, u32[]{:S(2)}) async-start(bf16[16,8,4096]{2,1,0:T(8,128)(2,1)} %bitcast.13), calls=%async_computation.1 | async-start | bytes 2097152 | tf_op jit(solution)/shard_map/all_to_all | solution.py:364
  44.9 1.7 %collective-permute-start.3 = (bf16[128,1024]{1,0:T(8,128)(2,1)S(1)}, bf16[128,1024]{1,0:T(8,128)(2,1)S(1)}, u32[]{:S(2)}, u32[]{:S(2)}) collective-permute-start(bf16[128,1024]{1,0:T(8,128)(2,1)S(1)} %copy-done.6), channel_id=1, source_target_pairs={{0,32},{32,64},{64,96},{96,0},{1,33},{33,65},{65,97},{97,1},{2,34}... | collective-permute-start | bytes 786440 | tf_op jit(solution)/shard_map/ppermute | solution.py:372
  46.6 3.3 %collective-permute-start.4 = (bf16[128,1024]{1,0:T(8,128)(2,1)S(1)}, bf16[128,1024]{1,0:T(8,128)(2,1)S(1)}, u32[]{:S(2)}, u32[]{:S(2)}) collective-permute-start(bf16[128,1024]{1,0:T(8,128)(2,1)S(1)} %copy-done.5), channel_id=1, source_target_pairs={{0,64},{32,96},{64,0},{96,32},{1,65},{33,97},{65,1},{97,33},{2,66}... | collective-permute-start | bytes 786440 | tf_op jit(solution)/shard_map/ppermute | solution.py:372
  50.7 5.0 %shard_map.100 = (f32[2,512]{1,0:T(2,128)S(1)}, f32[512,2]{1,0:T(8,128)S(1)}) custom-call(bf16[512,8192]{1,0:T(8,128)(2,1)} %refs_5_.1), custom_call_target="tpu_custom_call" | custom-call | flops 16777216 | bytes 8388608 | tf_op jit(solution)/shard_map/pallas_call | solution.py:34
  55.7 5.5 %all-to-all-done.1.parts = bf16[16,8,4096]{2,1,0:T(8,128)(2,1)S(1)} async-done(((bf16[16,8,4096]{2,1,0:T(8,128)(2,1)}), bf16[16,8,4096]{2,1,0:T(8,128)(2,1)S(1)}, u32[]{:S(2)}, u32[]{:S(2)}) %all-to-all-start.1) | async-done | bytes 1048608 | tf_op jit(solution)/shard_map/all_to_all | solution.py:364
  62.4 5.5 %all-to-all-start.2 = ((bf16[16,8,4224]{2,1,0:T(8,128)(2,1)}), bf16[16,8,4224]{2,1,0:T(8,128)(2,1)S(1)}, u32[]{:S(2)}, u32[]{:S(2)}) async-start(bf16[16,8,4224]{2,1,0:T(8,128)(2,1)} %shard_map.101), calls=%async_computation.2 | async-start | bytes 2162688 | tf_op jit(solution)/shard_map/all_to_all | solution.py:364
  67.9 1.9 %collective-permute-start.6 = (bf16[384,1024]{1,0:T(8,128)(2,1)S(1)}, bf16[384,1024]{1,0:T(8,128)(2,1)S(1)}, u32[]{:S(2)}, u32[]{:S(2)}) collective-permute-start(bf16[384,1024]{1,0:T(8,128)(2,1)S(1)} %shard_map.102.own), channel_id=1, source_target_pairs={{0,1},{1,0},{2,3},{3,2},{4,5},{5,4},{6,7},{7,6},{8,9},{9,8},{10,11... | collective-permute-start | bytes 2359304 | tf_op jit(solution)/shard_map/ppermute | solution.py:360
  69.8 2.6 %collective-permute-start.9 = (bf16[136,512]{1,0:T(8,128)(2,1)S(1)}, bf16[136,512]{1,0:T(8,128)(2,1)S(1)}, u32[]{:S(2)}, u32[]{:S(2)}) collective-permute-start(bf16[136,512]{1,0:T(8,128)(2,1)S(1)} %get-tuple-element.69.feats.refs_0_), channel_id=1, source_target_pairs={{0,96},{32,0},{64,32},{96,64},{1,97},{33,1},{65,33},{97,65},{2,98}... | collective-permute-start | bytes 417800 | tf_op jit(solution)/shard_map/ppermute | solution.py:372
  73.1 5.2 %collective-permute-done.9.refs_3_ = bf16[136,512]{1,0:T(8,128)(2,1)S(1)} collective-permute-done((bf16[136,512]{1,0:T(8,128)(2,1)S(1)}, bf16[136,512]{1,0:T(8,128)(2,1)S(1)}, u32[]{:S(2)}, u32[]{:S(2)}) %collective-permute-start.9) | collective-permute-done | bytes 139296 | tf_op jit(solution)/shard_map/ppermute | solution.py:372
  78.9 3.5 %collective-permute-done.7.refs_1_ = bf16[136,512]{1,0:T(8,128)(2,1)S(1)} collective-permute-done((bf16[136,512]{1,0:T(8,128)(2,1)S(1)}, bf16[136,512]{1,0:T(8,128)(2,1)S(1)}, u32[]{:S(2)}, u32[]{:S(2)}) %collective-permute-start.7) | collective-permute-done | bytes 139296 | tf_op jit(solution)/shard_map/ppermute | solution.py:372
  83.2 3.2 %collective-permute-start.10 = (bf16[128,4224]{1,0:T(8,128)(2,1)S(1)}, bf16[128,4224]{1,0:T(8,128)(2,1)S(1)}, u32[]{:S(2)}, u32[]{:S(2)}) collective-permute-start(bf16[128,4224]{1,0:T(8,128)(2,1)S(1)} %bitcast.6), channel_id=1, source_target_pairs={{0,1},{1,0},{2,3},{3,2},{4,5},{5,4},{6,7},{7,6},{8,9},{9,8},{10,11... | collective-permute-start | bytes 3244040 | tf_op jit(solution)/shard_map/ppermute | solution.py:360
  86.5 2.1 %collective-permute-start.14 = (bf16[128,1024]{1,0:T(8,128)(2,1)S(1)}, bf16[128,1024]{1,0:T(8,128)(2,1)S(1)}, u32[]{:S(2)}, u32[]{:S(2)}) collective-permute-start(bf16[128,1024]{1,0:T(8,128)(2,1)S(1)} %get-tuple-element.78), channel_id=1, source_target_pairs={{0,32},{32,64},{64,96},{96,0},{1,33},{33,65},{65,97},{97,1},{2,34}... | collective-permute-start | bytes 786440 | tf_op jit(solution)/shard_map/ppermute | solution.py:372
  88.6 2.4 %collective-permute-start.15 = (bf16[128,1024]{1,0:T(8,128)(2,1)S(1)}, bf16[128,1024]{1,0:T(8,128)(2,1)S(1)}, u32[]{:S(2)}, u32[]{:S(2)}) collective-permute-start(bf16[128,1024]{1,0:T(8,128)(2,1)S(1)} %get-tuple-element.79), channel_id=1, source_target_pairs={{0,64},{32,96},{64,0},{96,32},{1,65},{33,97},{65,1},{97,33},{2,66}... | collective-permute-start | bytes 786440 | tf_op jit(solution)/shard_map/ppermute | solution.py:372
  91.1 4.9 %shard_map.103.refs_6_.p0 = bf16[136,512]{1,0:T(8,128)(2,1)S(1)} custom-call(bf16[128,4224]{1,0:T(8,128)(2,1)S(1)} %bitcast.8, bf16[128,4224]{1,0:T(8,128)(2,1)S(1)} %collective-permute-done.10.e.e_other, bf16[128,128]{1,0:T(8,128)(2,1)S(1)} %get-tuple-element.49.mask, f32[2,512]{1,0:T(2,128)S(1)} %get-tuple-element.59.norm_row, ...), custom_call_target="tpu_custom_call" | custom-call | flops 1073741824 | bytes 10485760 | tf_op jit(solution)/shard_map/pallas_call | solution.py:34
  96.9 2.2 %collective-permute-start.12 = (bf16[136,512]{1,0:T(8,128)(2,1)S(1)}, bf16[136,512]{1,0:T(8,128)(2,1)S(1)}, u32[]{:S(2)}, u32[]{:S(2)}) collective-permute-start(bf16[136,512]{1,0:T(8,128)(2,1)S(1)} %shard_map.103.refs_6_.p0), channel_id=1, source_target_pairs={{0,64},{32,96},{64,0},{96,32},{1,65},{33,97},{65,1},{97,33},{2,66}... | collective-permute-start | bytes 417800 | tf_op jit(solution)/shard_map/ppermute | solution.py:372
  99.2 2.4 %shard_map.104 = (bf16[2,1024,512]{2,1,0:T(8,128)(2,1)S(1)}, bf16[512,512]{1,0:T(8,128)(2,1)S(1)}, f32[512,1]{1,0:T(8,128)S(1)}, f32[8,128]{1,0:T(8,128)S(1)}, bf16[512,2048]{1,0:T(8,128)(2,1)S(1)}) custom-call(bf16[128,1024]{1,0:T(8,128)(2,1)S(1)} %copy-done, bf16[128,1024]{1,0:T(8,128)(2,1)S(1)} %copy-done.1, bf16[384,1024]{1,0:T(8,128)(2,1)S(1)} %shard_map.102.own, ...), custom_call_target="tpu_custom_call" | custom-call | bytes 6291456 | tf_op jit(solution)/shard_map/pallas_call | solution.py:34
  103.1 2.5 %collective-permute-done.13.refs_3_.p3 = bf16[136,512]{1,0:T(8,128)(2,1)S(1)} collective-permute-done((bf16[136,512]{1,0:T(8,128)(2,1)S(1)}, bf16[136,512]{1,0:T(8,128)(2,1)S(1)}, u32[]{:S(2)}, u32[]{:S(2)}) %collective-permute-start.13) | collective-permute-done | bytes 139296 | tf_op jit(solution)/shard_map/ppermute | solution.py:372
  106.1 3.2 %collective-permute-done.11.refs_1_.p1 = bf16[136,512]{1,0:T(8,128)(2,1)S(1)} collective-permute-done((bf16[136,512]{1,0:T(8,128)(2,1)S(1)}, bf16[136,512]{1,0:T(8,128)(2,1)S(1)}, u32[]{:S(2)}, u32[]{:S(2)}) %collective-permute-start.11) | collective-permute-done | bytes 139296 | tf_op jit(solution)/shard_map/ppermute | solution.py:372
  110.0 3.0 %shard_map.107 = (bf16[2,1024,512]{2,1,0:T(8,128)(2,1)}, bf16[512,2048]{1,0:T(8,128)(2,1)}, f32[1,1]{1,0:T(1,128)}) custom-call(bf16[2,1024,512]{2,1,0:T(8,128)(2,1)S(1)} %get-tuple-element.76.xt, f32[8,128]{1,0:T(8,128)S(1)} %get-tuple-element.77.refs_0_.count, bf16[136,512]{1,0:T(8,128)(2,1)S(1)} %shard_map.103.refs_6_.p0, ...), custom_call_target="tpu_custom_call" | custom-call | flops 3221225472 | bytes 8388608 | tf_op jit(solution)/shard_map/pallas_call | solution.py:34
  113.0 1.8 %shard_map.108 = bf16[512,2048]{1,0:T(8,128)(2,1)} custom-call(bf16[128,4224]{1,0:T(8,128)(2,1)S(1)} %collective-permute-done.10.e.e_other, bf16[384,1024]{1,0:T(8,128)(2,1)S(1)} %collective-permute-done.17.other, bf16[512,512]{1,0:T(8,128)(2,1)S(1)} %get-tuple-element.81.ft, f32[512,1]{1,0:T(8,128)S(1)} %get-tuple-element.82.scale, ...), custom_call_target="tpu_custom_call", output_to_operand_aliasing={{}: (6, {})} | custom-call | flops 1073741824 | bytes 3145728 | tf_op jit(solution)/shard_map/pallas_call | solution.py:34
  (46 shorter events, 14.1 us)
Async XLA Ops:
  2.4 2.4 %collective-permute-start = (bf16[4,8320]{1,0:T(4,128)(2,1)S(1)}, bf16[4,8320]{1,0:T(4,128)(2,1)S(1)}, u32[]{:S(2)}, u32[]{:S(2)}) collective-permute-start(bf16[4,8320]{1,0:T(4,128)(2,1)S(1)} %get-tuple-element.46), channel_id=1, source_target_pairs={{0,1},{1,0},{2,3},{3,2},{4,5},{5,4},{6,7},{7,6},{8,9},{9,8},{10,11... | collective-permute-start | bytes 199688 | tf_op jit(solution)/shard_map/ppermute | solution.py:360
  28.6 5.4 %collective-permute-start.1 = (bf16[128,4224]{1,0:T(8,128)(2,1)S(1)}, bf16[128,4224]{1,0:T(8,128)(2,1)S(1)}, u32[]{:S(2)}, u32[]{:S(2)}) collective-permute-start(bf16[128,4224]{1,0:T(8,128)(2,1)S(1)} %bitcast.10), channel_id=1, source_target_pairs={{0,1},{1,0},{2,3},{3,2},{4,5},{5,4},{6,7},{7,6},{8,9},{9,8},{10,11... | collective-permute-start | bytes 3244040 | tf_op jit(solution)/shard_map/ppermute | solution.py:360
  37.3 2.7 %collective-permute-start.2 = (bf16[128,4096]{1,0:T(8,128)(2,1)S(1)}, bf16[128,4096]{1,0:T(8,128)(2,1)S(1)}, u32[]{:S(2)}, u32[]{:S(2)}) collective-permute-start(bf16[128,4096]{1,0:T(8,128)(2,1)S(1)} %get-tuple-element.54), channel_id=1, source_target_pairs={{0,1},{1,0},{2,3},{3,2},{4,5},{5,4},{6,7},{7,6},{8,9},{9,8},{10,11... | collective-permute-start | bytes 3145736 | tf_op jit(solution)/shard_map/ppermute | solution.py:360
  41.1 8.8 %copy-start.4 = (bf16[128,1024]{1,0:T(8,128)(2,1)S(1)}, bf16[128,1024]{1,0:T(8,128)(2,1)}, u32[]{:S(2)}) copy-start(bf16[128,1024]{1,0:T(8,128)(2,1)} %get-tuple-element.62) | copy-start | bytes 786436
  41.1 20.1 %all-to-all-start.1 = ((bf16[16,8,4096]{2,1,0:T(8,128)(2,1)}), bf16[16,8,4096]{2,1,0:T(8,128)(2,1)S(1)}, u32[]{:S(2)}, u32[]{:S(2)}) async-start(bf16[16,8,4096]{2,1,0:T(8,128)(2,1)} %bitcast.13), calls=%async_computation.1 | async-start | bytes 2097152 | tf_op jit(solution)/shard_map/all_to_all | solution.py:364
  44.9 17.4 %collective-permute-start.3 = (bf16[128,1024]{1,0:T(8,128)(2,1)S(1)}, bf16[128,1024]{1,0:T(8,128)(2,1)S(1)}, u32[]{:S(2)}, u32[]{:S(2)}) collective-permute-start(bf16[128,1024]{1,0:T(8,128)(2,1)S(1)} %copy-done.6), channel_id=1, source_target_pairs={{0,32},{32,64},{64,96},{96,0},{1,33},{33,65},{65,97},{97,1},{2,34}... | collective-permute-start | bytes 786440 | tf_op jit(solution)/shard_map/ppermute | solution.py:372
  46.6 15.7 %collective-permute-start.4 = (bf16[128,1024]{1,0:T(8,128)(2,1)S(1)}, bf16[128,1024]{1,0:T(8,128)(2,1)S(1)}, u32[]{:S(2)}, u32[]{:S(2)}) collective-permute-start(bf16[128,1024]{1,0:T(8,128)(2,1)S(1)} %copy-done.5), channel_id=1, source_target_pairs={{0,64},{32,96},{64,0},{96,32},{1,65},{33,97},{65,1},{97,33},{2,66}... | collective-permute-start | bytes 786440 | tf_op jit(solution)/shard_map/ppermute | solution.py:372
  50.0 11.3 %copy-start.2 = (f32[2,4096]{1,0:T(2,128)S(1)}, f32[2,4096]{1,0:T(2,128)}, u32[]{:S(2)}) copy-start(f32[2,4096]{1,0:T(2,128)} %bias.1) | copy-start | bytes 98308
  50.0 12.4 %collective-permute-start.5 = (bf16[128,1024]{1,0:T(8,128)(2,1)S(1)}, bf16[128,1024]{1,0:T(8,128)(2,1)S(1)}, u32[]{:S(2)}, u32[]{:S(2)}) collective-permute-start(bf16[128,1024]{1,0:T(8,128)(2,1)S(1)} %copy-done.4), channel_id=1, source_target_pairs={{0,96},{32,0},{64,32},{96,64},{1,97},{33,1},{65,33},{97,65},{2,98}... | collective-permute-start | bytes 786440 | tf_op jit(solution)/shard_map/ppermute | solution.py:372
  62.4 20.8 %all-to-all-start.2 = ((bf16[16,8,4224]{2,1,0:T(8,128)(2,1)}), bf16[16,8,4224]{2,1,0:T(8,128)(2,1)S(1)}, u32[]{:S(2)}, u32[]{:S(2)}) async-start(bf16[16,8,4224]{2,1,0:T(8,128)(2,1)} %shard_map.101), calls=%async_computation.2 | async-start | bytes 2162688 | tf_op jit(solution)/shard_map/all_to_all | solution.py:364
  67.9 14.4 %collective-permute-start.6 = (bf16[384,1024]{1,0:T(8,128)(2,1)S(1)}, bf16[384,1024]{1,0:T(8,128)(2,1)S(1)}, u32[]{:S(2)}, u32[]{:S(2)}) collective-permute-start(bf16[384,1024]{1,0:T(8,128)(2,1)S(1)} %shard_map.102.own), channel_id=1, source_target_pairs={{0,1},{1,0},{2,3},{3,2},{4,5},{5,4},{6,7},{7,6},{8,9},{9,8},{10,11... | collective-permute-start | bytes 2359304 | tf_op jit(solution)/shard_map/ppermute | solution.py:360
  69.8 8.4 %collective-permute-start.9 = (bf16[136,512]{1,0:T(8,128)(2,1)S(1)}, bf16[136,512]{1,0:T(8,128)(2,1)S(1)}, u32[]{:S(2)}, u32[]{:S(2)}) collective-permute-start(bf16[136,512]{1,0:T(8,128)(2,1)S(1)} %get-tuple-element.69.feats.refs_0_), channel_id=1, source_target_pairs={{0,96},{32,0},{64,32},{96,64},{1,97},{33,1},{65,33},{97,65},{2,98}... | collective-permute-start | bytes 417800 | tf_op jit(solution)/shard_map/ppermute | solution.py:372
  72.4 6.5 %collective-permute-start.8 = (bf16[136,512]{1,0:T(8,128)(2,1)S(1)}, bf16[136,512]{1,0:T(8,128)(2,1)S(1)}, u32[]{:S(2)}, u32[]{:S(2)}) collective-permute-start(bf16[136,512]{1,0:T(8,128)(2,1)S(1)} %get-tuple-element.69.feats.refs_0_), channel_id=1, source_target_pairs={{0,64},{32,96},{64,0},{96,32},{1,65},{33,97},{65,1},{97,33},{2,66}... | collective-permute-start | bytes 417800 | tf_op jit(solution)/shard_map/ppermute | solution.py:372
  72.6 9.7 %collective-permute-start.7 = (bf16[136,512]{1,0:T(8,128)(2,1)S(1)}, bf16[136,512]{1,0:T(8,128)(2,1)S(1)}, u32[]{:S(2)}, u32[]{:S(2)}) collective-permute-start(bf16[136,512]{1,0:T(8,128)(2,1)S(1)} %get-tuple-element.69.feats.refs_0_), channel_id=1, source_target_pairs={{0,32},{32,64},{64,96},{96,0},{1,33},{33,65},{65,97},{97,1},{2,34}... | collective-permute-start | bytes 417800 | tf_op jit(solution)/shard_map/ppermute | solution.py:372
  83.2 7.8 %collective-permute-start.10 = (bf16[128,4224]{1,0:T(8,128)(2,1)S(1)}, bf16[128,4224]{1,0:T(8,128)(2,1)S(1)}, u32[]{:S(2)}, u32[]{:S(2)}) collective-permute-start(bf16[128,4224]{1,0:T(8,128)(2,1)S(1)} %bitcast.6), channel_id=1, source_target_pairs={{0,1},{1,0},{2,3},{3,2},{4,5},{5,4},{6,7},{7,6},{8,9},{9,8},{10,11... | collective-permute-start | bytes 3244040 | tf_op jit(solution)/shard_map/ppermute | solution.py:360
  86.5 12.7 %collective-permute-start.14 = (bf16[128,1024]{1,0:T(8,128)(2,1)S(1)}, bf16[128,1024]{1,0:T(8,128)(2,1)S(1)}, u32[]{:S(2)}, u32[]{:S(2)}) collective-permute-start(bf16[128,1024]{1,0:T(8,128)(2,1)S(1)} %get-tuple-element.78), channel_id=1, source_target_pairs={{0,32},{32,64},{64,96},{96,0},{1,33},{33,65},{65,97},{97,1},{2,34}... | collective-permute-start | bytes 786440 | tf_op jit(solution)/shard_map/ppermute | solution.py:372
  88.6 14.5 %collective-permute-start.15 = (bf16[128,1024]{1,0:T(8,128)(2,1)S(1)}, bf16[128,1024]{1,0:T(8,128)(2,1)S(1)}, u32[]{:S(2)}, u32[]{:S(2)}) collective-permute-start(bf16[128,1024]{1,0:T(8,128)(2,1)S(1)} %get-tuple-element.79), channel_id=1, source_target_pairs={{0,64},{32,96},{64,0},{96,32},{1,65},{33,97},{65,1},{97,33},{2,66}... | collective-permute-start | bytes 786440 | tf_op jit(solution)/shard_map/ppermute | solution.py:372
  91.0 12.1 %collective-permute-start.16 = (bf16[128,1024]{1,0:T(8,128)(2,1)S(1)}, bf16[128,1024]{1,0:T(8,128)(2,1)S(1)}, u32[]{:S(2)}, u32[]{:S(2)}) collective-permute-start(bf16[128,1024]{1,0:T(8,128)(2,1)S(1)} %get-tuple-element.80), channel_id=1, source_target_pairs={{0,96},{32,0},{64,32},{96,64},{1,97},{33,1},{65,33},{97,65},{2,98}... | collective-permute-start | bytes 786440 | tf_op jit(solution)/shard_map/ppermute | solution.py:372
  91.1 8.1 %copy-start = (bf16[128,1024]{1,0:T(8,128)(2,1)S(1)}, bf16[128,1024]{1,0:T(8,128)(2,1)}, u32[]{:S(2)}) copy-start(bf16[128,1024]{1,0:T(8,128)(2,1)} %get-tuple-element.48.home_own) | copy-start | bytes 786436
  91.1 8.1 %copy-start.1 = (bf16[128,1024]{1,0:T(8,128)(2,1)S(1)}, bf16[128,1024]{1,0:T(8,128)(2,1)}, u32[]{:S(2)}) copy-start(bf16[128,1024]{1,0:T(8,128)(2,1)} %get-tuple-element.52.home_other) | copy-start | bytes 786436
  95.9 9.7 %collective-permute-start.13 = (bf16[136,512]{1,0:T(8,128)(2,1)S(1)}, bf16[136,512]{1,0:T(8,128)(2,1)S(1)}, u32[]{:S(2)}, u32[]{:S(2)}) collective-permute-start(bf16[136,512]{1,0:T(8,128)(2,1)S(1)} %shard_map.103.refs_6_.p0), channel_id=1, source_target_pairs={{0,96},{32,0},{64,32},{96,64},{1,97},{33,1},{65,33},{97,65},{2,98}... | collective-permute-start | bytes 417800 | tf_op jit(solution)/shard_map/ppermute | solution.py:372
  96.9 9.2 %collective-permute-start.12 = (bf16[136,512]{1,0:T(8,128)(2,1)S(1)}, bf16[136,512]{1,0:T(8,128)(2,1)S(1)}, u32[]{:S(2)}, u32[]{:S(2)}) collective-permute-start(bf16[136,512]{1,0:T(8,128)(2,1)S(1)} %shard_map.103.refs_6_.p0), channel_id=1, source_target_pairs={{0,64},{32,96},{64,0},{96,32},{1,65},{33,97},{65,1},{97,33},{2,66}... | collective-permute-start | bytes 417800 | tf_op jit(solution)/shard_map/ppermute | solution.py:372
  99.2 10.2 %collective-permute-start.11 = (bf16[136,512]{1,0:T(8,128)(2,1)S(1)}, bf16[136,512]{1,0:T(8,128)(2,1)S(1)}, u32[]{:S(2)}, u32[]{:S(2)}) collective-permute-start(bf16[136,512]{1,0:T(8,128)(2,1)S(1)} %shard_map.103.refs_6_.p0), channel_id=1, source_target_pairs={{0,32},{32,64},{64,96},{96,0},{1,33},{33,65},{65,97},{97,1},{2,34}... | collective-permute-start | bytes 417800 | tf_op jit(solution)/shard_map/ppermute | solution.py:372
  109.4 3.6 %collective-permute-start.17 = (bf16[384,1024]{1,0:T(8,128)(2,1)S(1)}, bf16[384,1024]{1,0:T(8,128)(2,1)S(1)}, u32[]{:S(2)}, u32[]{:S(2)}) collective-permute-start(bf16[384,1024]{1,0:T(8,128)(2,1)S(1)} %shard_map.106.own), channel_id=1, source_target_pairs={{0,1},{1,0},{2,3},{3,2},{4,5},{5,4},{6,7},{7,6},{8,9},{9,8},{10,11... | collective-permute-start | bytes 2359304 | tf_op jit(solution)/shard_map/ppermute | solution.py:360
  (3 other events, 14.8 us)

commit v7 on v6

--- a/solution.py
+++ b/solution.py
@@ -313,10 +313,10 @@
 def dec_half(side, plane, rest, ft, scale, w, factor, done, out, sems):
     z = lax.axis_index("z")
     copies = []
-    for i, m in enumerate(range(0, SUB, 512)):
-        cols = lanes(side * SUB + m, 512)
-        part = jnp.dot(ft[:, :ROWS], plane[:, lanes(z * SUB + m, 512)], preferred_element_type=f32)
-        part = part + jnp.dot(ft[:, ROWS:], rest[:, m : m + 512], preferred_element_type=f32)
+    for i, m in enumerate(range(0, SUB, 256)):
+        cols = lanes(side * SUB + m, 256)
+        part = jnp.dot(ft[:, :ROWS], plane[:, lanes(z * SUB + m, 256)], preferred_element_type=f32)
+        part = part + jnp.dot(ft[:, ROWS:], rest[:, m : m + 256], preferred_element_type=f32)
         part = part * (2.0 * factor) + (scale[...] * factor) * w[:, cols].astype(f32)
         done[i] = part.astype(bf16)
         copies.append(pltpu.make_async_copy(done.at[i], out.at[:, cols], sems[i]))
@@ -342,7 +342,7 @@
         copies.append(pltpu.make_async_copy(done.at[i // 2, rows], out_enc.at[i // 2, rows], sems.at[i]))
         copies[-1].start()
     copies += dec_half(
-        lax.axis_index("c"), e_own, own, ft, scale, w, factor, done_dec, out_dec, [sems.at[4], sems.at[5]]
+        lax.axis_index("c"), e_own, own, ft, scale, w, factor, done_dec, out_dec, [sems.at[i] for i in (4, 5, 7, 8)]
     )
     for copy in copies:
         copy.wait()
@@ -352,7 +352,7 @@
     del half
     side = 1 - lax.axis_index("c")
     factor = loss_scale / count[0:1, 0:1]
-    for copy in dec_half(side, e_other, other, ft, scale, w, factor, done, out, [sems.at[0], sems.at[1]]):
+    for copy in dec_half(side, e_other, other, ft, scale, w, factor, done, out, [sems.at[i] for i in range(4)]):
         copy.wait()
 
 
@@ -505,9 +505,9 @@
         scratch=[
             pltpu.VMEM((NZ * ROWS, LOCAL), bf16),
             pltpu.VMEM((2, SUB, LOCAL), bf16),
-            pltpu.VMEM((2, LOCAL, 512), bf16),
+            pltpu.VMEM((4, LOCAL, 256), bf16),
             pltpu.VMEM((1, 1), f32),
-            pltpu.SemaphoreType.DMA((7,)),
+            pltpu.SemaphoreType.DMA((9,)),
         ],
         out_specs=[hbm] * 3,
         flops=6 * half_flops,
@@ -518,7 +518,7 @@
         [((LOCAL, 2 * SUB), bf16)],
         (e_other, swap(es), ft, scale, count, w_slice, half),
         [VM] * 6 + [hbm],
-        [pltpu.VMEM((2, LOCAL, 512), bf16), pltpu.SemaphoreType.DMA((2,))],
+        [pltpu.VMEM((4, LOCAL, 256), bf16), pltpu.SemaphoreType.DMA((4,))],
         out_specs=[hbm],
         aliases={6: 0},
         flops=2 * half_flops,

time: 115 us -> 115 us (level)
  no operation moved by 1% of the time
where the time goes in v7:
time: 115 us
  starting transfers between devices  34.9 us (30%)
  Pallas kernels  30.4 us (26%)
  waiting for transfers between devices  24.4 us (21%)
  blocking collectives  23.7 us (21%)
  between operations  1.67 us (1%)
    pallas_call x15, Pallas kernels, call(): pl.pallas_call(body, out_shape=[o[2](o[0], o[1]) if len(o) == 3 else jax....  30.4 us
    all_to_all x1, blocking collectives, chips(): lax.all_to_all(v, ('x', 'y'), split_axis=0, concat_axis=0, tiled=True)  23.7 us
    ppermute x12, waiting for transfers between devices, shift(): return lax.ppermute(v, 'z', [(i, (i + k) % NZ) for i in range(NZ)])  16.9 us
    ppermute x12, starting transfers between devices, shift(): return lax.ppermute(v, 'z', [(i, (i + k) % NZ) for i in range(NZ)])  16.8 us
    all_to_all x2, starting transfers between devices, chips(): lax.all_to_all(v, ('x', 'y'), split_axis=0, concat_axis=0, tiled=True)  9.28 us
    ppermute x6, starting transfers between devices, swap(): return lax.ppermute(v, 'c', [(0, 1), (1, 0)])  8.75 us
    all_to_all x2, waiting for transfers between devices, chips(): lax.all_to_all(v, ('x', 'y'), split_axis=0, concat_axis=0, tiled=True)  6.43 us
  transfers between devices with their start and end apart: 20, of which 11 were waited for; matrix products, arithmetic and copies ran while one was open for 0% of the time, Pallas kernels for 20%

profile of v7, /device:TPU:1, one launch (start us, length us, event | category | flops | bytes accessed | tf_op | source)
XLA Modules:
  0.0 115.1 jit_solution(13860078660013735697)
XLA Ops:
  4.9 23.7 %all_to_all.15 = bf16[16,8,4224]{2,1,0:T(8,128)(2,1)S(1)} all-to-all(bf16[16,8,4224]{2,1,0:T(8,128)(2,1)S(1)} %get-tuple-element.47), channel_id=1, replica_groups=mesh['z'=4,'x'=4,'y'=4,'c'=2] {'x','y'}, dimensions={0} | all-to-all | bytes 2162688 | tf_op jit(solution)/shard_map/all_to_all | solution.py:364
  30.1 3.9 %shard_map.96 = (f32[128,512]{1,0:T(8,128)S(1)}, bf16[4096,512]{1,0:T(8,128)(2,1)S(1)}, bf16[128,128]{1,0:T(8,128)(2,1)S(1)}, bf16[128,1024]{1,0:T(8,128)(2,1)},...) custom-call(bf16[128,4224]{1,0:T(8,128)(2,1)S(1)} %bitcast.11, ...), custom_call_target="tpu_custom_call" | custom-call | flops 536870912 | bytes 10485760 | tf_op jit(solution)/shard_map/pallas_call | solution.py:34
  34.0 3.3 %shard_map.97 = (f32[128,512]{1,0:T(8,128)}, bf16[136,512]{1,0:T(8,128)(2,1)S(1)}, bf16[128,4096]{1,0:T(8,128)(2,1)S(1)}, bf16[128,1024]{1,0:T(8,128)(2,1)}) custom-call(bf16[128,4224]{1,0:T(8,128)(2,1)S(1)} %collective-permute-done.1.x, bf16[128,128]{1,0:T(8,128)(2,1)S(1)} %get-tuple-element.49.mask, f32[128,512]{1,0:T(8,128)S(1)} %get-tuple-element.50.part, ...), custom_call_target="tpu_custom_call" | custom-call | flops 1073741824 | bytes 8388608 | tf_op jit(solution)/shard_map/pallas_call | solution.py:34
  37.4 2.5 %shard_map.98.own = f32[128,4096]{1,0:T(8,128)S(1)} custom-call(bf16[136,512]{1,0:T(8,128)(2,1)S(1)} %get-tuple-element.69.feats.refs_0_, bf16[512,8192]{1,0:T(8,128)(2,1)} %refs_5_.1), custom_call_target="tpu_custom_call" | custom-call | flops 536870912 | bytes 6291456 | tf_op jit(solution)/shard_map/pallas_call | solution.py:34
  41.1 3.8 %all-to-all-start.1 = ((bf16[16,8,4096]{2,1,0:T(8,128)(2,1)}), bf16[16,8,4096]{2,1,0:T(8,128)(2,1)S(1)}, u32[]{:S(2)}, u32[]{:S(2)}) async-start(bf16[16,8,4096]{2,1,0:T(8,128)(2,1)} %bitcast.13), calls=%async_computation.1 | async-start | bytes 2097152 | tf_op jit(solution)/shard_map/all_to_all | solution.py:364
  44.9 1.7 %collective-permute-start.3 = (bf16[128,1024]{1,0:T(8,128)(2,1)S(1)}, bf16[128,1024]{1,0:T(8,128)(2,1)S(1)}, u32[]{:S(2)}, u32[]{:S(2)}) collective-permute-start(bf16[128,1024]{1,0:T(8,128)(2,1)S(1)} %copy-done.6), channel_id=1, source_target_pairs={{0,32},{32,64},{64,96},{96,0},{1,33},{33,65},{65,97},{97,1},{2,34}... | collective-permute-start | bytes 786440 | tf_op jit(solution)/shard_map/ppermute | solution.py:372
  46.6 3.3 %collective-permute-start.4 = (bf16[128,1024]{1,0:T(8,128)(2,1)S(1)}, bf16[128,1024]{1,0:T(8,128)(2,1)S(1)}, u32[]{:S(2)}, u32[]{:S(2)}) collective-permute-start(bf16[128,1024]{1,0:T(8,128)(2,1)S(1)} %copy-done.5), channel_id=1, source_target_pairs={{0,64},{32,96},{64,0},{96,32},{1,65},{33,97},{65,1},{97,33},{2,66}... | collective-permute-start | bytes 786440 | tf_op jit(solution)/shard_map/ppermute | solution.py:372
  50.7 5.0 %shard_map.100 = (f32[2,512]{1,0:T(2,128)S(1)}, f32[512,2]{1,0:T(8,128)S(1)}) custom-call(bf16[512,8192]{1,0:T(8,128)(2,1)} %refs_5_.1), custom_call_target="tpu_custom_call" | custom-call | flops 16777216 | bytes 8388608 | tf_op jit(solution)/shard_map/pallas_call | solution.py:34
  55.7 5.5 %all-to-all-done.1.parts = bf16[16,8,4096]{2,1,0:T(8,128)(2,1)S(1)} async-done(((bf16[16,8,4096]{2,1,0:T(8,128)(2,1)}), bf16[16,8,4096]{2,1,0:T(8,128)(2,1)S(1)}, u32[]{:S(2)}, u32[]{:S(2)}) %all-to-all-start.1) | async-done | bytes 1048608 | tf_op jit(solution)/shard_map/all_to_all | solution.py:364
  62.4 5.5 %all-to-all-start.2 = ((bf16[16,8,4224]{2,1,0:T(8,128)(2,1)}), bf16[16,8,4224]{2,1,0:T(8,128)(2,1)S(1)}, u32[]{:S(2)}, u32[]{:S(2)}) async-start(bf16[16,8,4224]{2,1,0:T(8,128)(2,1)} %shard_map.101), calls=%async_computation.2 | async-start | bytes 2162688 | tf_op jit(solution)/shard_map/all_to_all | solution.py:364
  67.9 1.9 %collective-permute-start.6 = (bf16[384,1024]{1,0:T(8,128)(2,1)S(1)}, bf16[384,1024]{1,0:T(8,128)(2,1)S(1)}, u32[]{:S(2)}, u32[]{:S(2)}) collective-permute-start(bf16[384,1024]{1,0:T(8,128)(2,1)S(1)} %shard_map.102.own), channel_id=1, source_target_pairs={{0,1},{1,0},{2,3},{3,2},{4,5},{5,4},{6,7},{7,6},{8,9},{9,8},{10,11... | collective-permute-start | bytes 2359304 | tf_op jit(solution)/shard_map/ppermute | solution.py:360
  69.8 2.6 %collective-permute-start.9 = (bf16[136,512]{1,0:T(8,128)(2,1)S(1)}, bf16[136,512]{1,0:T(8,128)(2,1)S(1)}, u32[]{:S(2)}, u32[]{:S(2)}) collective-permute-start(bf16[136,512]{1,0:T(8,128)(2,1)S(1)} %get-tuple-element.69.feats.refs_0_), channel_id=1, source_target_pairs={{0,96},{32,0},{64,32},{96,64},{1,97},{33,1},{65,33},{97,65},{2,98}... | collective-permute-start | bytes 417800 | tf_op jit(solution)/shard_map/ppermute | solution.py:372
  73.1 5.2 %collective-permute-done.9.refs_3_ = bf16[136,512]{1,0:T(8,128)(2,1)S(1)} collective-permute-done((bf16[136,512]{1,0:T(8,128)(2,1)S(1)}, bf16[136,512]{1,0:T(8,128)(2,1)S(1)}, u32[]{:S(2)}, u32[]{:S(2)}) %collective-permute-start.9) | collective-permute-done | bytes 139296 | tf_op jit(solution)/shard_map/ppermute | solution.py:372
  78.9 3.5 %collective-permute-done.7.refs_1_ = bf16[136,512]{1,0:T(8,128)(2,1)S(1)} collective-permute-done((bf16[136,512]{1,0:T(8,128)(2,1)S(1)}, bf16[136,512]{1,0:T(8,128)(2,1)S(1)}, u32[]{:S(2)}, u32[]{:S(2)}) %collective-permute-start.7) | collective-permute-done | bytes 139296 | tf_op jit(solution)/shard_map/ppermute | solution.py:372
  83.2 3.2 %collective-permute-start.10 = (bf16[128,4224]{1,0:T(8,128)(2,1)S(1)}, bf16[128,4224]{1,0:T(8,128)(2,1)S(1)}, u32[]{:S(2)}, u32[]{:S(2)}) collective-permute-start(bf16[128,4224]{1,0:T(8,128)(2,1)S(1)} %bitcast.6), channel_id=1, source_target_pairs={{0,1},{1,0},{2,3},{3,2},{4,5},{5,4},{6,7},{7,6},{8,9},{9,8},{10,11... | collective-permute-start | bytes 3244040 | tf_op jit(solution)/shard_map/ppermute | solution.py:360
  86.5 2.1 %collective-permute-start.14 = (bf16[128,1024]{1,0:T(8,128)(2,1)S(1)}, bf16[128,1024]{1,0:T(8,128)(2,1)S(1)}, u32[]{:S(2)}, u32[]{:S(2)}) collective-permute-start(bf16[128,1024]{1,0:T(8,128)(2,1)S(1)} %get-tuple-element.78), channel_id=1, source_target_pairs={{0,32},{32,64},{64,96},{96,0},{1,33},{33,65},{65,97},{97,1},{2,34}... | collective-permute-start | bytes 786440 | tf_op jit(solution)/shard_map/ppermute | solution.py:372
  88.6 2.4 %collective-permute-start.15 = (bf16[128,1024]{1,0:T(8,128)(2,1)S(1)}, bf16[128,1024]{1,0:T(8,128)(2,1)S(1)}, u32[]{:S(2)}, u32[]{:S(2)}) collective-permute-start(bf16[128,1024]{1,0:T(8,128)(2,1)S(1)} %get-tuple-element.79), channel_id=1, source_target_pairs={{0,64},{32,96},{64,0},{96,32},{1,65},{33,97},{65,1},{97,33},{2,66}... | collective-permute-start | bytes 786440 | tf_op jit(solution)/shard_map/ppermute | solution.py:372
  91.1 4.9 %shard_map.103.refs_6_.p0 = bf16[136,512]{1,0:T(8,128)(2,1)S(1)} custom-call(bf16[128,4224]{1,0:T(8,128)(2,1)S(1)} %bitcast.8, bf16[128,4224]{1,0:T(8,128)(2,1)S(1)} %collective-permute-done.10.e.e_other, bf16[128,128]{1,0:T(8,128)(2,1)S(1)} %get-tuple-element.49.mask, f32[2,512]{1,0:T(2,128)S(1)} %get-tuple-element.59.norm_row, ...), custom_call_target="tpu_custom_call" | custom-call | flops 1073741824 | bytes 10485760 | tf_op jit(solution)/shard_map/pallas_call | solution.py:34
  96.9 2.2 %collective-permute-start.12 = (bf16[136,512]{1,0:T(8,128)(2,1)S(1)}, bf16[136,512]{1,0:T(8,128)(2,1)S(1)}, u32[]{:S(2)}, u32[]{:S(2)}) collective-permute-start(bf16[136,512]{1,0:T(8,128)(2,1)S(1)} %shard_map.103.refs_6_.p0), channel_id=1, source_target_pairs={{0,64},{32,96},{64,0},{96,32},{1,65},{33,97},{65,1},{97,33},{2,66}... | collective-permute-start | bytes 417800 | tf_op jit(solution)/shard_map/ppermute | solution.py:372
  99.2 2.4 %shard_map.104 = (bf16[2,1024,512]{2,1,0:T(8,128)(2,1)S(1)}, bf16[512,512]{1,0:T(8,128)(2,1)S(1)}, f32[512,1]{1,0:T(8,128)S(1)}, f32[8,128]{1,0:T(8,128)S(1)}, bf16[512,2048]{1,0:T(8,128)(2,1)S(1)}) custom-call(bf16[128,1024]{1,0:T(8,128)(2,1)S(1)} %copy-done, bf16[128,1024]{1,0:T(8,128)(2,1)S(1)} %copy-done.1, bf16[384,1024]{1,0:T(8,128)(2,1)S(1)} %shard_map.102.own, ...), custom_call_target="tpu_custom_call" | custom-call | bytes 6291456 | tf_op jit(solution)/shard_map/pallas_call | solution.py:34
  103.1 2.5 %collective-permute-done.13.refs_3_.p3 = bf16[136,512]{1,0:T(8,128)(2,1)S(1)} collective-permute-done((bf16[136,512]{1,0:T(8,128)(2,1)S(1)}, bf16[136,512]{1,0:T(8,128)(2,1)S(1)}, u32[]{:S(2)}, u32[]{:S(2)}) %collective-permute-start.13) | collective-permute-done | bytes 139296 | tf_op jit(solution)/shard_map/ppermute | solution.py:372
  106.1 3.2 %collective-permute-done.11.refs_1_.p1 = bf16[136,512]{1,0:T(8,128)(2,1)S(1)} collective-permute-done((bf16[136,512]{1,0:T(8,128)(2,1)S(1)}, bf16[136,512]{1,0:T(8,128)(2,1)S(1)}, u32[]{:S(2)}, u32[]{:S(2)}) %collective-permute-start.11) | collective-permute-done | bytes 139296 | tf_op jit(solution)/shard_map/ppermute | solution.py:372
  110.0 3.0 %shard_map.107 = (bf16[2,1024,512]{2,1,0:T(8,128)(2,1)}, bf16[512,2048]{1,0:T(8,128)(2,1)}, f32[1,1]{1,0:T(1,128)}) custom-call(bf16[2,1024,512]{2,1,0:T(8,128)(2,1)S(1)} %get-tuple-element.76.xt, f32[8,128]{1,0:T(8,128)S(1)} %get-tuple-element.77.refs_0_.count, bf16[136,512]{1,0:T(8,128)(2,1)S(1)} %shard_map.103.refs_6_.p0, ...), custom_call_target="tpu_custom_call" | custom-call | flops 3221225472 | bytes 8388608 | tf_op jit(solution)/shard_map/pallas_call | solution.py:34
  113.0 1.9 %shard_map.108 = bf16[512,2048]{1,0:T(8,128)(2,1)} custom-call(bf16[128,4224]{1,0:T(8,128)(2,1)S(1)} %collective-permute-done.10.e.e_other, bf16[384,1024]{1,0:T(8,128)(2,1)S(1)} %collective-permute-done.17.other, bf16[512,512]{1,0:T(8,128)(2,1)S(1)} %get-tuple-element.81.ft, f32[512,1]{1,0:T(8,128)S(1)} %get-tuple-element.82.scale, ...), custom_call_target="tpu_custom_call", output_to_operand_aliasing={{}: (6, {})} | custom-call | flops 1073741824 | bytes 3145728 | tf_op jit(solution)/shard_map/pallas_call | solution.py:34
  (46 shorter events, 14.1 us)
Async XLA Ops:
  2.4 2.4 %collective-permute-start = (bf16[4,8320]{1,0:T(4,128)(2,1)S(1)}, bf16[4,8320]{1,0:T(4,128)(2,1)S(1)}, u32[]{:S(2)}, u32[]{:S(2)}) collective-permute-start(bf16[4,8320]{1,0:T(4,128)(2,1)S(1)} %get-tuple-element.46), channel_id=1, source_target_pairs={{0,1},{1,0},{2,3},{3,2},{4,5},{5,4},{6,7},{7,6},{8,9},{9,8},{10,11... | collective-permute-start | bytes 199688 | tf_op jit(solution)/shard_map/ppermute | solution.py:360
  28.6 5.4 %collective-permute-start.1 = (bf16[128,4224]{1,0:T(8,128)(2,1)S(1)}, bf16[128,4224]{1,0:T(8,128)(2,1)S(1)}, u32[]{:S(2)}, u32[]{:S(2)}) collective-permute-start(bf16[128,4224]{1,0:T(8,128)(2,1)S(1)} %bitcast.10), channel_id=1, source_target_pairs={{0,1},{1,0},{2,3},{3,2},{4,5},{5,4},{6,7},{7,6},{8,9},{9,8},{10,11... | collective-permute-start | bytes 3244040 | tf_op jit(solution)/shard_map/ppermute | solution.py:360
  37.3 2.7 %collective-permute-start.2 = (bf16[128,4096]{1,0:T(8,128)(2,1)S(1)}, bf16[128,4096]{1,0:T(8,128)(2,1)S(1)}, u32[]{:S(2)}, u32[]{:S(2)}) collective-permute-start(bf16[128,4096]{1,0:T(8,128)(2,1)S(1)} %get-tuple-element.54), channel_id=1, source_target_pairs={{0,1},{1,0},{2,3},{3,2},{4,5},{5,4},{6,7},{7,6},{8,9},{9,8},{10,11... | collective-permute-start | bytes 3145736 | tf_op jit(solution)/shard_map/ppermute | solution.py:360
  41.1 8.8 %copy-start.4 = (bf16[128,1024]{1,0:T(8,128)(2,1)S(1)}, bf16[128,1024]{1,0:T(8,128)(2,1)}, u32[]{:S(2)}) copy-start(bf16[128,1024]{1,0:T(8,128)(2,1)} %get-tuple-element.62) | copy-start | bytes 786436
  41.1 20.1 %all-to-all-start.1 = ((bf16[16,8,4096]{2,1,0:T(8,128)(2,1)}), bf16[16,8,4096]{2,1,0:T(8,128)(2,1)S(1)}, u32[]{:S(2)}, u32[]{:S(2)}) async-start(bf16[16,8,4096]{2,1,0:T(8,128)(2,1)} %bitcast.13), calls=%async_computation.1 | async-start | bytes 2097152 | tf_op jit(solution)/shard_map/all_to_all | solution.py:364
  44.9 17.4 %collective-permute-start.3 = (bf16[128,1024]{1,0:T(8,128)(2,1)S(1)}, bf16[128,1024]{1,0:T(8,128)(2,1)S(1)}, u32[]{:S(2)}, u32[]{:S(2)}) collective-permute-start(bf16[128,1024]{1,0:T(8,128)(2,1)S(1)} %copy-done.6), channel_id=1, source_target_pairs={{0,32},{32,64},{64,96},{96,0},{1,33},{33,65},{65,97},{97,1},{2,34}... | collective-permute-start | bytes 786440 | tf_op jit(solution)/shard_map/ppermute | solution.py:372
  46.6 15.7 %collective-permute-start.4 = (bf16[128,1024]{1,0:T(8,128)(2,1)S(1)}, bf16[128,1024]{1,0:T(8,128)(2,1)S(1)}, u32[]{:S(2)}, u32[]{:S(2)}) collective-permute-start(bf16[128,1024]{1,0:T(8,128)(2,1)S(1)} %copy-done.5), channel_id=1, source_target_pairs={{0,64},{32,96},{64,0},{96,32},{1,65},{33,97},{65,1},{97,33},{2,66}... | collective-permute-start | bytes 786440 | tf_op jit(solution)/shard_map/ppermute | solution.py:372
  50.0 11.3 %copy-start.2 = (f32[2,4096]{1,0:T(2,128)S(1)}, f32[2,4096]{1,0:T(2,128)}, u32[]{:S(2)}) copy-start(f32[2,4096]{1,0:T(2,128)} %bias.1) | copy-start | bytes 98308
  50.0 12.4 %collective-permute-start.5 = (bf16[128,1024]{1,0:T(8,128)(2,1)S(1)}, bf16[128,1024]{1,0:T(8,128)(2,1)S(1)}, u32[]{:S(2)}, u32[]{:S(2)}) collective-permute-start(bf16[128,1024]{1,0:T(8,128)(2,1)S(1)} %copy-done.4), channel_id=1, source_target_pairs={{0,96},{32,0},{64,32},{96,64},{1,97},{33,1},{65,33},{97,65},{2,98}... | collective-permute-start | bytes 786440 | tf_op jit(solution)/shard_map/ppermute | solution.py:372
  62.4 20.8 %all-to-all-start.2 = ((bf16[16,8,4224]{2,1,0:T(8,128)(2,1)}), bf16[16,8,4224]{2,1,0:T(8,128)(2,1)S(1)}, u32[]{:S(2)}, u32[]{:S(2)}) async-start(bf16[16,8,4224]{2,1,0:T(8,128)(2,1)} %shard_map.101), calls=%async_computation.2 | async-start | bytes 2162688 | tf_op jit(solution)/shard_map/all_to_all | solution.py:364
  67.9 14.4 %collective-permute-start.6 = (bf16[384,1024]{1,0:T(8,128)(2,1)S(1)}, bf16[384,1024]{1,0:T(8,128)(2,1)S(1)}, u32[]{:S(2)}, u32[]{:S(2)}) collective-permute-start(bf16[384,1024]{1,0:T(8,128)(2,1)S(1)} %shard_map.102.own), channel_id=1, source_target_pairs={{0,1},{1,0},{2,3},{3,2},{4,5},{5,4},{6,7},{7,6},{8,9},{9,8},{10,11... | collective-permute-start | bytes 2359304 | tf_op jit(solution)/shard_map/ppermute | solution.py:360
  69.8 8.4 %collective-permute-start.9 = (bf16[136,512]{1,0:T(8,128)(2,1)S(1)}, bf16[136,512]{1,0:T(8,128)(2,1)S(1)}, u32[]{:S(2)}, u32[]{:S(2)}) collective-permute-start(bf16[136,512]{1,0:T(8,128)(2,1)S(1)} %get-tuple-element.69.feats.refs_0_), channel_id=1, source_target_pairs={{0,96},{32,0},{64,32},{96,64},{1,97},{33,1},{65,33},{97,65},{2,98}... | collective-permute-start | bytes 417800 | tf_op jit(solution)/shard_map/ppermute | solution.py:372
  72.4 6.5 %collective-permute-start.8 = (bf16[136,512]{1,0:T(8,128)(2,1)S(1)}, bf16[136,512]{1,0:T(8,128)(2,1)S(1)}, u32[]{:S(2)}, u32[]{:S(2)}) collective-permute-start(bf16[136,512]{1,0:T(8,128)(2,1)S(1)} %get-tuple-element.69.feats.refs_0_), channel_id=1, source_target_pairs={{0,64},{32,96},{64,0},{96,32},{1,65},{33,97},{65,1},{97,33},{2,66}... | collective-permute-start | bytes 417800 | tf_op jit(solution)/shard_map/ppermute | solution.py:372
  72.6 9.7 %collective-permute-start.7 = (bf16[136,512]{1,0:T(8,128)(2,1)S(1)}, bf16[136,512]{1,0:T(8,128)(2,1)S(1)}, u32[]{:S(2)}, u32[]{:S(2)}) collective-permute-start(bf16[136,512]{1,0:T(8,128)(2,1)S(1)} %get-tuple-element.69.feats.refs_0_), channel_id=1, source_target_pairs={{0,32},{32,64},{64,96},{96,0},{1,33},{33,65},{65,97},{97,1},{2,34}... | collective-permute-start | bytes 417800 | tf_op jit(solution)/shard_map/ppermute | solution.py:372
  83.2 7.8 %collective-permute-start.10 = (bf16[128,4224]{1,0:T(8,128)(2,1)S(1)}, bf16[128,4224]{1,0:T(8,128)(2,1)S(1)}, u32[]{:S(2)}, u32[]{:S(2)}) collective-permute-start(bf16[128,4224]{1,0:T(8,128)(2,1)S(1)} %bitcast.6), channel_id=1, source_target_pairs={{0,1},{1,0},{2,3},{3,2},{4,5},{5,4},{6,7},{7,6},{8,9},{9,8},{10,11... | collective-permute-start | bytes 3244040 | tf_op jit(solution)/shard_map/ppermute | solution.py:360
  86.5 12.7 %collective-permute-start.14 = (bf16[128,1024]{1,0:T(8,128)(2,1)S(1)}, bf16[128,1024]{1,0:T(8,128)(2,1)S(1)}, u32[]{:S(2)}, u32[]{:S(2)}) collective-permute-start(bf16[128,1024]{1,0:T(8,128)(2,1)S(1)} %get-tuple-element.78), channel_id=1, source_target_pairs={{0,32},{32,64},{64,96},{96,0},{1,33},{33,65},{65,97},{97,1},{2,34}... | collective-permute-start | bytes 786440 | tf_op jit(solution)/shard_map/ppermute | solution.py:372
  88.6 14.5 %collective-permute-start.15 = (bf16[128,1024]{1,0:T(8,128)(2,1)S(1)}, bf16[128,1024]{1,0:T(8,128)(2,1)S(1)}, u32[]{:S(2)}, u32[]{:S(2)}) collective-permute-start(bf16[128,1024]{1,0:T(8,128)(2,1)S(1)} %get-tuple-element.79), channel_id=1, source_target_pairs={{0,64},{32,96},{64,0},{96,32},{1,65},{33,97},{65,1},{97,33},{2,66}... | collective-permute-start | bytes 786440 | tf_op jit(solution)/shard_map/ppermute | solution.py:372
  91.0 12.1 %collective-permute-start.16 = (bf16[128,1024]{1,0:T(8,128)(2,1)S(1)}, bf16[128,1024]{1,0:T(8,128)(2,1)S(1)}, u32[]{:S(2)}, u32[]{:S(2)}) collective-permute-start(bf16[128,1024]{1,0:T(8,128)(2,1)S(1)} %get-tuple-element.80), channel_id=1, source_target_pairs={{0,96},{32,0},{64,32},{96,64},{1,97},{33,1},{65,33},{97,65},{2,98}... | collective-permute-start | bytes 786440 | tf_op jit(solution)/shard_map/ppermute | solution.py:372
  91.1 8.1 %copy-start = (bf16[128,1024]{1,0:T(8,128)(2,1)S(1)}, bf16[128,1024]{1,0:T(8,128)(2,1)}, u32[]{:S(2)}) copy-start(bf16[128,1024]{1,0:T(8,128)(2,1)} %get-tuple-element.48.home_own) | copy-start | bytes 786436
  91.1 8.1 %copy-start.1 = (bf16[128,1024]{1,0:T(8,128)(2,1)S(1)}, bf16[128,1024]{1,0:T(8,128)(2,1)}, u32[]{:S(2)}) copy-start(bf16[128,1024]{1,0:T(8,128)(2,1)} %get-tuple-element.52.home_other) | copy-start | bytes 786436
  95.9 9.7 %collective-permute-start.13 = (bf16[136,512]{1,0:T(8,128)(2,1)S(1)}, bf16[136,512]{1,0:T(8,128)(2,1)S(1)}, u32[]{:S(2)}, u32[]{:S(2)}) collective-permute-start(bf16[136,512]{1,0:T(8,128)(2,1)S(1)} %shard_map.103.refs_6_.p0), channel_id=1, source_target_pairs={{0,96},{32,0},{64,32},{96,64},{1,97},{33,1},{65,33},{97,65},{2,98}... | collective-permute-start | bytes 417800 | tf_op jit(solution)/shard_map/ppermute | solution.py:372
  96.9 9.2 %collective-permute-start.12 = (bf16[136,512]{1,0:T(8,128)(2,1)S(1)}, bf16[136,512]{1,0:T(8,128)(2,1)S(1)}, u32[]{:S(2)}, u32[]{:S(2)}) collective-permute-start(bf16[136,512]{1,0:T(8,128)(2,1)S(1)} %shard_map.103.refs_6_.p0), channel_id=1, source_target_pairs={{0,64},{32,96},{64,0},{96,32},{1,65},{33,97},{65,1},{97,33},{2,66}... | collective-permute-start | bytes 417800 | tf_op jit(solution)/shard_map/ppermute | solution.py:372
  99.2 10.2 %collective-permute-start.11 = (bf16[136,512]{1,0:T(8,128)(2,1)S(1)}, bf16[136,512]{1,0:T(8,128)(2,1)S(1)}, u32[]{:S(2)}, u32[]{:S(2)}) collective-permute-start(bf16[136,512]{1,0:T(8,128)(2,1)S(1)} %shard_map.103.refs_6_.p0), channel_id=1, source_target_pairs={{0,32},{32,64},{64,96},{96,0},{1,33},{33,65},{65,97},{97,1},{2,34}... | collective-permute-start | bytes 417800 | tf_op jit(solution)/shard_map/ppermute | solution.py:372
  109.4 3.6 %collective-permute-start.17 = (bf16[384,1024]{1,0:T(8,128)(2,1)S(1)}, bf16[384,1024]{1,0:T(8,128)(2,1)S(1)}, u32[]{:S(2)}, u32[]{:S(2)}) collective-permute-start(bf16[384,1024]{1,0:T(8,128)(2,1)S(1)} %shard_map.106.own), channel_id=1, source_target_pairs={{0,1},{1,0},{2,3},{3,2},{4,5},{5,4},{6,7},{7,6},{8,9},{9,8},{10,11... | collective-permute-start | bytes 2359304 | tf_op jit(solution)/shard_map/ppermute | solution.py:360
  (3 other events, 14.8 us)
